TPU v7x, 32 devices: a whole 2x2x4 slice. The times are simulated.
32 devices in a mesh: dp: 8 (over z, y), tensor: 4 (over x, core).
Axes of the slice: x: 2, y: 2, z: 4, core: 2. Of those that a mesh axis runs over, the one named last changes fastest.
Arguments:
- states: bfloat16 [4, 1024, 5120], P(None, 'dp', 'tensor'), may hold values from -6 to 6
- mix_weights: float32 [4], replicated, may hold values from 0.3 to 1
- router: bfloat16 [5120], P('tensor'), may hold values from -0.078125 to 0.078125
- norm_gain: bfloat16 [5120], P('tensor'), may hold values from 0.5 to 1.5
- gate_weight: bfloat16 [5120, 6912], P('tensor', 'dp'), may hold values from -0.078125 to 0.078125
- up_weight: bfloat16 [5120, 6912], P('tensor', 'dp'), may hold values from -0.078125 to 0.078125
- down_weight: bfloat16 [6912, 5120], P('dp', 'tensor'), may hold values from -0.078125 to 0.078125
- counts: int32 [1, 8], replicated, may hold values from 1 to 24, 128 in all within a row
- chosen: int32 [8, 24], P('dp'), may hold values from 0 to 127, as said below
- cotangent: bfloat16 [1024, 5120], P('dp', 'tensor'), may hold values from -6 to 6
Outputs:
- updated: bfloat16 [1024, 5120], P('dp', 'tensor')
- grad_input: bfloat16 [1024, 5120], P('dp', 'tensor')
- grad_gate: float32 [5120, 6912], P('tensor', 'dp')
- grad_up: float32 [5120, 6912], P('tensor', 'dp')
- grad_down: float32 [6912, 5120], P('dp', 'tensor')
Inputs may be any that keep to these rules, and one draw needn't show every extreme that they name: Each row of counts sums to one eighth of 1024; entry [s, j] belongs to index s * 8 + j of dp. `chosen`: each row holds 24 distinct positions; the first counts entries of row p are the selected tokens of index p of dp, the rest are padding.
All inputs are finite; a program needn't handle non-finite values.
Results may differ from a plain program's by a relative error of at most 0.014.
Values may be sent and summed in bfloat16 or wider, within the bound.
No kernel may reach another device: no remote copies, remote signals or barrier semaphores. Data moves between devices by JAX's collectives and lax.ppermute only.
A program may use at most 128 MiB of HBM per device.

v0:
```python
import functools
import jax
import jax.numpy as jnp
from jax import lax
from jax.experimental import pallas as pl
from jax.experimental.pallas import tpu as pltpu
from jax.sharding import PartitionSpec as P


epsilon = 1e-05
f32, bf16 = jnp.float32, jnp.bfloat16
SMEM = pl.BlockSpec(memory_space=pltpu.SMEM)
VMEM = pl.BlockSpec(memory_space=pltpu.VMEM)
PARTS = 3


def call(kernel, out, ins, scratch=(), flops=0, nbytes=0, vmem=32 << 20):
    return pl.pallas_call(
        kernel,
        out_shape=out,
        in_specs=ins,
        out_specs=jax.tree.map(lambda _: VMEM, out),
        scratch_shapes=list(scratch),
        cost_estimate=pl.CostEstimate(flops=flops, bytes_accessed=nbytes, transcendentals=0),
        compiler_params=pltpu.CompilerParams(vmem_limit_bytes=vmem),
    )


def sds(shape, dtype):
    return jax.ShapeDtypeStruct(shape, dtype)


def terms(value):
    out, rest = [], value
    for _ in range(PARTS):
        term = rest.astype(bf16).astype(f32)
        out.append(term)
        rest = rest - term
    return out


def in_lanes(values, width, first):
    rows = values[0].shape[0]
    lane = lax.broadcasted_iota(jnp.int32, (rows, width), 1)
    total = jnp.zeros((rows, width), f32)
    for i, value in enumerate(values):
        total = jnp.where(lane == first + i, value, total)
    return total


def dot_nt(a, b):
    return lax.dot_general(a, b, (((1,), (1,)), ((), ())), preferred_element_type=f32)


def dot_nn(a, b):
    return jnp.dot(a, b, preferred_element_type=f32)


def placement(counts_ref, me, slots, slot_rows, total, packed_axis):
    shape = (total, slots * slot_rows) if packed_axis == 0 else (slots * slot_rows, total)
    packed = lax.broadcasted_iota(jnp.int32, shape, packed_axis)
    slotted = lax.broadcasted_iota(jnp.int32, shape, 1 - packed_axis)
    hit, at = packed < 0, 0
    for k in range(slots):
        here = counts_ref[0, me ^ k]
        row = slotted - k * slot_rows
        hit = hit | ((row >= 0) & (row < here) & (packed == row + at))
        at = at + here
    return jnp.where(hit, 1.0, 0.0).astype(bf16)


def fetch(pairs, sem):
    copies = [pltpu.make_async_copy(src, dst, sem.at[i]) for i, (src, dst) in enumerate(pairs)]
    for copy in copies:
        copy.start()
    return copies


def pick_kernel(cap, chosen, mixw, states, cot, router, gain, picked_ref, load_ref, *scratch):
    *places, sem = scratch
    for copy in fetch(list(zip((chosen, mixw, states, cot, router, gain), places)), sem):
        copy.wait()
    chosen, mixw, states, cot, router, gain = places
    tokens, width = cot.shape
    row = lax.broadcasted_iota(jnp.int32, (cap, tokens), 0)
    col = lax.broadcasted_iota(jnp.int32, (cap, tokens), 1)
    want = jnp.zeros((cap, tokens), f32)
    for k in range(cap):
        want = jnp.where((row == k) & (col == chosen[0, k]), 1.0, want)
    want = want.astype(bf16)
    picked = mixw[0] * dot_nn(want, states[0])
    for j in range(1, states.shape[0]):
        picked = picked + mixw[j] * dot_nn(want, states[j])
    picked_ref[...] = picked
    load_ref[:, :width] = (picked * gain[...].astype(f32).reshape(1, width)).astype(bf16)
    load_ref[:, width : 2 * width] = dot_nn(want, cot[...]).astype(bf16)
    logit = jnp.sum(picked * router[...].astype(f32).reshape(1, width), axis=1, keepdims=True)
    square = jnp.sum(picked * picked, axis=1, keepdims=True)
    first = 2 * PARTS * lax.axis_index("tensor")
    load_ref[:, 2 * width :] = in_lanes(terms(logit) + terms(square), 128, first).astype(bf16)


def weights_kernel(slots, slot_rows, total, after, *refs):
    *pairs, pack_ref, unpack_ref, counts, sem = refs
    half = len(pairs) // 2
    copies = fetch(list(zip(pairs[: half + 1], [counts] + pairs[half + 1 :])), sem)
    copies[0].wait()
    me = lax.axis_index("dp")
    pack_ref[...] = placement(counts, me, slots, slot_rows, total, 0)
    unpack_ref[...] = placement(counts, me, slots, slot_rows, total, 1)
    for copy in copies[1:]:
        copy.wait()


def prep_kernel(after, counts, chosen, mixw, states, cot, *refs):
    mixed_ref, cot_ref, want_ref, *places, sem = refs
    for copy in fetch(list(zip((counts, chosen, mixw, states, cot), places)), sem):
        copy.wait()
    counts, chosen, mixw, states, cot = places
    me = lax.axis_index("dp")
    mine = counts[0, me]
    tokens, cap = want_ref.shape
    row = lax.broadcasted_iota(jnp.int32, (tokens, cap), 0)
    col = lax.broadcasted_iota(jnp.int32, (tokens, cap), 1)
    want = jnp.zeros((tokens, cap), f32)
    for k in range(cap):
        want = jnp.where((col == k) & (row == chosen[0, k]) & (k < mine), 1.0, want)
    want_ref[...] = want.astype(bf16)
    keep = jnp.sum(want, axis=1, keepdims=True) == 0.0
    mixed = mixw[0] * states[0].astype(f32)
    for j in range(1, states.shape[0]):
        mixed = mixed + mixw[j] * states[j].astype(f32)
    mixed_ref[...] = jnp.where(keep, mixed, 0.0).astype(bf16)
    cot_ref[...] = jnp.where(keep, cot[...].astype(f32), 0.0).astype(bf16)


def first_kernel(slots, cap, slot_rows, lanes, want, *refs):
    blocks = refs[:slots]
    gate_w, up_w, down_w, own_ref, send_ref, pg_ref, cot_ref, rows_ref, sums_ref, mine_ref, sem = refs[slots:]
    copies = fetch([(blocks[0], mine_ref)], sem)
    core = lax.axis_index("tensor") % 2
    ff, width = gate_w.shape
    total = pg_ref.shape[0]
    for k in reversed(range(slots)):
        if k == 0:
            copies[0].wait()
        rows_ref[k * slot_rows : k * slot_rows + cap, :] = (blocks[k] if k else mine_ref)[...]
        rows_ref[k * slot_rows + cap : (k + 1) * slot_rows, :] = jnp.zeros((slot_rows - cap, rows_ref.shape[1]), bf16)
    pg = dot_nn(want[...], rows_ref[:, :width]).astype(bf16)
    cot = dot_nn(want[...], rows_ref[:, width : 2 * width]).astype(bf16)
    pg_ref[...] = pg
    cot_ref[...] = cot
    spare = lanes - ff
    zeros = jnp.zeros((total, spare), f32)
    sums_ref[:, :ff] = dot_nt(pg, gate_w[...])
    sums_ref[:, ff:lanes] = dot_nn(want[...], rows_ref[:, 2 * width :])[:, :spare]
    sums_ref[:, lanes : lanes + ff] = dot_nt(pg, up_w[...])
    sums_ref[:, lanes + ff : 2 * lanes] = zeros
    sums_ref[:, 2 * lanes : 2 * lanes + ff] = dot_nt(cot, down_w[...])
    sums_ref[:, 2 * lanes + ff :] = zeros
    half = total // 2
    own_ref[...] = sums_ref[pl.ds(pl.multiple_of(core * half, half), half), :]
    send_ref[...] = sums_ref[pl.ds(pl.multiple_of((1 - core) * half, half), half), :].astype(bf16)


def add_kernel(own, got, out_ref, sum_ref):
    total = own[...] + got[...].astype(f32)
    sum_ref[...] = total
    out_ref[...] = total.astype(bf16)


def act_kernel(ff, lanes, model_width, own, got, out_ref):
    def part(i, size=ff, at=0):
        return own[:, i * lanes + at : i * lanes + at + size] + got[
            :, i * lanes + at : i * lanes + at + size
        ].astype(f32)

    scalars = part(0, lanes - ff, ff)
    kind = lax.broadcasted_iota(jnp.int32, scalars.shape, 1) % (2 * PARTS)
    logits = jnp.sum(jnp.where(kind < PARTS, scalars, 0.0), axis=1, keepdims=True)
    squares = jnp.sum(jnp.where(kind < PARTS, 0.0, scalars), axis=1, keepdims=True)
    gating = jax.nn.sigmoid(logits)
    inverse = lax.rsqrt(squares / model_width + epsilon)
    gate_raw, up_raw, dh_raw = part(0), part(1), part(2)
    gate_pre, up_pre = gate_raw * inverse, up_raw * inverse
    dhidden = dh_raw * gating
    sig = jax.nn.sigmoid(gate_pre)
    silu = gate_pre * sig
    hidden = (gating * silu * up_pre).astype(bf16)
    scaled = dhidden * inverse
    dgate = (scaled * up_pre * sig * (1.0 + gate_pre * (1.0 - sig))).astype(bf16)
    dup = (scaled * silu).astype(bf16)
    dlogit = (1.0 - gating) * jnp.sum(hidden.astype(f32) * dh_raw, axis=1, keepdims=True)
    inner = jnp.sum(dgate.astype(f32) * gate_raw + dup.astype(f32) * up_raw, axis=1, keepdims=True)
    inner = inner * inverse * inverse / model_width
    spare = lanes - ff
    zeros = jnp.zeros((own.shape[0], spare), bf16)
    first = 2 * PARTS * (lax.axis_index("dp") % 4)
    out_ref[:, :ff] = hidden
    out_ref[:, ff:lanes] = in_lanes(terms(dlogit) + terms(inner), spare, first).astype(bf16)
    out_ref[:, lanes : lanes + ff] = dgate
    out_ref[:, lanes + ff : 2 * lanes] = zeros
    out_ref[:, 2 * lanes : 2 * lanes + ff] = dup
    out_ref[:, 2 * lanes + ff :] = zeros


def second_kernel(slots, cap, slot_rows, lanes, want, own, got, gate_w, up_w, down_w, *refs):
    outs = refs[:slots]
    hidden_ref, dgate_ref, dup_ref, act_ref, rows_ref = refs[slots:]
    core = lax.axis_index("tensor") % 2
    ff, width = gate_w.shape
    half = own.shape[0]
    total = 2 * half
    act_ref[pl.ds(pl.multiple_of(core * half, half), half), :] = own[...]
    act_ref[pl.ds(pl.multiple_of((1 - core) * half, half), half), :] = got[...]
    hidden = act_ref[:, :ff]
    dgate = act_ref[:, lanes : lanes + ff]
    dup = act_ref[:, 2 * lanes : 2 * lanes + ff]
    hidden_ref[...] = hidden
    dgate_ref[...] = dgate
    dup_ref[...] = dup
    rows_ref[:, :width] = dot_nn(hidden, down_w[...]).astype(bf16)
    rows_ref[:, width : 2 * width] = (dot_nn(dgate, gate_w[...]) + dot_nn(dup, up_w[...])).astype(bf16)
    spare = lanes - ff
    rows_ref[:, 2 * width : 2 * width + spare] = act_ref[:, ff:lanes]
    rows_ref[:, 2 * width + spare :] = jnp.zeros((total, rows_ref.shape[1] - 2 * width - spare), bf16)
    slotted = dot_nn(want[...], rows_ref[...]).astype(bf16)
    for k in range(slots):
        outs[k][...] = slotted[k * slot_rows : k * slot_rows + cap]


def last_kernel(want, picked, load, mixed, cot, router, gain, *refs):
    *blocks, updated_ref, grad_ref = refs
    _, width = cot.shape
    sums = blocks[0][...].astype(f32)
    for block in blocks[1:]:
        sums = sums + block[...].astype(f32)
    scalars = sums[:, 2 * width :]
    kind = lax.broadcasted_iota(jnp.int32, scalars.shape, 1) % (2 * PARTS)
    dlogit = jnp.sum(jnp.where(kind < PARTS, scalars, 0.0), axis=1, keepdims=True)
    inner = jnp.sum(jnp.where(kind < PARTS, 0.0, scalars), axis=1, keepdims=True)
    new_rows = (picked[...] + sums[:, :width]).astype(bf16)
    drows = (
        load[:, width : 2 * width].astype(f32)
        + sums[:, width : 2 * width] * gain[...].astype(f32)
        - picked[...] * inner
        + dlogit * router[...].astype(f32)
    ).astype(bf16)
    updated_ref[...] = (mixed[...].astype(f32) + dot_nn(want[...], new_rows)).astype(bf16)
    grad_ref[...] = (cot[...].astype(f32) + dot_nn(want[...], drows)).astype(bf16)


def fast(states, mix_weights, router, norm_gain, gate_weight, up_weight, down_weight, counts, chosen, cotangent):
    slots = lax.axis_size("dp")
    tensor = lax.axis_size("tensor")
    cap = chosen.shape[1]
    tokens, width = cotangent.shape
    ff = gate_weight.shape[1]
    model_width = width * tensor
    total = counts.shape[0] * counts.shape[1] * tokens // 8
    half = total // 2
    slot_rows = (cap + 15) // 16 * 16
    lanes = (ff + 2 * PARTS * tensor + 127) // 128 * 128
    columns = 2 * width + 128
    anywhere = pl.BlockSpec(memory_space=pltpu.HBM)
    block = sds((cap, columns), bf16)

    def over_dp(x, k):
        return lax.ppermute(x, "dp", [(i, i ^ k) for i in range(slots)])

    def over_tensor(x, k):
        return lax.ppermute(x, "tensor", [(i, i ^ k) for i in range(tensor)])

    def copy_of(x, space=pltpu.VMEM):
        return space(x.shape, x.dtype)

    sem = pltpu.SemaphoreType.DMA((8,))
    picked, load = call(
        functools.partial(pick_kernel, cap),
        (sds((cap, width), f32), block),
        [anywhere] * 6,
        [copy_of(chosen, pltpu.SMEM), copy_of(mix_weights, pltpu.SMEM)]
        + [copy_of(x) for x in (states, cotangent, router, norm_gain)]
        + [sem],
        vmem=65_000_000,
    )(chosen, mix_weights, states, cotangent, router, norm_gain)
    gate_t, up_t = gate_weight.T, up_weight.T
    blocks = {0: load}
    for step in (4, 2, 1):
        for k in list(blocks):
            blocks[k ^ step] = over_dp(blocks[k], step)
    weight = sds((ff, width), bf16)
    gate_v, up_v, down_v, pack, unpack = call(
        functools.partial(weights_kernel, slots, slot_rows, total),
        (weight,) * 3 + (sds((total, slots * slot_rows), bf16), sds((slots * slot_rows, total), bf16)),
        [pl.BlockSpec(memory_space=pl.ANY)] + [anywhere] * 4,
        [copy_of(counts, pltpu.SMEM), sem],
        nbytes=13 << 20,
        vmem=48_000_000,
    )(load, counts, gate_t, up_t, down_weight)
    weights = (gate_v, up_v, down_v)
    own, send, pg, cot = call(
        functools.partial(first_kernel, slots, cap, slot_rows, lanes),
        (sds((half, 3 * lanes), f32), sds((half, 3 * lanes), bf16), sds((total, width), bf16), sds((total, width), bf16)),
        [VMEM, pl.BlockSpec(memory_space=pl.ANY)] + [VMEM] * (slots + 2),
        [pltpu.VMEM((slots * slot_rows, columns), bf16), pltpu.VMEM((total, 3 * lanes), f32), copy_of(load), sem],
    )(pack, *[blocks[k] for k in range(slots)], *weights)
    send, own = call(
        add_kernel, (sds((half, 3 * lanes), bf16), sds((half, 3 * lanes), f32)), [VMEM] * 2
    )(own, over_tensor(send, 1))
    mixed, cot_kept, want = call(
        prep_kernel,
        (sds((tokens, width), bf16), sds((tokens, width), bf16), sds((tokens, cap), bf16)),
        [VMEM] + [anywhere] * 5,
        [copy_of(x, pltpu.SMEM) for x in (counts, chosen, mix_weights)] + [copy_of(states), copy_of(cotangent), sem],
        nbytes=3 << 20,
    )(send, counts, chosen, mix_weights, states, cotangent)
    act = call(
        functools.partial(act_kernel, ff, lanes, model_width), sds((half, 3 * lanes), bf16), [VMEM] * 2
    )(own, over_tensor(send, 2))
    *blocks, hidden, dgate, dup = call(
        functools.partial(second_kernel, slots, cap, slot_rows, lanes),
        tuple([block] * slots + [sds((total, ff), bf16)] * 3),
        [VMEM] * 6,
        [pltpu.VMEM((total, 3 * lanes), bf16), pltpu.VMEM((total, columns), bf16)],
    )(unpack, act, over_tensor(act, 1), *weights)

    def moved(value, step):
        return over_dp(value, step).astype(f32)

    def total_of(k, *more):
        return sum(more, blocks[k].astype(f32) + moved(blocks[k ^ 1], 1)).astype(bf16)

    sum_4 = total_of(4, moved(total_of(6), 2))
    back = [over_dp(blocks[1], 1), over_dp(total_of(2), 2), over_dp(sum_4, 4)]
    dot_tn = functools.partial(lax.dot_general, dimension_numbers=(((0,), (0,)), ((), ())), preferred_element_type=f32)
    grad_down = dot_tn(hidden, cot)
    grad_gate = dot_tn(dgate, pg).T
    grad_up = dot_tn(dup, pg).T
    updated, grad_input = call(
        last_kernel, (sds((tokens, width), bf16), sds((tokens, width), bf16)), [VMEM] * 11
    )(want, picked, load, mixed, cot_kept, router.reshape(1, width), norm_gain.reshape(1, width), blocks[0], *back)
    return updated, grad_input, grad_gate, grad_up, grad_down


def general(
    states,
    mix_weights,
    router,
    norm_gain,
    gate_weight,
    up_weight,
    down_weight,
    counts,
    chosen,
    cotangent,
):
    width_here = cotangent.shape[1]
    my_rank = lax.axis_index("dp")
    model_width = width_here * lax.axis_size("tensor")
    mixed = jnp.tensordot(mix_weights, states.astype(jnp.float32), axes=1)
    flat_counts = counts.reshape(-1)
    my_count = flat_counts[my_rank]
    positions = chosen[0]
    capacity = positions.shape[0]
    slot_ids = jnp.arange(capacity, dtype=jnp.int32)
    is_valid = slot_ids < my_count
    valid = is_valid.astype(jnp.float32)[:, None]
    picked = mixed[positions]
    router_float = router.astype(jnp.float32)
    gain_float = norm_gain.astype(jnp.float32)
    logit_part = jnp.sum(picked * router_float, axis=1)
    square_part = jnp.sum(picked * picked, axis=1)
    logits, squares = lax.psum((logit_part, square_part), "tensor")
    gating = jax.nn.sigmoid(logits)
    inverse = lax.rsqrt(squares / model_width + epsilon)
    normed = (picked * inverse[:, None] * gain_float * valid).astype(jnp.bfloat16)
    gathered = lax.all_gather(normed, "dp", axis=0, tiled=True)
    gate_part = jnp.dot(gathered, gate_weight, preferred_element_type=jnp.float32)
    up_part = jnp.dot(gathered, up_weight, preferred_element_type=jnp.float32)
    gate_pre, up_pre = lax.psum((gate_part, up_part), "tensor")
    hidden = (jax.nn.silu(gate_pre) * up_pre).astype(jnp.bfloat16)
    update_work = lax.psum_scatter(
        jnp.dot(hidden, down_weight, preferred_element_type=jnp.float32),
        "dp",
        scatter_dimension=0,
        tiled=True,
    ).astype(jnp.bfloat16)
    update_float = update_work.astype(jnp.float32) * valid
    new_rows = picked + gating[:, None] * update_float
    result = mixed.at[positions].set(new_rows).astype(jnp.bfloat16)
    cot_rows = cotangent[positions].astype(jnp.float32)
    dupdate = (gating[:, None] * cot_rows * valid).astype(jnp.bfloat16)
    dlogit_part = jnp.sum(cot_rows * update_float, axis=1)
    dgathered = lax.all_gather(dupdate, "dp", axis=0, tiled=True)
    dhidden_part = jnp.dot(dgathered, down_weight.T, preferred_element_type=jnp.float32)
    dhidden = lax.psum(dhidden_part, "tensor")
    sigmoid_pre = jax.nn.sigmoid(gate_pre)
    dgate_pre = (dhidden * up_pre * sigmoid_pre * (1.0 + gate_pre * (1.0 - sigmoid_pre))).astype(
        jnp.bfloat16
    )
    dup_pre = (dhidden * gate_pre * sigmoid_pre).astype(jnp.bfloat16)
    grad_down = jnp.dot(hidden.T, dgathered, preferred_element_type=jnp.float32)
    grad_gate = jnp.dot(gathered.T, dgate_pre, preferred_element_type=jnp.float32)
    grad_up = jnp.dot(gathered.T, dup_pre, preferred_element_type=jnp.float32)
    first_term = jnp.dot(dgate_pre, gate_weight.T, preferred_element_type=jnp.float32)
    dnormed_work = lax.psum_scatter(
        first_term + jnp.dot(dup_pre, up_weight.T, preferred_element_type=jnp.float32),
        "dp",
        scatter_dimension=0,
        tiled=True,
    )
    scaled = dnormed_work * gain_float * valid
    inner_part = jnp.sum(scaled * picked, axis=1)
    dlogit_sum, inner_sum = lax.psum((dlogit_part, inner_part), "tensor")
    dlogit = dlogit_sum * gating * (1.0 - gating)
    drows = (
        cot_rows
        + inverse[:, None] * scaled
        - picked * (inverse**3 * inner_sum / model_width)[:, None]
        + valid * dlogit[:, None] * router_float
    )
    grad_input = cotangent.astype(jnp.float32).at[positions].set(drows).astype(jnp.bfloat16)
    return (result, grad_input, grad_gate, grad_up, grad_down)


def solution(mesh):
    small = (mesh.shape["dp"], mesh.shape["tensor"]) == (8, 4)
    return jax.shard_map(
        fast if small else general,
        mesh=mesh,
        in_specs=(
            P(None, "dp", "tensor"),
            P(),
            P("tensor"),
            P("tensor"),
            P("tensor", "dp"),
            P("tensor", "dp"),
            P("dp", "tensor"),
            P(),
            P("dp", None),
            P("dp", "tensor"),
        ),
        out_specs=(
            P("dp", "tensor"),
            P("dp", "tensor"),
            P("tensor", "dp"),
            P("tensor", "dp"),
            P("dp", "tensor"),
        ),
        check_vma=False,
    )
```

profile of v0, /device:TPU:0, one launch (start us, length us, event | category | flops | bytes accessed | tf_op | source)
XLA Modules:
  0.0 76.7 jit_solution(9834915434738200568)
XLA Ops:
  0.6 2.5 %shard_map.137 = (f32[24,1280]{1,0:T(8,128)}, bf16[24,2688]{1,0:T(8,128)(2,1)}) custom-call(s32[1,24]{1,0:T(1,128)} %chosen.3, f32[4]{0:T(128)} %mixw.3, bf16[4,128,1280]{2,1,0:T(8,128)(2,1)} %states.3, bf16[128,1280]{1,0:T(8,128)(2,1)} %cot.3, bf16[1280]{0:T(1024)(128)(2,1)} %router.1, bf16[1280]{0:T(1024)(128)(2,1)} %gain.1), custom_call_target="tpu_custom_call" | custom-call | tf_op jit(solution)/shard_map/pallas_call | solution.py:278
  3.1 4.1 %collective-permute-start.3 = (bf16[24,2688]{1,0:T(8,128)(2,1)}, bf16[24,2688]{1,0:T(8,128)(2,1)S(1)}, u32[]{:S(2)}, u32[]{:S(2)}) collective-permute-start(bf16[24,2688]{1,0:T(8,128)(2,1)} %get-tuple-element.34.after.refs_0_.load), channel_id=1, source_target_pairs={{0,16},{4,20},{8,24},{12,28},{16,0},{20,4},{24,8},{28,12},{1,17},{... | collective-permute-start | bytes 387080 | tf_op jit(solution)/shard_map/ppermute | solution.py:269
  7.3 1.6 %collective-permute-start.1 = (bf16[24,2688]{1,0:T(8,128)(2,1)}, bf16[24,2688]{1,0:T(8,128)(2,1)S(1)}, u32[]{:S(2)}, u32[]{:S(2)}) collective-permute-start(bf16[24,2688]{1,0:T(8,128)(2,1)} %get-tuple-element.34.after.refs_0_.load), channel_id=1, source_target_pairs={{0,8},{4,12},{8,0},{12,4},{16,24},{20,28},{24,16},{28,20},{1,9},{5... | collective-permute-start | bytes 387080 | tf_op jit(solution)/shard_map/ppermute | solution.py:269
  8.8 5.0 %collective-permute-done.3.refs_4_ = bf16[24,2688]{1,0:T(8,128)(2,1)S(1)} collective-permute-done((bf16[24,2688]{1,0:T(8,128)(2,1)}, bf16[24,2688]{1,0:T(8,128)(2,1)S(1)}, u32[]{:S(2)}, u32[]{:S(2)}) %collective-permute-start.3) | collective-permute-done | bytes 129056 | tf_op jit(solution)/shard_map/ppermute | solution.py:269
  13.8 0.7 collective-permute-start.5
  14.5 1.5 %collective-permute-start = (bf16[24,2688]{1,0:T(8,128)(2,1)}, bf16[24,2688]{1,0:T(8,128)(2,1)S(1)}, u32[]{:S(2)}, u32[]{:S(2)}) collective-permute-start(bf16[24,2688]{1,0:T(8,128)(2,1)} %get-tuple-element.34.after.refs_0_.load), channel_id=1, source_target_pairs={{0,4},{4,0},{8,12},{12,8},{16,20},{20,16},{24,28},{28,24},{1,5},{5... | collective-permute-start | bytes 387080 | tf_op jit(solution)/shard_map/ppermute | solution.py:269
  16.0 0.5 collective-permute-start.4
  16.5 0.0 collective-permute-done.1.refs_2_
  16.5 1.5 %collective-permute-start.2 = (bf16[24,2688]{1,0:T(8,128)(2,1)S(1)}, bf16[24,2688]{1,0:T(8,128)(2,1)S(1)}, u32[]{:S(2)}, u32[]{:S(2)}) collective-permute-start(bf16[24,2688]{1,0:T(8,128)(2,1)S(1)} %collective-permute-done.1.refs_2_), channel_id=1, source_target_pairs={{0,4},{4,0},{8,12},{12,8},{16,20},{20,16},{24,28},{28,24},{1,5},{5... | collective-permute-start | bytes 387080 | tf_op jit(solution)/shard_map/ppermute | solution.py:269
  18.1 0.7 collective-permute-done.5.refs_6_
  18.7 1.6 %collective-permute-start.6 = (bf16[24,2688]{1,0:T(8,128)(2,1)S(1)}, bf16[24,2688]{1,0:T(8,128)(2,1)S(1)}, u32[]{:S(2)}, u32[]{:S(2)}) collective-permute-start(bf16[24,2688]{1,0:T(8,128)(2,1)S(1)} %collective-permute-done.5.refs_6_), channel_id=1, source_target_pairs={{0,4},{4,0},{8,12},{12,8},{16,20},{20,16},{24,28},{28,24},{1,5},{5... | collective-permute-start | bytes 387080 | tf_op jit(solution)/shard_map/ppermute | solution.py:269
  20.3 0.0 copy-start.2
  20.3 0.9 %copy-done.2 = bf16[24,2688]{1,0:T(8,128)(2,1)S(1)} copy-done((bf16[24,2688]{1,0:T(8,128)(2,1)S(1)}, bf16[24,2688]{1,0:T(8,128)(2,1)}, u32[]{:S(2)}) %copy-start.2) | copy-done | bytes 129048
  21.2 0.7 copy-done.6
  21.9 3.0 %shard_map.138 = (bf16[864,1280]{1,0:T(8,128)(2,1)S(1)}, bf16[864,1280]{1,0:T(8,128)(2,1)S(1)}, bf16[864,1280]{1,0:T(8,128)(2,1)S(1)}, bf16[128,256]{1,0:T(8,128)(2,1)S(1)}, bf16[256,128]{1,0:T(8,128)(2,1)S(1)}) custom-call(bf16[24,2688]{1,0:T(8,128)(2,1)S(1)} %copy-done.2, s32[1,8]{1,0:T(1,128)S(1)} %copy-done.6, bf16[864,1280]{1,0:T(8,128)(2,1)} %bitcast.8, ...), custom_call_target="tpu_custom_call" | custom-call | bytes 13631488 | tf_op jit(solution)/shard_map/pallas_call | solution.py:293
  24.9 0.0 collective-permute-done.refs_1_
  24.9 0.0 collective-permute-done.4.refs_5_
  24.9 1.7 %collective-permute-done.2.refs_3_ = bf16[24,2688]{1,0:T(8,128)(2,1)S(1)} collective-permute-done((bf16[24,2688]{1,0:T(8,128)(2,1)S(1)}, bf16[24,2688]{1,0:T(8,128)(2,1)S(1)}, u32[]{:S(2)}, u32[]{:S(2)}) %collective-permute-start.2) | collective-permute-done | bytes 129056 | tf_op jit(solution)/shard_map/ppermute | solution.py:269
  26.6 1.5 %collective-permute-done.6.refs_7_ = bf16[24,2688]{1,0:T(8,128)(2,1)S(1)} collective-permute-done((bf16[24,2688]{1,0:T(8,128)(2,1)S(1)}, bf16[24,2688]{1,0:T(8,128)(2,1)S(1)}, u32[]{:S(2)}, u32[]{:S(2)}) %collective-permute-start.6) | collective-permute-done | bytes 129056 | tf_op jit(solution)/shard_map/ppermute | solution.py:269
  28.1 2.8 %shard_map.139 = (f32[64,2688]{1,0:T(8,128)S(1)}, bf16[64,2688]{1,0:T(8,128)(2,1)S(1)}, bf16[128,1280]{1,0:T(8,128)(2,1)S(1)}, bf16[128,1280]{1,0:T(8,128)(2,1)S(1)}) custom-call(bf16[128,256]{1,0:T(8,128)(2,1)S(1)} %get-tuple-element.35.want, bf16[24,2688]{1,0:T(8,128)(2,1)S(1)} %copy-done.2, bf16[24,2688]{1,0:T(8,128)(2,1)S(1)} %collective-permute-done.refs_1_, ...), custom_call_target="tpu_custom_call" | custom-call | tf_op jit(solution)/shard_map/pallas_call | solution.py:302
  30.9 0.0 copy-start.8
  31.0 0.0 copy-start.9
  31.0 0.0 copy-start
  31.0 0.0 copy-start.1
  31.0 0.0 copy-start.4
  31.0 0.0 copy-start.5
  31.0 0.0 copy-start.7
  31.0 0.1 collective-permute-start.7
  31.1 1.6 %collective-permute-done.7.got = bf16[64,2688]{1,0:T(8,128)(2,1)S(1)} collective-permute-done((bf16[64,2688]{1,0:T(8,128)(2,1)S(1)}, bf16[64,2688]{1,0:T(8,128)(2,1)S(1)}, u32[]{:S(2)}, u32[]{:S(2)}) %collective-permute-start.7) | collective-permute-done | bytes 344096 | tf_op jit(solution)/shard_map/ppermute | solution.py:272
  32.7 0.1 shard_map.140
  32.9 1.6 %collective-permute-start.8 = (bf16[64,2688]{1,0:T(8,128)(2,1)S(1)}, bf16[64,2688]{1,0:T(8,128)(2,1)S(1)}, u32[]{:S(2)}, u32[]{:S(2)}) collective-permute-start(bf16[64,2688]{1,0:T(8,128)(2,1)S(1)} %get-tuple-element.41.after), channel_id=1, source_target_pairs={{0,2},{1,3},{2,0},{3,1},{4,6},{5,7},{6,4},{7,5},{8,10},{9,11},{10,... | collective-permute-start | bytes 1032200 | tf_op jit(solution)/shard_map/ppermute | solution.py:272
  34.4 8.6 %collective-permute-done.8.got = bf16[64,2688]{1,0:T(8,128)(2,1)S(1)} collective-permute-done((bf16[64,2688]{1,0:T(8,128)(2,1)S(1)}, bf16[64,2688]{1,0:T(8,128)(2,1)S(1)}, u32[]{:S(2)}, u32[]{:S(2)}) %collective-permute-start.8) | collective-permute-done | bytes 344096 | tf_op jit(solution)/shard_map/ppermute | solution.py:272
  43.0 0.6 shard_map.142.own
  43.6 0.0 collective-permute-start.9
  43.6 0.0 copy-done.8
  43.7 0.0 copy-done.9
  43.7 0.0 copy-done
  43.7 0.0 copy-done.1
  43.7 0.0 copy-done.4
  43.7 0.0 copy-done.5
  43.7 0.0 copy-done.7
  43.7 1.6 %shard_map.141 = (bf16[128,1280]{1,0:T(8,128)(2,1)S(1)}, bf16[128,1280]{1,0:T(8,128)(2,1)S(1)}, bf16[128,24]{1,0:T(8,128)(2,1)S(1)}) custom-call(bf16[64,2688]{1,0:T(8,128)(2,1)S(1)} %get-tuple-element.41.after, s32[1,8]{1,0:T(1,128)S(1)} %copy-done.7, s32[1,24]{1,0:T(1,128)S(1)} %copy-done.4, f32[4]{0:T(128)S(1)} %copy-done.5, ...), custom_call_target="tpu_custom_call" | custom-call | bytes 3145728 | tf_op jit(solution)/shard_map/pallas_call | solution.py:311
  45.3 0.0 collective-permute-done.9.got
  45.3 1.6 %shard_map.143 = (bf16[24,2688]{1,0:T(8,128)(2,1)S(1)}, bf16[24,2688]{1,0:T(8,128)(2,1)S(1)}, bf16[24,2688]{1,0:T(8,128)(2,1)S(1)}, bf16[24,2688]{1,0:T(8,128)(2...) custom-call(bf16[256,128]{1,0:T(8,128)(2,1)S(1)} %get-tuple-element., ...), custom_call_target="tpu_custom_call" | custom-call | tf_op jit(solution)/shard_map/pallas_call | solution.py:321
  46.9 1.6 %collective-permute-start.10 = (bf16[24,2688]{1,0:T(8,128)(2,1)S(1)}, bf16[24,2688]{1,0:T(8,128)(2,1)S(1)}, u32[]{:S(2)}, u32[]{:S(2)}) collective-permute-start(bf16[24,2688]{1,0:T(8,128)(2,1)S(1)} %get-tuple-element.49), channel_id=1, source_target_pairs={{0,4},{4,0},{8,12},{12,8},{16,20},{20,16},{24,28},{28,24},{1,5},{5... | collective-permute-start | bytes 387080 | tf_op jit(solution)/shard_map/ppermute | solution.py:269
  48.5 0.5 collective-permute-start.11
  49.0 1.5 %collective-permute-start.13 = (bf16[24,2688]{1,0:T(8,128)(2,1)S(1)}, bf16[24,2688]{1,0:T(8,128)(2,1)S(1)}, u32[]{:S(2)}, u32[]{:S(2)}) collective-permute-start(bf16[24,2688]{1,0:T(8,128)(2,1)S(1)} %get-tuple-element.53), channel_id=1, source_target_pairs={{0,4},{4,0},{8,12},{12,8},{16,20},{20,16},{24,28},{28,24},{1,5},{5... | collective-permute-start | bytes 387080 | tf_op jit(solution)/shard_map/ppermute | solution.py:269
  50.5 0.5 collective-permute-start.14
  51.0 2.9 %fusion = f32[1280,864]{0,1:T(8,128)} fusion(bf16[128,1280]{1,0:T(8,128)(2,1)S(1)} %get-tuple-element.58, bf16[128,864]{1,0:T(8,128)(2,1)S(1)} %get-tuple-element.59), kind=kOutput, calls=%fused_computation.3 | convolution fusion | flops 283115520 | bytes 4972544 | tf_op jit(solution)/shard_map/dot_general | solution.py:338
  53.9 2.9 %fusion.1 = f32[1280,864]{0,1:T(8,128)} fusion(bf16[128,1280]{1,0:T(8,128)(2,1)S(1)} %get-tuple-element.58, bf16[128,864]{1,0:T(8,128)(2,1)S(1)} %get-tuple-element.60), kind=kOutput, calls=%fused_computation.4 | convolution fusion | flops 283115520 | bytes 4972544 | tf_op jit(solution)/shard_map/dot_general | solution.py:339
  56.8 4.4 %collective-permute-done.14 = bf16[24,2688]{1,0:T(8,128)(2,1)S(1)} collective-permute-done((bf16[24,2688]{1,0:T(8,128)(2,1)S(1)}, bf16[24,2688]{1,0:T(8,128)(2,1)S(1)}, u32[]{:S(2)}, u32[]{:S(2)}) %collective-permute-start.14) | collective-permute-done | bytes 129056 | tf_op jit(solution)/shard_map/ppermute | solution.py:269
  61.2 0.4 collective-permute-start.15
  61.5 0.0 collective-permute-done.11
  61.6 1.8 %collective-permute-start.12 = (bf16[24,2688]{1,0:T(8,128)(2,1)S(1)}, bf16[24,2688]{1,0:T(8,128)(2,1)S(1)}, u32[]{:S(2)}, u32[]{:S(2)}) collective-permute-start(bf16[24,2688]{1,0:T(8,128)(2,1)S(1)} %add_convert_fusion.2), channel_id=1, source_target_pairs={{0,8},{4,12},{8,0},{12,4},{16,24},{20,28},{24,16},{28,20},{1,9},{5... | collective-permute-start | bytes 387080 | tf_op jit(solution)/shard_map/ppermute | solution.py:269
  63.4 0.0 collective-permute-done.13
  63.4 4.2 %collective-permute-done.15 = bf16[24,2688]{1,0:T(8,128)(2,1)S(1)} collective-permute-done((bf16[24,2688]{1,0:T(8,128)(2,1)S(1)}, bf16[24,2688]{1,0:T(8,128)(2,1)S(1)}, u32[]{:S(2)}, u32[]{:S(2)}) %collective-permute-start.15) | collective-permute-done | bytes 129056 | tf_op jit(solution)/shard_map/ppermute | solution.py:269
  67.6 0.1 add_convert_fusion
  67.6 3.3 %collective-permute-start.16 = (bf16[24,2688]{1,0:T(8,128)(2,1)S(1)}, bf16[24,2688]{1,0:T(8,128)(2,1)S(1)}, u32[]{:S(2)}, u32[]{:S(2)}) collective-permute-start(bf16[24,2688]{1,0:T(8,128)(2,1)S(1)} %add_convert_fusion), channel_id=1, source_target_pairs={{0,16},{4,20},{8,24},{12,28},{16,0},{20,4},{24,8},{28,12},{1,17},{... | collective-permute-start | bytes 387080 | tf_op jit(solution)/shard_map/ppermute | solution.py:269
  71.0 2.9 %fusion.2 = f32[864,1280]{1,0:T(8,128)} fusion(bf16[128,864]{1,0:T(8,128)(2,1)S(1)} %get-tuple-element.61, bf16[128,1280]{1,0:T(8,128)(2,1)S(1)} %get-tuple-element.62), kind=kOutput, calls=%fused_computation.5 | convolution fusion | flops 283115520 | bytes 4972544 | tf_op jit(solution)/shard_map/dot_general | solution.py:337
  73.8 0.0 collective-permute-done.10.refs_1_
  73.8 0.0 collective-permute-done.12.refs_2_
  73.8 1.8 %collective-permute-done.16.refs_3_ = bf16[24,2688]{1,0:T(8,128)(2,1)S(1)} collective-permute-done((bf16[24,2688]{1,0:T(8,128)(2,1)S(1)}, bf16[24,2688]{1,0:T(8,128)(2,1)S(1)}, u32[]{:S(2)}, u32[]{:S(2)}) %collective-permute-start.16) | collective-permute-done | bytes 129056 | tf_op jit(solution)/shard_map/ppermute | solution.py:269
  75.6 0.0 copy-done.3
  75.6 1.1 %shard_map.144 = (bf16[128,1280]{1,0:T(8,128)(2,1)}, bf16[128,1280]{1,0:T(8,128)(2,1)}) custom-call(bf16[128,24]{1,0:T(8,128)(2,1)S(1)} %get-tuple-element.42.want, f32[24,1280]{1,0:T(8,128)S(1)} %copy-done.3, bf16[24,2688]{1,0:T(8,128)(2,1)S(1)} %copy-done.2, bf16[128,1280]{1,0:T(8,128)(2,1)S(1)} %get-tuple-element.44.mixed, ...), custom_call_target="tpu_custom_call" | custom-call | tf_op jit(solution)/shard_map/pallas_call | solution.py:340
  (6 shorter events, 0.1 us)
Async XLA Ops:
  3.1 10.7 %collective-permute-start.3 = (bf16[24,2688]{1,0:T(8,128)(2,1)}, bf16[24,2688]{1,0:T(8,128)(2,1)S(1)}, u32[]{:S(2)}, u32[]{:S(2)}) collective-permute-start(bf16[24,2688]{1,0:T(8,128)(2,1)} %get-tuple-element.34.after.refs_0_.load), channel_id=1, source_target_pairs={{0,16},{4,20},{8,24},{12,28},{16,0},{20,4},{24,8},{28,12},{1,17},{... | collective-permute-start | bytes 387080 | tf_op jit(solution)/shard_map/ppermute | solution.py:269
  7.3 9.3 %collective-permute-start.1 = (bf16[24,2688]{1,0:T(8,128)(2,1)}, bf16[24,2688]{1,0:T(8,128)(2,1)S(1)}, u32[]{:S(2)}, u32[]{:S(2)}) collective-permute-start(bf16[24,2688]{1,0:T(8,128)(2,1)} %get-tuple-element.34.after.refs_0_.load), channel_id=1, source_target_pairs={{0,8},{4,12},{8,0},{12,4},{16,24},{20,28},{24,16},{28,20},{1,9},{5... | collective-permute-start | bytes 387080 | tf_op jit(solution)/shard_map/ppermute | solution.py:269
  13.8 4.9 %collective-permute-start.5 = (bf16[24,2688]{1,0:T(8,128)(2,1)S(1)}, bf16[24,2688]{1,0:T(8,128)(2,1)S(1)}, u32[]{:S(2)}, u32[]{:S(2)}) collective-permute-start(bf16[24,2688]{1,0:T(8,128)(2,1)S(1)} %collective-permute-done.3.refs_4_), channel_id=1, source_target_pairs={{0,8},{4,12},{8,0},{12,4},{16,24},{20,28},{24,16},{28,20},{1,9},{5... | collective-permute-start | bytes 387080 | tf_op jit(solution)/shard_map/ppermute | solution.py:269
  14.5 10.4 %collective-permute-start = (bf16[24,2688]{1,0:T(8,128)(2,1)}, bf16[24,2688]{1,0:T(8,128)(2,1)S(1)}, u32[]{:S(2)}, u32[]{:S(2)}) collective-permute-start(bf16[24,2688]{1,0:T(8,128)(2,1)} %get-tuple-element.34.after.refs_0_.load), channel_id=1, source_target_pairs={{0,4},{4,0},{8,12},{12,8},{16,20},{20,16},{24,28},{28,24},{1,5},{5... | collective-permute-start | bytes 387080 | tf_op jit(solution)/shard_map/ppermute | solution.py:269
  16.0 8.9 %collective-permute-start.4 = (bf16[24,2688]{1,0:T(8,128)(2,1)S(1)}, bf16[24,2688]{1,0:T(8,128)(2,1)S(1)}, u32[]{:S(2)}, u32[]{:S(2)}) collective-permute-start(bf16[24,2688]{1,0:T(8,128)(2,1)S(1)} %collective-permute-done.3.refs_4_), channel_id=1, source_target_pairs={{0,4},{4,0},{8,12},{12,8},{16,20},{20,16},{24,28},{28,24},{1,5},{5... | collective-permute-start | bytes 387080 | tf_op jit(solution)/shard_map/ppermute | solution.py:269
  16.5 10.0 %collective-permute-start.2 = (bf16[24,2688]{1,0:T(8,128)(2,1)S(1)}, bf16[24,2688]{1,0:T(8,128)(2,1)S(1)}, u32[]{:S(2)}, u32[]{:S(2)}) collective-permute-start(bf16[24,2688]{1,0:T(8,128)(2,1)S(1)} %collective-permute-done.1.refs_2_), channel_id=1, source_target_pairs={{0,4},{4,0},{8,12},{12,8},{16,20},{20,16},{24,28},{28,24},{1,5},{5... | collective-permute-start | bytes 387080 | tf_op jit(solution)/shard_map/ppermute | solution.py:269
  18.7 9.4 %collective-permute-start.6 = (bf16[24,2688]{1,0:T(8,128)(2,1)S(1)}, bf16[24,2688]{1,0:T(8,128)(2,1)S(1)}, u32[]{:S(2)}, u32[]{:S(2)}) collective-permute-start(bf16[24,2688]{1,0:T(8,128)(2,1)S(1)} %collective-permute-done.5.refs_6_), channel_id=1, source_target_pairs={{0,4},{4,0},{8,12},{12,8},{16,20},{20,16},{24,28},{28,24},{1,5},{5... | collective-permute-start | bytes 387080 | tf_op jit(solution)/shard_map/ppermute | solution.py:269
  20.3 0.9 %copy-start.2 = (bf16[24,2688]{1,0:T(8,128)(2,1)S(1)}, bf16[24,2688]{1,0:T(8,128)(2,1)}, u32[]{:S(2)}) copy-start(bf16[24,2688]{1,0:T(8,128)(2,1)} %get-tuple-element.34.after.refs_0_.load) | copy-start | bytes 387076
  21.2 0.7 copy-start.6
  30.9 12.7 %copy-start.8 = (bf16[1280]{0:T(1024)(128)(2,1)S(1)}, bf16[1280]{0:T(1024)(128)(2,1)}, u32[]{:S(2)}) copy-start(bf16[1280]{0:T(1024)(128)(2,1)} %router.1) | copy-start | bytes 7684
  31.0 12.7 %copy-start.9 = (bf16[1280]{0:T(1024)(128)(2,1)S(1)}, bf16[1280]{0:T(1024)(128)(2,1)}, u32[]{:S(2)}) copy-start(bf16[1280]{0:T(1024)(128)(2,1)} %gain.1) | copy-start | bytes 7684
  31.0 12.7 %copy-start = (bf16[4,128,1280]{2,1,0:T(8,128)(2,1)S(1)}, bf16[4,128,1280]{2,1,0:T(8,128)(2,1)}, u32[]{:S(2)}) copy-start(bf16[4,128,1280]{2,1,0:T(8,128)(2,1)} %states.3) | copy-start | bytes 3932164
  31.0 12.7 %copy-start.1 = (bf16[128,1280]{1,0:T(8,128)(2,1)S(1)}, bf16[128,1280]{1,0:T(8,128)(2,1)}, u32[]{:S(2)}) copy-start(bf16[128,1280]{1,0:T(8,128)(2,1)} %cot.3) | copy-start | bytes 983044
  31.0 12.7 %copy-start.4 = (s32[1,24]{1,0:T(1,128)S(1)}, s32[1,24]{1,0:T(1,128)}, u32[]{:S(2)}) copy-start(s32[1,24]{1,0:T(1,128)} %chosen.3) | copy-start | bytes 292
  31.0 12.7 %copy-start.5 = (f32[4]{0:T(128)S(1)}, f32[4]{0:T(128)}, u32[]{:S(2)}) copy-start(f32[4]{0:T(128)} %mixw.3) | copy-start | bytes 52
  31.0 12.7 %copy-start.7 = (s32[1,8]{1,0:T(1,128)S(1)}, s32[1,8]{1,0:T(1,128)}, u32[]{:S(2)}) copy-start(s32[1,8]{1,0:T(1,128)} %counts.1) | copy-start | bytes 100
  31.0 1.7 %collective-permute-start.7 = (bf16[64,2688]{1,0:T(8,128)(2,1)S(1)}, bf16[64,2688]{1,0:T(8,128)(2,1)S(1)}, u32[]{:S(2)}, u32[]{:S(2)}) collective-permute-start(bf16[64,2688]{1,0:T(8,128)(2,1)S(1)} %get-tuple-element.40), channel_id=1, source_target_pairs={{0,1},{1,0},{2,3},{3,2},{4,5},{5,4},{6,7},{7,6},{8,9},{9,8},{10,11... | collective-permute-start | bytes 1032200 | tf_op jit(solution)/shard_map/ppermute | solution.py:272
  32.9 10.2 %collective-permute-start.8 = (bf16[64,2688]{1,0:T(8,128)(2,1)S(1)}, bf16[64,2688]{1,0:T(8,128)(2,1)S(1)}, u32[]{:S(2)}, u32[]{:S(2)}) collective-permute-start(bf16[64,2688]{1,0:T(8,128)(2,1)S(1)} %get-tuple-element.41.after), channel_id=1, source_target_pairs={{0,2},{1,3},{2,0},{3,1},{4,6},{5,7},{6,4},{7,5},{8,10},{9,11},{10,... | collective-permute-start | bytes 1032200 | tf_op jit(solution)/shard_map/ppermute | solution.py:272
  43.6 1.7 %collective-permute-start.9 = (bf16[64,2688]{1,0:T(8,128)(2,1)S(1)}, bf16[64,2688]{1,0:T(8,128)(2,1)S(1)}, u32[]{:S(2)}, u32[]{:S(2)}) collective-permute-start(bf16[64,2688]{1,0:T(8,128)(2,1)S(1)} %shard_map.142.own), channel_id=1, source_target_pairs={{0,1},{1,0},{2,3},{3,2},{4,5},{5,4},{6,7},{7,6},{8,9},{9,8},{10,11... | collective-permute-start | bytes 1032200 | tf_op jit(solution)/shard_map/ppermute | solution.py:272
  46.9 26.9 %collective-permute-start.10 = (bf16[24,2688]{1,0:T(8,128)(2,1)S(1)}, bf16[24,2688]{1,0:T(8,128)(2,1)S(1)}, u32[]{:S(2)}, u32[]{:S(2)}) collective-permute-start(bf16[24,2688]{1,0:T(8,128)(2,1)S(1)} %get-tuple-element.49), channel_id=1, source_target_pairs={{0,4},{4,0},{8,12},{12,8},{16,20},{20,16},{24,28},{28,24},{1,5},{5... | collective-permute-start | bytes 387080 | tf_op jit(solution)/shard_map/ppermute | solution.py:269
  48.5 13.0 %collective-permute-start.11 = (bf16[24,2688]{1,0:T(8,128)(2,1)S(1)}, bf16[24,2688]{1,0:T(8,128)(2,1)S(1)}, u32[]{:S(2)}, u32[]{:S(2)}) collective-permute-start(bf16[24,2688]{1,0:T(8,128)(2,1)S(1)} %get-tuple-element.51), channel_id=1, source_target_pairs={{0,4},{4,0},{8,12},{12,8},{16,20},{20,16},{24,28},{28,24},{1,5},{5... | collective-permute-start | bytes 387080 | tf_op jit(solution)/shard_map/ppermute | solution.py:269
  49.0 14.4 %collective-permute-start.13 = (bf16[24,2688]{1,0:T(8,128)(2,1)S(1)}, bf16[24,2688]{1,0:T(8,128)(2,1)S(1)}, u32[]{:S(2)}, u32[]{:S(2)}) collective-permute-start(bf16[24,2688]{1,0:T(8,128)(2,1)S(1)} %get-tuple-element.53), channel_id=1, source_target_pairs={{0,4},{4,0},{8,12},{12,8},{16,20},{20,16},{24,28},{28,24},{1,5},{5... | collective-permute-start | bytes 387080 | tf_op jit(solution)/shard_map/ppermute | solution.py:269
  50.5 10.6 %collective-permute-start.14 = (bf16[24,2688]{1,0:T(8,128)(2,1)S(1)}, bf16[24,2688]{1,0:T(8,128)(2,1)S(1)}, u32[]{:S(2)}, u32[]{:S(2)}) collective-permute-start(bf16[24,2688]{1,0:T(8,128)(2,1)S(1)} %get-tuple-element.55), channel_id=1, source_target_pairs={{0,4},{4,0},{8,12},{12,8},{16,20},{20,16},{24,28},{28,24},{1,5},{5... | collective-permute-start | bytes 387080 | tf_op jit(solution)/shard_map/ppermute | solution.py:269
  61.2 6.4 %collective-permute-start.15 = (bf16[24,2688]{1,0:T(8,128)(2,1)S(1)}, bf16[24,2688]{1,0:T(8,128)(2,1)S(1)}, u32[]{:S(2)}, u32[]{:S(2)}) collective-permute-start(bf16[24,2688]{1,0:T(8,128)(2,1)S(1)} %add_convert_fusion.1), channel_id=1, source_target_pairs={{0,8},{4,12},{8,0},{12,4},{16,24},{20,28},{24,16},{28,20},{1,9},{5... | collective-permute-start | bytes 387080 | tf_op jit(solution)/shard_map/ppermute | solution.py:269
  61.6 12.3 %collective-permute-start.12 = (bf16[24,2688]{1,0:T(8,128)(2,1)S(1)}, bf16[24,2688]{1,0:T(8,128)(2,1)S(1)}, u32[]{:S(2)}, u32[]{:S(2)}) collective-permute-start(bf16[24,2688]{1,0:T(8,128)(2,1)S(1)} %add_convert_fusion.2), channel_id=1, source_target_pairs={{0,8},{4,12},{8,0},{12,4},{16,24},{20,28},{24,16},{28,20},{1,9},{5... | collective-permute-start | bytes 387080 | tf_op jit(solution)/shard_map/ppermute | solution.py:269
  67.6 8.0 %collective-permute-start.16 = (bf16[24,2688]{1,0:T(8,128)(2,1)S(1)}, bf16[24,2688]{1,0:T(8,128)(2,1)S(1)}, u32[]{:S(2)}, u32[]{:S(2)}) collective-permute-start(bf16[24,2688]{1,0:T(8,128)(2,1)S(1)} %add_convert_fusion), channel_id=1, source_target_pairs={{0,16},{4,20},{8,24},{12,28},{16,0},{20,4},{24,8},{28,12},{1,17},{... | collective-permute-start | bytes 387080 | tf_op jit(solution)/shard_map/ppermute | solution.py:269
  71.0 4.7 %copy-start.3 = (f32[24,1280]{1,0:T(8,128)S(1)}, f32[24,1280]{1,0:T(8,128)}, u32[]{:S(2)}) copy-start(f32[24,1280]{1,0:T(8,128)} %get-tuple-element.43.picked) | copy-start | bytes 368644
where the time goes:
time: 76.9 us; the launch traced here: 76.7 us
  waiting for transfers between devices  29.4 us (38%)
  starting transfers between devices  22.8 us (30%)
  Pallas kernels  13.3 us (17%)
  matrix products  8.62 us (11%)
  local copies, waits for them, and re-layouts  1.62 us (2%)
  between operations  0.87 us (1%)
    ppermute x14, starting transfers between devices, over_dp(): return lax.ppermute(x, 'dp', [(i, i ^ k) for i in range(slots)])  21.2 us
    ppermute x14, waiting for transfers between devices, over_dp(): return lax.ppermute(x, 'dp', [(i, i ^ k) for i in range(slots)])  19.1 us
    ppermute x3, waiting for transfers between devices, over_tensor(): return lax.ppermute(x, 'tensor', [(i, i ^ k) for i in range(tensor)])  10.2 us
    pallas_call x1, Pallas kernels, fast(): call(functools.partial(weights_kernel, slots, slot_rows, total), (weight,...  3.03 us
    dot_general x1, matrix products, fast(): grad_up = dot_tn(dup, pg).T  2.88 us
    dot_general x1, matrix products, fast(): grad_gate = dot_tn(dgate, pg).T  2.88 us
    dot_general x1, matrix products, fast(): grad_down = dot_tn(hidden, cot)  2.86 us
    pallas_call x1, Pallas kernels, fast(): call(functools.partial(first_kernel, slots, cap, slot_rows, lanes), (sds(...  2.82 us
  transfers between devices with their start and end apart: 17, of which 9 were waited for; matrix products, arithmetic and copies ran while one was open for 11% of the time, Pallas kernels for 6%

commit v1 on v0

--- a/solution.py
+++ b/solution.py
@@ -56,19 +56,6 @@
     return jnp.dot(a, b, preferred_element_type=f32)
 
 
-def placement(counts_ref, me, slots, slot_rows, total, packed_axis):
-    shape = (total, slots * slot_rows) if packed_axis == 0 else (slots * slot_rows, total)
-    packed = lax.broadcasted_iota(jnp.int32, shape, packed_axis)
-    slotted = lax.broadcasted_iota(jnp.int32, shape, 1 - packed_axis)
-    hit, at = packed < 0, 0
-    for k in range(slots):
-        here = counts_ref[0, me ^ k]
-        row = slotted - k * slot_rows
-        hit = hit | ((row >= 0) & (row < here) & (packed == row + at))
-        at = at + here
-    return jnp.where(hit, 1.0, 0.0).astype(bf16)
-
-
 def fetch(pairs, sem):
     copies = [pltpu.make_async_copy(src, dst, sem.at[i]) for i, (src, dst) in enumerate(pairs)]
     for copy in copies:
@@ -76,17 +63,18 @@
     return copies
 
 
-def pick_kernel(cap, chosen, mixw, states, cot, router, gain, picked_ref, load_ref, *scratch):
+def pick_kernel(cap, counts, chosen, mixw, states, cot, router, gain, picked_ref, load_ref, *scratch):
     *places, sem = scratch
-    for copy in fetch(list(zip((chosen, mixw, states, cot, router, gain), places)), sem):
+    for copy in fetch(list(zip((counts, chosen, mixw, states, cot, router, gain), places)), sem):
         copy.wait()
-    chosen, mixw, states, cot, router, gain = places
+    counts, chosen, mixw, states, cot, router, gain = places
+    mine = counts[0, lax.axis_index("dp")]
     tokens, width = cot.shape
     row = lax.broadcasted_iota(jnp.int32, (cap, tokens), 0)
     col = lax.broadcasted_iota(jnp.int32, (cap, tokens), 1)
     want = jnp.zeros((cap, tokens), f32)
     for k in range(cap):
-        want = jnp.where((row == k) & (col == chosen[0, k]), 1.0, want)
+        want = jnp.where((row == k) & (col == chosen[0, k]) & (k < mine), 1.0, want)
     want = want.astype(bf16)
     picked = mixw[0] * dot_nn(want, states[0])
     for j in range(1, states.shape[0]):
@@ -100,15 +88,10 @@
     load_ref[:, 2 * width :] = in_lanes(terms(logit) + terms(square), 128, first).astype(bf16)
 
 
-def weights_kernel(slots, slot_rows, total, after, *refs):
-    *pairs, pack_ref, unpack_ref, counts, sem = refs
+def weights_kernel(after, *refs):
+    *pairs, sem = refs
     half = len(pairs) // 2
-    copies = fetch(list(zip(pairs[: half + 1], [counts] + pairs[half + 1 :])), sem)
-    copies[0].wait()
-    me = lax.axis_index("dp")
-    pack_ref[...] = placement(counts, me, slots, slot_rows, total, 0)
-    unpack_ref[...] = placement(counts, me, slots, slot_rows, total, 1)
-    for copy in copies[1:]:
+    for copy in fetch(list(zip(pairs[:half], pairs[half:])), sem):
         copy.wait()
 
 
@@ -134,33 +117,29 @@
     cot_ref[...] = jnp.where(keep, cot[...].astype(f32), 0.0).astype(bf16)
 
 
-def first_kernel(slots, cap, slot_rows, lanes, want, *refs):
-    blocks = refs[:slots]
-    gate_w, up_w, down_w, own_ref, send_ref, pg_ref, cot_ref, rows_ref, sums_ref, mine_ref, sem = refs[slots:]
-    copies = fetch([(blocks[0], mine_ref)], sem)
+def first_kernel(slots, lanes, *refs):
+    blocks, (gate_w, up_w, down_w, own_ref, send_ref, rows_ref, sums_ref) = refs[:slots], refs[slots : slots + 7]
+    if len(refs) > slots + 7:
+        mine_ref, sem = refs[slots + 7 :]
+        (copy,) = fetch([(blocks[0], mine_ref)], sem)
+        copy.wait()
+        blocks = (mine_ref,) + blocks[1:]
     core = lax.axis_index("tensor") % 2
     ff, width = gate_w.shape
-    total = pg_ref.shape[0]
-    for k in reversed(range(slots)):
-        if k == 0:
-            copies[0].wait()
-        rows_ref[k * slot_rows : k * slot_rows + cap, :] = (blocks[k] if k else mine_ref)[...]
-        rows_ref[k * slot_rows + cap : (k + 1) * slot_rows, :] = jnp.zeros((slot_rows - cap, rows_ref.shape[1]), bf16)
-    pg = dot_nn(want[...], rows_ref[:, :width]).astype(bf16)
-    cot = dot_nn(want[...], rows_ref[:, width : 2 * width]).astype(bf16)
-    pg_ref[...] = pg
-    cot_ref[...] = cot
+    rows = jnp.concatenate([block[...].astype(f32) for block in blocks], axis=0)
     spare = lanes - ff
-    zeros = jnp.zeros((total, spare), f32)
+    zeros = jnp.zeros((rows.shape[0], spare), f32)
+    sums_ref[:, ff:lanes] = rows[:, 2 * width : 2 * width + spare]
+    rows_ref[...] = rows[:, : 2 * width].astype(bf16)
+    pg = rows_ref[:, :width]
     sums_ref[:, :ff] = dot_nt(pg, gate_w[...])
-    sums_ref[:, ff:lanes] = dot_nn(want[...], rows_ref[:, 2 * width :])[:, :spare]
     sums_ref[:, lanes : lanes + ff] = dot_nt(pg, up_w[...])
     sums_ref[:, lanes + ff : 2 * lanes] = zeros
-    sums_ref[:, 2 * lanes : 2 * lanes + ff] = dot_nt(cot, down_w[...])
+    sums_ref[:, 2 * lanes : 2 * lanes + ff] = dot_nt(rows_ref[:, width:], down_w[...])
     sums_ref[:, 2 * lanes + ff :] = zeros
-    half = total // 2
-    own_ref[...] = sums_ref[pl.ds(pl.multiple_of(core * half, half), half), :]
-    send_ref[...] = sums_ref[pl.ds(pl.multiple_of((1 - core) * half, half), half), :].astype(bf16)
+    half = own_ref.shape[0]
+    own_ref[...] = sums_ref[pl.ds(pl.multiple_of(core * half, 8), half), :]
+    send_ref[...] = sums_ref[pl.ds(pl.multiple_of((1 - core) * half, 8), half), :].astype(bf16)
 
 
 def add_kernel(own, got, out_ref, sum_ref):
@@ -204,29 +183,54 @@
     out_ref[:, 2 * lanes + ff :] = zeros
 
 
-def second_kernel(slots, cap, slot_rows, lanes, want, own, got, gate_w, up_w, down_w, *refs):
-    outs = refs[:slots]
-    hidden_ref, dgate_ref, dup_ref, act_ref, rows_ref = refs[slots:]
+def second_kernel(slots, lanes, own, got, gate_w, up_w, down_w, *refs):
+    outs, (act_ref,) = refs[:slots], refs[slots:]
     core = lax.axis_index("tensor") % 2
     ff, width = gate_w.shape
-    half = own.shape[0]
-    total = 2 * half
-    act_ref[pl.ds(pl.multiple_of(core * half, half), half), :] = own[...]
-    act_ref[pl.ds(pl.multiple_of((1 - core) * half, half), half), :] = got[...]
-    hidden = act_ref[:, :ff]
-    dgate = act_ref[:, lanes : lanes + ff]
-    dup = act_ref[:, 2 * lanes : 2 * lanes + ff]
-    hidden_ref[...] = hidden
-    dgate_ref[...] = dgate
-    dup_ref[...] = dup
-    rows_ref[:, :width] = dot_nn(hidden, down_w[...]).astype(bf16)
-    rows_ref[:, width : 2 * width] = (dot_nn(dgate, gate_w[...]) + dot_nn(dup, up_w[...])).astype(bf16)
+    cap = outs[0].shape[0]
+    mine, other = own[...].astype(f32), got[...].astype(f32)
+    order = (jnp.where(core == 0, mine, other), jnp.where(core == 0, other, mine))
+    act_ref[...] = jnp.concatenate(order, axis=0).astype(bf16)
     spare = lanes - ff
-    rows_ref[:, 2 * width : 2 * width + spare] = act_ref[:, ff:lanes]
-    rows_ref[:, 2 * width + spare :] = jnp.zeros((total, rows_ref.shape[1] - 2 * width - spare), bf16)
-    slotted = dot_nn(want[...], rows_ref[...]).astype(bf16)
-    for k in range(slots):
-        outs[k][...] = slotted[k * slot_rows : k * slot_rows + cap]
+    update = dot_nn(act_ref[:, :ff], down_w[...])
+    dnormed = dot_nn(act_ref[:, lanes : lanes + ff], gate_w[...])
+    dnormed = dnormed + dot_nn(act_ref[:, 2 * lanes : 2 * lanes + ff], up_w[...])
+    scalars = act_ref[:, ff:lanes].astype(f32)
+    for k, out in enumerate(outs):
+        rows = slice(k * cap, (k + 1) * cap)
+        out[:, :width] = update[rows].astype(bf16)
+        out[:, width : 2 * width] = dnormed[rows].astype(bf16)
+        out[:, 2 * width : 2 * width + spare] = scalars[rows].astype(bf16)
+        out[:, 2 * width + spare :] = jnp.zeros((cap, out.shape[1] - 2 * width - spare), bf16)
+
+
+def join_kernel(lanes, parts, *refs):
+    acts, taken, (hidden, dgate, dup, pg, cot) = refs[:parts], refs[parts : 2 * parts], refs[2 * parts :]
+    ff, width = hidden.shape[1], pg.shape[1]
+    start = 0
+    for act, rows in zip(acts, taken):
+        at = slice(start, start + act.shape[0])
+        start += act.shape[0]
+        for j, out in enumerate((hidden, dgate, dup)):
+            out[at, :] = act[:, j * lanes : j * lanes + ff]
+        pg[at, :] = rows[:, :width]
+        cot[at, :] = rows[:, width:]
+
+
+def grad_kernel(tile, count, *refs):
+    lefts, rights, outs, buffers, (sem,) = (refs[i * count : (i + 1) * count] for i in range(5))
+    copies = []
+    for left, right, out, buffer in zip(lefts, rights, outs, buffers):
+        for start in range(0, left.shape[1], tile):
+            at = slice(start, min(start + tile, left.shape[1]))
+            buffer[at, :] = lax.dot_general(
+                left[:, at], right[...], (((0,), (0,)), ((), ())), preferred_element_type=f32
+            )
+            copy = pltpu.make_async_copy(buffer.at[at, :], out.at[at, :], sem.at[len(copies)])
+            copy.start()
+            copies.append(copy)
+    for copy in copies:
+        copy.wait()
 
 
 def last_kernel(want, picked, load, mixed, cot, router, gain, *refs):
@@ -257,12 +261,10 @@
     tokens, width = cotangent.shape
     ff = gate_weight.shape[1]
     model_width = width * tensor
-    total = counts.shape[0] * counts.shape[1] * tokens // 8
-    half = total // 2
-    slot_rows = (cap + 15) // 16 * 16
     lanes = (ff + 2 * PARTS * tensor + 127) // 128 * 128
     columns = 2 * width + 128
-    anywhere = pl.BlockSpec(memory_space=pltpu.HBM)
+    hbm = pl.BlockSpec(memory_space=pltpu.HBM)
+    anywhere = pl.BlockSpec(memory_space=pl.ANY)
     block = sds((cap, columns), bf16)
 
     def over_dp(x, k):
@@ -278,68 +280,96 @@
     picked, load = call(
         functools.partial(pick_kernel, cap),
         (sds((cap, width), f32), block),
-        [anywhere] * 6,
-        [copy_of(chosen, pltpu.SMEM), copy_of(mix_weights, pltpu.SMEM)]
+        [hbm] * 7,
+        [copy_of(x, pltpu.SMEM) for x in (counts, chosen, mix_weights)]
         + [copy_of(x) for x in (states, cotangent, router, norm_gain)]
         + [sem],
         vmem=65_000_000,
-    )(chosen, mix_weights, states, cotangent, router, norm_gain)
-    gate_t, up_t = gate_weight.T, up_weight.T
+    )(counts, chosen, mix_weights, states, cotangent, router, norm_gain)
     blocks = {0: load}
     for step in (4, 2, 1):
         for k in list(blocks):
             blocks[k ^ step] = over_dp(blocks[k], step)
     weight = sds((ff, width), bf16)
-    gate_v, up_v, down_v, pack, unpack = call(
-        functools.partial(weights_kernel, slots, slot_rows, total),
-        (weight,) * 3 + (sds((total, slots * slot_rows), bf16), sds((slots * slot_rows, total), bf16)),
-        [pl.BlockSpec(memory_space=pl.ANY)] + [anywhere] * 4,
-        [copy_of(counts, pltpu.SMEM), sem],
-        nbytes=13 << 20,
-        vmem=48_000_000,
-    )(load, counts, gate_t, up_t, down_weight)
-    weights = (gate_v, up_v, down_v)
-    own, send, pg, cot = call(
-        functools.partial(first_kernel, slots, cap, slot_rows, lanes),
-        (sds((half, 3 * lanes), f32), sds((half, 3 * lanes), bf16), sds((total, width), bf16), sds((total, width), bf16)),
-        [VMEM, pl.BlockSpec(memory_space=pl.ANY)] + [VMEM] * (slots + 2),
-        [pltpu.VMEM((slots * slot_rows, columns), bf16), pltpu.VMEM((total, 3 * lanes), f32), copy_of(load), sem],
-    )(pack, *[blocks[k] for k in range(slots)], *weights)
-    send, own = call(
-        add_kernel, (sds((half, 3 * lanes), bf16), sds((half, 3 * lanes), f32)), [VMEM] * 2
-    )(own, over_tensor(send, 1))
+    weights = call(
+        weights_kernel, (weight,) * 3, [anywhere] + [hbm] * 3, [sem], nbytes=13 << 20, vmem=48_000_000,
+    )(load, gate_weight.T, up_weight.T, down_weight)
+
+    def summed(chosen_slots):
+        part = len(chosen_slots)
+        rows, half = part * cap, part * cap // 2
+        near = chosen_slots[0] == 0
+        own, send, taken = call(
+            functools.partial(first_kernel, part, lanes),
+            (sds((half, 3 * lanes), f32), sds((half, 3 * lanes), bf16), sds((rows, 2 * width), bf16)),
+            [anywhere if near else VMEM] + [VMEM] * (part + 2),
+            [pltpu.VMEM((rows, 3 * lanes), f32)] + ([copy_of(load), sem] if near else []),
+        )(*[blocks[k] for k in chosen_slots], *weights)
+        send, own = call(
+            add_kernel, (sds((half, 3 * lanes), bf16), sds((half, 3 * lanes), f32)), [VMEM] * 2
+        )(own, over_tensor(send, 1))
+        return own, over_tensor(send, 2), taken
+
+    def acted(part, own, got):
+        act = call(functools.partial(act_kernel, ff, lanes, model_width), sds(got.shape, bf16), [VMEM] * 2)(own, got)
+        *some, act = call(
+            functools.partial(second_kernel, part, lanes),
+            tuple([block] * part + [sds((part * cap, 3 * lanes), bf16)]),
+            [VMEM] * 5,
+        )(act, over_tensor(act, 1), *weights)
+        return some, act
+
     mixed, cot_kept, want = call(
         prep_kernel,
         (sds((tokens, width), bf16), sds((tokens, width), bf16), sds((tokens, cap), bf16)),
-        [VMEM] + [anywhere] * 5,
+        [anywhere] + [hbm] * 5,
         [copy_of(x, pltpu.SMEM) for x in (counts, chosen, mix_weights)] + [copy_of(states), copy_of(cotangent), sem],
         nbytes=3 << 20,
-    )(send, counts, chosen, mix_weights, states, cotangent)
-    act = call(
-        functools.partial(act_kernel, ff, lanes, model_width), sds((half, 3 * lanes), bf16), [VMEM] * 2
-    )(own, over_tensor(send, 2))
-    *blocks, hidden, dgate, dup = call(
-        functools.partial(second_kernel, slots, cap, slot_rows, lanes),
-        tuple([block] * slots + [sds((total, ff), bf16)] * 3),
-        [VMEM] * 6,
-        [pltpu.VMEM((total, 3 * lanes), bf16), pltpu.VMEM((total, columns), bf16)],
-    )(unpack, act, over_tensor(act, 1), *weights)
+    )(load, counts, chosen, mix_weights, states, cotangent)
+    chunks = {"near": (0, 1, 2, 3), "mid": (4, 5), "far": (6, 7)}
+    sums = {name: summed(some) for name, some in chunks.items()}
+    outs, acts, taken = [], [], []
+    for name, some in chunks.items():
+        own, got, rows_of = sums[name]
+        blocks_of, act = acted(len(some), own, got)
+        outs += blocks_of
+        acts.append(act)
+        taken.append(rows_of)
 
     def moved(value, step):
         return over_dp(value, step).astype(f32)
 
     def total_of(k, *more):
-        return sum(more, blocks[k].astype(f32) + moved(blocks[k ^ 1], 1)).astype(bf16)
+        return sum(more, outs[k].astype(f32) + moved(outs[k ^ 1], 1)).astype(bf16)
 
     sum_4 = total_of(4, moved(total_of(6), 2))
-    back = [over_dp(blocks[1], 1), over_dp(total_of(2), 2), over_dp(sum_4, 4)]
-    dot_tn = functools.partial(lax.dot_general, dimension_numbers=(((0,), (0,)), ((), ())), preferred_element_type=f32)
-    grad_down = dot_tn(hidden, cot)
-    grad_gate = dot_tn(dgate, pg).T
-    grad_up = dot_tn(dup, pg).T
+    back = [over_dp(outs[1], 1), over_dp(total_of(2), 2), over_dp(sum_4, 4)]
+    hidden, dgate, dup, pg, cot = call(
+        functools.partial(join_kernel, lanes, len(chunks)),
+        tuple([sds((slots * cap, ff), bf16)] * 3 + [sds((slots * cap, width), bf16)] * 2),
+        [VMEM] * (2 * len(chunks)),
+    )(*acts, *taken)
+    tile = 256
+
+    def grads(lefts, rights):
+        out = sds((ff, width), f32)
+        count = len(lefts)
+        return pl.pallas_call(
+            functools.partial(grad_kernel, tile, count),
+            out_shape=(out,) * count,
+            in_specs=[VMEM] * (2 * count),
+            out_specs=(anywhere,) * count,
+            scratch_shapes=[pltpu.VMEM(out.shape, f32)] * count
+            + [pltpu.SemaphoreType.DMA((count * pl.cdiv(ff, tile),))],
+            compiler_params=pltpu.CompilerParams(vmem_limit_bytes=32 << 20),
+            cost_estimate=pl.CostEstimate(flops=0, bytes_accessed=count * ff * width * 4, transcendentals=0),
+        )(*lefts, *rights)
+
+    (grad_down,) = grads((hidden,), (cot,))
+    grad_gate, grad_up = (grad.T for grad in grads((dgate, dup), (pg, pg)))
     updated, grad_input = call(
         last_kernel, (sds((tokens, width), bf16), sds((tokens, width), bf16)), [VMEM] * 11
-    )(want, picked, load, mixed, cot_kept, router.reshape(1, width), norm_gain.reshape(1, width), blocks[0], *back)
+    )(want, picked, load, mixed, cot_kept, router.reshape(1, width), norm_gain.reshape(1, width), outs[0], *back)
     return updated, grad_input, grad_gate, grad_up, grad_down
 
 

time: 76.9 us -> 69.2 us (0.90)
  waiting for transfers between devices: 29.4 us -> 16.5 us
  Pallas kernels: 13.3 us -> 26 us
  matrix products: 8.62 us -> 0 us
  starting transfers between devices: 22.8 us -> 24.5 us
    pallas_call x5 -> x16, Pallas kernels: 8.11 us -> 20.8 us  [the longest x2 6.38 us: grads(): pl.pallas_call(functools.partial(grad_kernel, tile, count), out_shape=(ou...]
    dot_general x3 -> x0, matrix products: 8.62 us -> none  [the longest x1 2.88 us: fast(): grad_up = dot_tn(dup, pg).T]
    ppermute x14, waiting for transfers between devices: 19.1 us -> 11.4 us  [over_dp(): return lax.ppermute(x, 'dp', [(i, i ^ k) for i in range(slots)])]
    ppermute x3 -> x9, waiting for transfers between devices: 10.2 us -> 5.07 us  [over_tensor(): return lax.ppermute(x, 'tensor', [(i, i ^ k) for i in range(tensor)])]
    ppermute x3 -> x9, starting transfers between devices: 1.65 us -> 4.51 us  [over_tensor(): return lax.ppermute(x, 'tensor', [(i, i ^ k) for i in range(tensor)])]
    ppermute x14, starting transfers between devices: 21.2 us -> 20 us  [over_dp(): return lax.ppermute(x, 'dp', [(i, i ^ k) for i in range(slots)])]
    unnamed x20 -> x18, local copies, waits for them, and re-layouts: 1.61 us -> 0.95 us
  transfers between devices with their start and end apart: 17 -> 23, of which waited for: 9 -> 8; matrix products, arithmetic and copies ran while one was open for 11% -> 0% of each run, Pallas kernels for 6% -> 32%
where the time goes in v1:
time: 69.2 us; the launch traced here: 69 us
  Pallas kernels  26 us (38%)
  starting transfers between devices  24.5 us (35%)
  waiting for transfers between devices  16.5 us (24%)
  local copies, waits for them, and re-layouts  0.97 us (1%)
  between operations  0.95 us (1%)
    ppermute x14, starting transfers between devices, over_dp(): return lax.ppermute(x, 'dp', [(i, i ^ k) for i in range(slots)])  20 us
    ppermute x14, waiting for transfers between devices, over_dp(): return lax.ppermute(x, 'dp', [(i, i ^ k) for i in range(slots)])  11.4 us
    pallas_call x2, Pallas kernels, grads(): pl.pallas_call(functools.partial(grad_kernel, tile, count), out_shape=(ou...  6.38 us
    pallas_call x3, Pallas kernels, summed(): call(functools.partial(first_kernel, part, lanes), (sds((half, 3 * lanes)...  6.26 us
    ppermute x9, waiting for transfers between devices, over_tensor(): return lax.ppermute(x, 'tensor', [(i, i ^ k) for i in range(tensor)])  5.07 us
    ppermute x9, starting transfers between devices, over_tensor(): return lax.ppermute(x, 'tensor', [(i, i ^ k) for i in range(tensor)])  4.51 us
    pallas_call x3, Pallas kernels, acted(): call(functools.partial(second_kernel, part, lanes), tuple([block] * part...  3.51 us
    pallas_call x1, Pallas kernels, fast(): call(weights_kernel, (weight,) * 3, [anywhere] + [hbm] * 3, [sem], nbytes...  3.03 us
  transfers between devices with their start and end apart: 23, of which 8 were waited for; matrix products, arithmetic and copies ran while one was open for 0% of the time, Pallas kernels for 32%

profile of v1, /device:TPU:0, one launch (start us, length us, event | category | flops | bytes accessed | tf_op | source)
XLA Modules:
  0.0 69.0 jit_solution(11527264317749994768)
XLA Ops:
  0.6 2.5 %shard_map.137 = (f32[24,1280]{1,0:T(8,128)}, bf16[24,2688]{1,0:T(8,128)(2,1)}) custom-call(s32[1,8]{1,0:T(1,128)} %counts.3, s32[1,24]{1,0:T(1,128)} %chosen.3, f32[4]{0:T(128)} %mixw.3, bf16[4,128,1280]{2,1,0:T(8,128)(2,1)} %states.3, bf16[128,1280]{1,0:T(8,128)(2,1)} %cot.3, bf16[1280]{0:T(1024)(128)(2,1)} %router.1, bf16[1280]{0:T(1024)(128)(2,1)} %gain.1), custom_call_target="tpu_custom_call" | custom-call | tf_op jit(solution)/shard_map/pallas_call | solution.py:280
  3.1 4.1 %collective-permute-start.9 = (bf16[24,2688]{1,0:T(8,128)(2,1)}, bf16[24,2688]{1,0:T(8,128)(2,1)S(1)}, u32[]{:S(2)}, u32[]{:S(2)}) collective-permute-start(bf16[24,2688]{1,0:T(8,128)(2,1)} %get-tuple-element.48.after.refs_0_.load), channel_id=1, source_target_pairs={{0,16},{4,20},{8,24},{12,28},{16,0},{20,4},{24,8},{28,12},{1,17},{... | collective-permute-start | bytes 387080 | tf_op jit(solution)/shard_map/ppermute | solution.py:271
  7.3 1.6 %collective-permute-start.1 = (bf16[24,2688]{1,0:T(8,128)(2,1)}, bf16[24,2688]{1,0:T(8,128)(2,1)S(1)}, u32[]{:S(2)}, u32[]{:S(2)}) collective-permute-start(bf16[24,2688]{1,0:T(8,128)(2,1)} %get-tuple-element.48.after.refs_0_.load), channel_id=1, source_target_pairs={{0,8},{4,12},{8,0},{12,4},{16,24},{20,28},{24,16},{28,20},{1,9},{5... | collective-permute-start | bytes 387080 | tf_op jit(solution)/shard_map/ppermute | solution.py:271
  8.9 5.0 %collective-permute-done.9.refs_0_ = bf16[24,2688]{1,0:T(8,128)(2,1)S(1)} collective-permute-done((bf16[24,2688]{1,0:T(8,128)(2,1)}, bf16[24,2688]{1,0:T(8,128)(2,1)S(1)}, u32[]{:S(2)}, u32[]{:S(2)}) %collective-permute-start.9) | collective-permute-done | bytes 129056 | tf_op jit(solution)/shard_map/ppermute | solution.py:271
  13.8 0.7 %collective-permute-start.15 = (bf16[24,2688]{1,0:T(8,128)(2,1)S(1)}, bf16[24,2688]{1,0:T(8,128)(2,1)S(1)}, u32[]{:S(2)}, u32[]{:S(2)}) collective-permute-start(bf16[24,2688]{1,0:T(8,128)(2,1)S(1)} %collective-permute-done.9.refs_0_), channel_id=1, source_target_pairs={{0,8},{4,12},{8,0},{12,4},{16,24},{20,28},{24,16},{28,20},{1,9},{5... | collective-permute-start | bytes 387080 | tf_op jit(solution)/shard_map/ppermute | solution.py:271
  14.5 1.5 %collective-permute-start = (bf16[24,2688]{1,0:T(8,128)(2,1)}, bf16[24,2688]{1,0:T(8,128)(2,1)S(1)}, u32[]{:S(2)}, u32[]{:S(2)}) collective-permute-start(bf16[24,2688]{1,0:T(8,128)(2,1)} %get-tuple-element.48.after.refs_0_.load), channel_id=1, source_target_pairs={{0,4},{4,0},{8,12},{12,8},{16,20},{20,16},{24,28},{28,24},{1,5},{5... | collective-permute-start | bytes 387080 | tf_op jit(solution)/shard_map/ppermute | solution.py:271
  16.1 0.0 collective-permute-done.1.refs_2_
  16.1 0.5 collective-permute-start.2
  16.6 2.2 %collective-permute-done.15.refs_0_ = bf16[24,2688]{1,0:T(8,128)(2,1)S(1)} collective-permute-done((bf16[24,2688]{1,0:T(8,128)(2,1)S(1)}, bf16[24,2688]{1,0:T(8,128)(2,1)S(1)}, u32[]{:S(2)}, u32[]{:S(2)}) %collective-permute-start.15) | collective-permute-done | bytes 129056 | tf_op jit(solution)/shard_map/ppermute | solution.py:271
  18.8 1.6 %collective-permute-start.16 = (bf16[24,2688]{1,0:T(8,128)(2,1)S(1)}, bf16[24,2688]{1,0:T(8,128)(2,1)S(1)}, u32[]{:S(2)}, u32[]{:S(2)}) collective-permute-start(bf16[24,2688]{1,0:T(8,128)(2,1)S(1)} %collective-permute-done.15.refs_0_), channel_id=1, source_target_pairs={{0,4},{4,0},{8,12},{12,8},{16,20},{20,16},{24,28},{28,24},{1,5},{5... | collective-permute-start | bytes 387080 | tf_op jit(solution)/shard_map/ppermute | solution.py:271
  20.3 0.9 %copy-done.1 = bf16[24,2688]{1,0:T(8,128)(2,1)S(1)} copy-done((bf16[24,2688]{1,0:T(8,128)(2,1)S(1)}, bf16[24,2688]{1,0:T(8,128)(2,1)}, u32[]{:S(2)}) %copy-start.1) | copy-done | bytes 129048
  21.2 3.0 %shard_map.139 = (bf16[864,1280]{1,0:T(8,128)(2,1)S(1)}, bf16[864,1280]{1,0:T(8,128)(2,1)S(1)}, bf16[864,1280]{1,0:T(8,128)(2,1)S(1)}) custom-call(bf16[24,2688]{1,0:T(8,128)(2,1)S(1)} %copy-done.1, bf16[864,1280]{1,0:T(8,128)(2,1)} %bitcast.4, bf16[864,1280]{1,0:T(8,128)(2,1)} %bitcast.5, bf16[864,1280]{1,0:T(8,128)(2,1)} %refs_2_.1), custom_call_target="tpu_custom_call" | custom-call | bytes 13631488 | tf_op jit(solution)/shard_map/pallas_call | solution.py:294
  24.3 0.5 collective-permute-start.10
  24.8 0.0 collective-permute-done.refs_1_
  24.8 0.0 collective-permute-done.2.refs_3_
  24.8 2.4 %shard_map.140 = (f32[48,2688]{1,0:T(8,128)S(1)}, bf16[48,2688]{1,0:T(8,128)(2,1)S(1)}, bf16[96,2560]{1,0:T(8,128)(2,1)S(1)}) custom-call(bf16[24,2688]{1,0:T(8,128)(2,1)S(1)} %copy-done.1, bf16[24,2688]{1,0:T(8,128)(2,1)S(1)} %collective-permute-done.refs_1_, bf16[24,2688]{1,0:T(8,128)(2,1)S(1)} %collective-permute-done.1.refs_2_, ...), custom_call_target="tpu_custom_call" | custom-call | tf_op jit(solution)/shard_map/pallas_call | solution.py:302
  27.2 0.1 collective-permute-start.3
  27.2 0.0 collective-permute-done.16.refs_1_
  27.2 2.0 %shard_map.148 = (f32[24,2688]{1,0:T(8,128)S(1)}, bf16[24,2688]{1,0:T(8,128)(2,1)S(1)}, bf16[48,2560]{1,0:T(8,128)(2,1)S(1)}) custom-call(bf16[24,2688]{1,0:T(8,128)(2,1)S(1)} %collective-permute-done.15.refs_0_, bf16[24,2688]{1,0:T(8,128)(2,1)S(1)} %collective-permute-done.16.refs_1_, bf16[864,1280]{1,0:T(8,128)(2,1)S(1)} %get-tuple-element.53.refs_4_.gate_w.refs_2_, ...), custom_call_target="tpu_custom_call" | custom-call | tf_op jit(solution)/shard_map/pallas_call | solution.py:302
  29.2 0.6 collective-permute-start.17
  29.8 2.0 %shard_map.144 = (f32[24,2688]{1,0:T(8,128)S(1)}, bf16[24,2688]{1,0:T(8,128)(2,1)S(1)}, bf16[48,2560]{1,0:T(8,128)(2,1)S(1)}) custom-call(bf16[24,2688]{1,0:T(8,128)(2,1)S(1)} %collective-permute-done.9.refs_0_, bf16[24,2688]{1,0:T(8,128)(2,1)S(1)} %collective-permute-done.10.refs_1_, bf16[864,1280]{1,0:T(8,128)(2,1)S(1)} %get-tuple-element.53.refs_4_.gate_w.refs_2_, ...), custom_call_target="tpu_custom_call" | custom-call | tf_op jit(solution)/shard_map/pallas_call | solution.py:302
  31.7 0.1 collective-permute-start.11
  31.9 1.6 %collective-permute-start.18 = (bf16[24,2688]{1,0:T(8,128)(2,1)S(1)}, bf16[24,2688]{1,0:T(8,128)(2,1)S(1)}, u32[]{:S(2)}, u32[]{:S(2)}) collective-permute-start(bf16[24,2688]{1,0:T(8,128)(2,1)S(1)} %get-tuple-element.73), channel_id=1, source_target_pairs={{0,2},{1,3},{2,0},{3,1},{4,6},{5,7},{6,4},{7,5},{8,10},{9,11},{10,... | collective-permute-start | bytes 387080 | tf_op jit(solution)/shard_map/ppermute | solution.py:274
  33.5 0.0 collective-permute-done.11.got
  33.5 1.3 %collective-permute-start.12 = (bf16[24,2688]{1,0:T(8,128)(2,1)S(1)}, bf16[24,2688]{1,0:T(8,128)(2,1)S(1)}, u32[]{:S(2)}, u32[]{:S(2)}) collective-permute-start(bf16[24,2688]{1,0:T(8,128)(2,1)S(1)} %get-tuple-element.67), channel_id=1, source_target_pairs={{0,2},{1,3},{2,0},{3,1},{4,6},{5,7},{6,4},{7,5},{8,10},{9,11},{10,... | collective-permute-start | bytes 387080 | tf_op jit(solution)/shard_map/ppermute | solution.py:274
  34.8 0.0 collective-permute-done.3.got
  34.8 0.1 shard_map.141
  34.9 0.9 %collective-permute-start.4 = (bf16[48,2688]{1,0:T(8,128)(2,1)S(1)}, bf16[48,2688]{1,0:T(8,128)(2,1)S(1)}, u32[]{:S(2)}, u32[]{:S(2)}) collective-permute-start(bf16[48,2688]{1,0:T(8,128)(2,1)S(1)} %get-tuple-element.59), channel_id=1, source_target_pairs={{0,2},{1,3},{2,0},{3,1},{4,6},{5,7},{6,4},{7,5},{8,10},{9,11},{10,... | collective-permute-start | bytes 774152 | tf_op jit(solution)/shard_map/ppermute | solution.py:274
  35.8 2.5 %collective-permute-done.18.got = bf16[24,2688]{1,0:T(8,128)(2,1)S(1)} collective-permute-done((bf16[24,2688]{1,0:T(8,128)(2,1)S(1)}, bf16[24,2688]{1,0:T(8,128)(2,1)S(1)}, u32[]{:S(2)}, u32[]{:S(2)}) %collective-permute-start.18) | collective-permute-done | bytes 129056 | tf_op jit(solution)/shard_map/ppermute | solution.py:274
  38.3 0.4 shard_map.150.own
  38.7 2.3 %collective-permute-done.12.got = bf16[24,2688]{1,0:T(8,128)(2,1)S(1)} collective-permute-done((bf16[24,2688]{1,0:T(8,128)(2,1)S(1)}, bf16[24,2688]{1,0:T(8,128)(2,1)S(1)}, u32[]{:S(2)}, u32[]{:S(2)}) %collective-permute-start.12) | collective-permute-done | bytes 129056 | tf_op jit(solution)/shard_map/ppermute | solution.py:274
  41.0 0.4 shard_map.146.own
  41.4 0.0 collective-permute-start.13
  41.5 1.1 %shard_map.151 = (bf16[24,2688]{1,0:T(8,128)(2,1)S(1)}, bf16[24,2688]{1,0:T(8,128)(2,1)S(1)}, bf16[48,2688]{1,0:T(8,128)(2,1)S(1)}) custom-call(bf16[24,2688]{1,0:T(8,128)(2,1)S(1)} %shard_map.150.own, bf16[24,2688]{1,0:T(8,128)(2,1)S(1)} %collective-permute-done.19.got, bf16[864,1280]{1,0:T(8,128)(2,1)S(1)} %get-tuple-element.53.refs_4_.gate_w.refs_2_, ...), custom_call_target="tpu_custom_call" | custom-call | tf_op jit(solution)/shard_map/pallas_call | solution.py:315
  42.6 1.6 %collective-permute-start.20 = (bf16[24,2688]{1,0:T(8,128)(2,1)S(1)}, bf16[24,2688]{1,0:T(8,128)(2,1)S(1)}, u32[]{:S(2)}, u32[]{:S(2)}) collective-permute-start(bf16[24,2688]{1,0:T(8,128)(2,1)S(1)} %get-tuple-element.75), channel_id=1, source_target_pairs={{0,4},{4,0},{8,12},{12,8},{16,20},{20,16},{24,28},{28,24},{1,5},{5... | collective-permute-start | bytes 387080 | tf_op jit(solution)/shard_map/ppermute | solution.py:271
  44.2 0.0 collective-permute-done.13.got
  44.2 1.1 %shard_map.147 = (bf16[24,2688]{1,0:T(8,128)(2,1)S(1)}, bf16[24,2688]{1,0:T(8,128)(2,1)S(1)}, bf16[48,2688]{1,0:T(8,128)(2,1)S(1)}) custom-call(bf16[24,2688]{1,0:T(8,128)(2,1)S(1)} %shard_map.146.own, bf16[24,2688]{1,0:T(8,128)(2,1)S(1)} %collective-permute-done.13.got, bf16[864,1280]{1,0:T(8,128)(2,1)S(1)} %get-tuple-element.53.refs_4_.gate_w.refs_2_, ...), custom_call_target="tpu_custom_call" | custom-call | tf_op jit(solution)/shard_map/pallas_call | solution.py:315
  45.3 0.5 collective-permute-start.14
  45.9 0.2 collective-permute-done.4.got
  46.1 0.5 shard_map.142.own
  46.6 0.0 collective-permute-start.5
  46.6 2.2 %collective-permute-done.20 = bf16[24,2688]{1,0:T(8,128)(2,1)S(1)} collective-permute-done((bf16[24,2688]{1,0:T(8,128)(2,1)S(1)}, bf16[24,2688]{1,0:T(8,128)(2,1)S(1)}, u32[]{:S(2)}, u32[]{:S(2)}) %collective-permute-start.20) | collective-permute-done | bytes 129056 | tf_op jit(solution)/shard_map/ppermute | solution.py:271
  48.8 0.0 copy-start
  48.8 0.0 copy-start.2
  48.9 0.0 copy-start.4
  48.9 0.0 copy-start.5
  48.9 0.0 copy-start.6
  48.9 1.3 %collective-permute-start.21 = (bf16[24,2688]{1,0:T(8,128)(2,1)S(1)}, bf16[24,2688]{1,0:T(8,128)(2,1)S(1)}, u32[]{:S(2)}, u32[]{:S(2)}) collective-permute-start(bf16[24,2688]{1,0:T(8,128)(2,1)S(1)} %add_convert_fusion.1), channel_id=1, source_target_pairs={{0,8},{4,12},{8,0},{12,4},{16,24},{20,28},{24,16},{28,20},{1,9},{5... | collective-permute-start | bytes 387080 | tf_op jit(solution)/shard_map/ppermute | solution.py:271
  50.2 1.3 %shard_map.143 = (bf16[24,2688]{1,0:T(8,128)(2,1)S(1)}, bf16[24,2688]{1,0:T(8,128)(2,1)S(1)}, bf16[24,2688]{1,0:T(8,128)(2,1)S(1)}, bf16[24,2688]{1,0:T(8,128)(2,1)S(1)}, bf16[96,2688]{1,0:T(8,128)(2,1)S(1)}) custom-call(bf16[48,2688]{1,0:T(8,128)(2,1)S(1)} %shard_map.142.own, bf16[48,2688]{1,0:T(8,128)(2,1)S(1)} %collective-permute-done.5.got, ...), custom_call_target="tpu_custom_call" | custom-call | tf_op jit(solution)/shard_map/pallas_call | solution.py:315
  51.5 0.0 copy-start.7
  51.5 0.0 copy-start.8
  51.5 1.7 %collective-permute-start.6 = (bf16[24,2688]{1,0:T(8,128)(2,1)S(1)}, bf16[24,2688]{1,0:T(8,128)(2,1)S(1)}, u32[]{:S(2)}, u32[]{:S(2)}) collective-permute-start(bf16[24,2688]{1,0:T(8,128)(2,1)S(1)} %get-tuple-element.61), channel_id=1, source_target_pairs={{0,4},{4,0},{8,12},{12,8},{16,20},{20,16},{24,28},{28,24},{1,5},{5... | collective-permute-start | bytes 387080 | tf_op jit(solution)/shard_map/ppermute | solution.py:271
  53.2 0.4 collective-permute-start.7
  53.6 0.3 collective-permute-done.21
  53.9 0.1 add_convert_fusion
  54.0 3.0 %collective-permute-start.22 = (bf16[24,2688]{1,0:T(8,128)(2,1)S(1)}, bf16[24,2688]{1,0:T(8,128)(2,1)S(1)}, u32[]{:S(2)}, u32[]{:S(2)}) collective-permute-start(bf16[24,2688]{1,0:T(8,128)(2,1)S(1)} %add_convert_fusion), channel_id=1, source_target_pairs={{0,16},{4,20},{8,24},{12,28},{16,0},{20,4},{24,8},{28,12},{1,17},{... | collective-permute-start | bytes 387080 | tf_op jit(solution)/shard_map/ppermute | solution.py:271
  57.0 1.7 %collective-permute-done.7 = bf16[24,2688]{1,0:T(8,128)(2,1)S(1)} collective-permute-done((bf16[24,2688]{1,0:T(8,128)(2,1)S(1)}, bf16[24,2688]{1,0:T(8,128)(2,1)S(1)}, u32[]{:S(2)}, u32[]{:S(2)}) %collective-permute-start.7) | collective-permute-done | bytes 129056 | tf_op jit(solution)/shard_map/ppermute | solution.py:271
  58.7 0.9 %collective-permute-start.8 = (bf16[24,2688]{1,0:T(8,128)(2,1)S(1)}, bf16[24,2688]{1,0:T(8,128)(2,1)S(1)}, u32[]{:S(2)}, u32[]{:S(2)}) collective-permute-start(bf16[24,2688]{1,0:T(8,128)(2,1)S(1)} %add_convert_fusion.2), channel_id=1, source_target_pairs={{0,8},{4,12},{8,0},{12,4},{16,24},{20,28},{24,16},{28,20},{1,9},{5... | collective-permute-start | bytes 387080 | tf_op jit(solution)/shard_map/ppermute | solution.py:271
  59.7 1.6 %shard_map.138 = (bf16[128,1280]{1,0:T(8,128)(2,1)S(1)}, bf16[128,1280]{1,0:T(8,128)(2,1)S(1)}, bf16[128,24]{1,0:T(8,128)(2,1)S(1)}) custom-call(bf16[24,2688]{1,0:T(8,128)(2,1)S(1)} %copy-done.1, s32[1,8]{1,0:T(1,128)S(1)} %copy-done.4, s32[1,24]{1,0:T(1,128)S(1)} %copy-done.5, f32[4]{0:T(128)S(1)} %copy-done.6, bf16[4,128,1280]{2,1,0:T(8,128)(2,1)S(1)} %copy-done, ...), custom_call_target="tpu_custom_call" | custom-call | bytes 3145728 | tf_op jit(solution)/shard_map/pallas_call | solution.py:322
  61.3 0.1 shard_map.153
  61.5 0.0 copy-start.3
  61.5 2.5 %shard_map.155 = f32[864,1280]{1,0:T(8,128)} custom-call(bf16[192,864]{1,0:T(8,128)(2,1)S(1)} %get-tuple-element.89.refs_0_, bf16[192,1280]{1,0:T(8,128)(2,1)S(1)} %get-tuple-element.90.refs_1_), custom_call_target="tpu_custom_call" | custom-call | bytes 4423680 | tf_op jit(solution)/shard_map/pallas_call | solution.py:357
  64.0 3.9 %shard_map.154 = (f32[864,1280]{1,0:T(8,128)}, f32[864,1280]{1,0:T(8,128)}) custom-call(bf16[192,864]{1,0:T(8,128)(2,1)S(1)} %get-tuple-element.84.refs_0_, bf16[192,864]{1,0:T(8,128)(2,1)S(1)} %get-tuple-element.85.refs_1_, bf16[192,1280]{1,0:T(8,128)(2,1)S(1)} %get-tuple-element.86.refs_2_.refs_3_, bf16[192,1280]{1,0:T(8,128)(2,1)S(1)} %get-tuple-element.86.refs_2_.refs_3_), custom_call_target="tpu_custom_call" | custom-call | bytes 8847360 | tf_op jit(solution)/shard_map/pallas_call | solution.py:357
  67.9 1.1 %shard_map.152 = (bf16[128,1280]{1,0:T(8,128)(2,1)}, bf16[128,1280]{1,0:T(8,128)(2,1)}) custom-call(bf16[128,24]{1,0:T(8,128)(2,1)S(1)} %get-tuple-element.49.want, f32[24,1280]{1,0:T(8,128)S(1)} %copy-done.3, bf16[24,2688]{1,0:T(8,128)(2,1)S(1)} %copy-done.1, bf16[128,1280]{1,0:T(8,128)(2,1)S(1)} %get-tuple-element.51.mixed, ...), custom_call_target="tpu_custom_call" | custom-call | tf_op jit(solution)/shard_map/pallas_call | solution.py:370
  (24 shorter events, 0.2 us)
Async XLA Ops:
  3.1 10.7 %collective-permute-start.9 = (bf16[24,2688]{1,0:T(8,128)(2,1)}, bf16[24,2688]{1,0:T(8,128)(2,1)S(1)}, u32[]{:S(2)}, u32[]{:S(2)}) collective-permute-start(bf16[24,2688]{1,0:T(8,128)(2,1)} %get-tuple-element.48.after.refs_0_.load), channel_id=1, source_target_pairs={{0,16},{4,20},{8,24},{12,28},{16,0},{20,4},{24,8},{28,12},{1,17},{... | collective-permute-start | bytes 387080 | tf_op jit(solution)/shard_map/ppermute | solution.py:271
  7.3 8.8 %collective-permute-start.1 = (bf16[24,2688]{1,0:T(8,128)(2,1)}, bf16[24,2688]{1,0:T(8,128)(2,1)S(1)}, u32[]{:S(2)}, u32[]{:S(2)}) collective-permute-start(bf16[24,2688]{1,0:T(8,128)(2,1)} %get-tuple-element.48.after.refs_0_.load), channel_id=1, source_target_pairs={{0,8},{4,12},{8,0},{12,4},{16,24},{20,28},{24,16},{28,20},{1,9},{5... | collective-permute-start | bytes 387080 | tf_op jit(solution)/shard_map/ppermute | solution.py:271
  13.8 4.9 %collective-permute-start.15 = (bf16[24,2688]{1,0:T(8,128)(2,1)S(1)}, bf16[24,2688]{1,0:T(8,128)(2,1)S(1)}, u32[]{:S(2)}, u32[]{:S(2)}) collective-permute-start(bf16[24,2688]{1,0:T(8,128)(2,1)S(1)} %collective-permute-done.9.refs_0_), channel_id=1, source_target_pairs={{0,8},{4,12},{8,0},{12,4},{16,24},{20,28},{24,16},{28,20},{1,9},{5... | collective-permute-start | bytes 387080 | tf_op jit(solution)/shard_map/ppermute | solution.py:271
  14.5 10.3 %collective-permute-start = (bf16[24,2688]{1,0:T(8,128)(2,1)}, bf16[24,2688]{1,0:T(8,128)(2,1)S(1)}, u32[]{:S(2)}, u32[]{:S(2)}) collective-permute-start(bf16[24,2688]{1,0:T(8,128)(2,1)} %get-tuple-element.48.after.refs_0_.load), channel_id=1, source_target_pairs={{0,4},{4,0},{8,12},{12,8},{16,20},{20,16},{24,28},{28,24},{1,5},{5... | collective-permute-start | bytes 387080 | tf_op jit(solution)/shard_map/ppermute | solution.py:271
  16.1 8.7 %collective-permute-start.2 = (bf16[24,2688]{1,0:T(8,128)(2,1)S(1)}, bf16[24,2688]{1,0:T(8,128)(2,1)S(1)}, u32[]{:S(2)}, u32[]{:S(2)}) collective-permute-start(bf16[24,2688]{1,0:T(8,128)(2,1)S(1)} %collective-permute-done.1.refs_2_), channel_id=1, source_target_pairs={{0,4},{4,0},{8,12},{12,8},{16,20},{20,16},{24,28},{28,24},{1,5},{5... | collective-permute-start | bytes 387080 | tf_op jit(solution)/shard_map/ppermute | solution.py:271
  18.8 8.5 %collective-permute-start.16 = (bf16[24,2688]{1,0:T(8,128)(2,1)S(1)}, bf16[24,2688]{1,0:T(8,128)(2,1)S(1)}, u32[]{:S(2)}, u32[]{:S(2)}) collective-permute-start(bf16[24,2688]{1,0:T(8,128)(2,1)S(1)} %collective-permute-done.15.refs_0_), channel_id=1, source_target_pairs={{0,4},{4,0},{8,12},{12,8},{16,20},{20,16},{24,28},{28,24},{1,5},{5... | collective-permute-start | bytes 387080 | tf_op jit(solution)/shard_map/ppermute | solution.py:271
  20.3 0.9 %copy-start.1 = (bf16[24,2688]{1,0:T(8,128)(2,1)S(1)}, bf16[24,2688]{1,0:T(8,128)(2,1)}, u32[]{:S(2)}) copy-start(bf16[24,2688]{1,0:T(8,128)(2,1)} %get-tuple-element.48.after.refs_0_.load) | copy-start | bytes 387076
  24.3 5.5 %collective-permute-start.10 = (bf16[24,2688]{1,0:T(8,128)(2,1)S(1)}, bf16[24,2688]{1,0:T(8,128)(2,1)S(1)}, u32[]{:S(2)}, u32[]{:S(2)}) collective-permute-start(bf16[24,2688]{1,0:T(8,128)(2,1)S(1)} %collective-permute-done.9.refs_0_), channel_id=1, source_target_pairs={{0,4},{4,0},{8,12},{12,8},{16,20},{20,16},{24,28},{28,24},{1,5},{5... | collective-permute-start | bytes 387080 | tf_op jit(solution)/shard_map/ppermute | solution.py:271
  27.2 7.6 %collective-permute-start.3 = (bf16[48,2688]{1,0:T(8,128)(2,1)S(1)}, bf16[48,2688]{1,0:T(8,128)(2,1)S(1)}, u32[]{:S(2)}, u32[]{:S(2)}) collective-permute-start(bf16[48,2688]{1,0:T(8,128)(2,1)S(1)} %get-tuple-element.57), channel_id=1, source_target_pairs={{0,1},{1,0},{2,3},{3,2},{4,5},{5,4},{6,7},{7,6},{8,9},{9,8},{10,11... | collective-permute-start | bytes 774152 | tf_op jit(solution)/shard_map/ppermute | solution.py:274
  29.2 2.6 %collective-permute-start.17 = (bf16[24,2688]{1,0:T(8,128)(2,1)S(1)}, bf16[24,2688]{1,0:T(8,128)(2,1)S(1)}, u32[]{:S(2)}, u32[]{:S(2)}) collective-permute-start(bf16[24,2688]{1,0:T(8,128)(2,1)S(1)} %get-tuple-element.71), channel_id=1, source_target_pairs={{0,1},{1,0},{2,3},{3,2},{4,5},{5,4},{6,7},{7,6},{8,9},{9,8},{10,11... | collective-permute-start | bytes 387080 | tf_op jit(solution)/shard_map/ppermute | solution.py:274
  31.7 1.7 %collective-permute-start.11 = (bf16[24,2688]{1,0:T(8,128)(2,1)S(1)}, bf16[24,2688]{1,0:T(8,128)(2,1)S(1)}, u32[]{:S(2)}, u32[]{:S(2)}) collective-permute-start(bf16[24,2688]{1,0:T(8,128)(2,1)S(1)} %get-tuple-element.65), channel_id=1, source_target_pairs={{0,1},{1,0},{2,3},{3,2},{4,5},{5,4},{6,7},{7,6},{8,9},{9,8},{10,11... | collective-permute-start | bytes 387080 | tf_op jit(solution)/shard_map/ppermute | solution.py:274
  31.9 6.4 %collective-permute-start.18 = (bf16[24,2688]{1,0:T(8,128)(2,1)S(1)}, bf16[24,2688]{1,0:T(8,128)(2,1)S(1)}, u32[]{:S(2)}, u32[]{:S(2)}) collective-permute-start(bf16[24,2688]{1,0:T(8,128)(2,1)S(1)} %get-tuple-element.73), channel_id=1, source_target_pairs={{0,2},{1,3},{2,0},{3,1},{4,6},{5,7},{6,4},{7,5},{8,10},{9,11},{10,... | collective-permute-start | bytes 387080 | tf_op jit(solution)/shard_map/ppermute | solution.py:274
  33.5 7.5 %collective-permute-start.12 = (bf16[24,2688]{1,0:T(8,128)(2,1)S(1)}, bf16[24,2688]{1,0:T(8,128)(2,1)S(1)}, u32[]{:S(2)}, u32[]{:S(2)}) collective-permute-start(bf16[24,2688]{1,0:T(8,128)(2,1)S(1)} %get-tuple-element.67), channel_id=1, source_target_pairs={{0,2},{1,3},{2,0},{3,1},{4,6},{5,7},{6,4},{7,5},{8,10},{9,11},{10,... | collective-permute-start | bytes 387080 | tf_op jit(solution)/shard_map/ppermute | solution.py:274
  34.9 11.2 %collective-permute-start.4 = (bf16[48,2688]{1,0:T(8,128)(2,1)S(1)}, bf16[48,2688]{1,0:T(8,128)(2,1)S(1)}, u32[]{:S(2)}, u32[]{:S(2)}) collective-permute-start(bf16[48,2688]{1,0:T(8,128)(2,1)S(1)} %get-tuple-element.59), channel_id=1, source_target_pairs={{0,2},{1,3},{2,0},{3,1},{4,6},{5,7},{6,4},{7,5},{8,10},{9,11},{10,... | collective-permute-start | bytes 774152 | tf_op jit(solution)/shard_map/ppermute | solution.py:274
  38.7 2.8 %collective-permute-start.19 = (bf16[24,2688]{1,0:T(8,128)(2,1)S(1)}, bf16[24,2688]{1,0:T(8,128)(2,1)S(1)}, u32[]{:S(2)}, u32[]{:S(2)}) collective-permute-start(bf16[24,2688]{1,0:T(8,128)(2,1)S(1)} %shard_map.150.own), channel_id=1, source_target_pairs={{0,1},{1,0},{2,3},{3,2},{4,5},{5,4},{6,7},{7,6},{8,9},{9,8},{10,11... | collective-permute-start | bytes 387080 | tf_op jit(solution)/shard_map/ppermute | solution.py:274
  41.4 2.8 %collective-permute-start.13 = (bf16[24,2688]{1,0:T(8,128)(2,1)S(1)}, bf16[24,2688]{1,0:T(8,128)(2,1)S(1)}, u32[]{:S(2)}, u32[]{:S(2)}) collective-permute-start(bf16[24,2688]{1,0:T(8,128)(2,1)S(1)} %shard_map.146.own), channel_id=1, source_target_pairs={{0,1},{1,0},{2,3},{3,2},{4,5},{5,4},{6,7},{7,6},{8,9},{9,8},{10,11... | collective-permute-start | bytes 387080 | tf_op jit(solution)/shard_map/ppermute | solution.py:274
  42.6 6.2 %collective-permute-start.20 = (bf16[24,2688]{1,0:T(8,128)(2,1)S(1)}, bf16[24,2688]{1,0:T(8,128)(2,1)S(1)}, u32[]{:S(2)}, u32[]{:S(2)}) collective-permute-start(bf16[24,2688]{1,0:T(8,128)(2,1)S(1)} %get-tuple-element.75), channel_id=1, source_target_pairs={{0,4},{4,0},{8,12},{12,8},{16,20},{20,16},{24,28},{28,24},{1,5},{5... | collective-permute-start | bytes 387080 | tf_op jit(solution)/shard_map/ppermute | solution.py:271
  45.3 8.2 %collective-permute-start.14 = (bf16[24,2688]{1,0:T(8,128)(2,1)S(1)}, bf16[24,2688]{1,0:T(8,128)(2,1)S(1)}, u32[]{:S(2)}, u32[]{:S(2)}) collective-permute-start(bf16[24,2688]{1,0:T(8,128)(2,1)S(1)} %get-tuple-element.69), channel_id=1, source_target_pairs={{0,4},{4,0},{8,12},{12,8},{16,20},{20,16},{24,28},{28,24},{1,5},{5... | collective-permute-start | bytes 387080 | tf_op jit(solution)/shard_map/ppermute | solution.py:271
  46.6 3.6 %collective-permute-start.5 = (bf16[48,2688]{1,0:T(8,128)(2,1)S(1)}, bf16[48,2688]{1,0:T(8,128)(2,1)S(1)}, u32[]{:S(2)}, u32[]{:S(2)}) collective-permute-start(bf16[48,2688]{1,0:T(8,128)(2,1)S(1)} %shard_map.142.own), channel_id=1, source_target_pairs={{0,1},{1,0},{2,3},{3,2},{4,5},{5,4},{6,7},{7,6},{8,9},{9,8},{10,11... | collective-permute-start | bytes 774152 | tf_op jit(solution)/shard_map/ppermute | solution.py:274
  48.8 10.8 %copy-start = (bf16[4,128,1280]{2,1,0:T(8,128)(2,1)S(1)}, bf16[4,128,1280]{2,1,0:T(8,128)(2,1)}, u32[]{:S(2)}) copy-start(bf16[4,128,1280]{2,1,0:T(8,128)(2,1)} %states.3) | copy-start | bytes 3932164
  48.8 10.8 %copy-start.2 = (bf16[128,1280]{1,0:T(8,128)(2,1)S(1)}, bf16[128,1280]{1,0:T(8,128)(2,1)}, u32[]{:S(2)}) copy-start(bf16[128,1280]{1,0:T(8,128)(2,1)} %cot.3) | copy-start | bytes 983044
  48.9 10.8 %copy-start.4 = (s32[1,8]{1,0:T(1,128)S(1)}, s32[1,8]{1,0:T(1,128)}, u32[]{:S(2)}) copy-start(s32[1,8]{1,0:T(1,128)} %counts.3) | copy-start | bytes 100
  48.9 10.8 %copy-start.5 = (s32[1,24]{1,0:T(1,128)S(1)}, s32[1,24]{1,0:T(1,128)}, u32[]{:S(2)}) copy-start(s32[1,24]{1,0:T(1,128)} %chosen.3) | copy-start | bytes 292
  48.9 10.8 %copy-start.6 = (f32[4]{0:T(128)S(1)}, f32[4]{0:T(128)}, u32[]{:S(2)}) copy-start(f32[4]{0:T(128)} %mixw.3) | copy-start | bytes 52
  48.9 5.0 %collective-permute-start.21 = (bf16[24,2688]{1,0:T(8,128)(2,1)S(1)}, bf16[24,2688]{1,0:T(8,128)(2,1)S(1)}, u32[]{:S(2)}, u32[]{:S(2)}) collective-permute-start(bf16[24,2688]{1,0:T(8,128)(2,1)S(1)} %add_convert_fusion.1), channel_id=1, source_target_pairs={{0,8},{4,12},{8,0},{12,4},{16,24},{20,28},{24,16},{28,20},{1,9},{5... | collective-permute-start | bytes 387080 | tf_op jit(solution)/shard_map/ppermute | solution.py:271
  51.5 9.8 %copy-start.7 = (bf16[1280]{0:T(1024)(128)(2,1)S(1)}, bf16[1280]{0:T(1024)(128)(2,1)}, u32[]{:S(2)}) copy-start(bf16[1280]{0:T(1024)(128)(2,1)} %router.1) | copy-start | bytes 7684
  51.5 9.8 %copy-start.8 = (bf16[1280]{0:T(1024)(128)(2,1)S(1)}, bf16[1280]{0:T(1024)(128)(2,1)}, u32[]{:S(2)}) copy-start(bf16[1280]{0:T(1024)(128)(2,1)} %gain.1) | copy-start | bytes 7684
  51.5 16.4 %collective-permute-start.6 = (bf16[24,2688]{1,0:T(8,128)(2,1)S(1)}, bf16[24,2688]{1,0:T(8,128)(2,1)S(1)}, u32[]{:S(2)}, u32[]{:S(2)}) collective-permute-start(bf16[24,2688]{1,0:T(8,128)(2,1)S(1)} %get-tuple-element.61), channel_id=1, source_target_pairs={{0,4},{4,0},{8,12},{12,8},{16,20},{20,16},{24,28},{28,24},{1,5},{5... | collective-permute-start | bytes 387080 | tf_op jit(solution)/shard_map/ppermute | solution.py:271
  53.2 5.5 %collective-permute-start.7 = (bf16[24,2688]{1,0:T(8,128)(2,1)S(1)}, bf16[24,2688]{1,0:T(8,128)(2,1)S(1)}, u32[]{:S(2)}, u32[]{:S(2)}) collective-permute-start(bf16[24,2688]{1,0:T(8,128)(2,1)S(1)} %get-tuple-element.63), channel_id=1, source_target_pairs={{0,4},{4,0},{8,12},{12,8},{16,20},{20,16},{24,28},{28,24},{1,5},{5... | collective-permute-start | bytes 387080 | tf_op jit(solution)/shard_map/ppermute | solution.py:271
  54.0 13.9 %collective-permute-start.22 = (bf16[24,2688]{1,0:T(8,128)(2,1)S(1)}, bf16[24,2688]{1,0:T(8,128)(2,1)S(1)}, u32[]{:S(2)}, u32[]{:S(2)}) collective-permute-start(bf16[24,2688]{1,0:T(8,128)(2,1)S(1)} %add_convert_fusion), channel_id=1, source_target_pairs={{0,16},{4,20},{8,24},{12,28},{16,0},{20,4},{24,8},{28,12},{1,17},{... | collective-permute-start | bytes 387080 | tf_op jit(solution)/shard_map/ppermute | solution.py:271
  58.7 9.2 %collective-permute-start.8 = (bf16[24,2688]{1,0:T(8,128)(2,1)S(1)}, bf16[24,2688]{1,0:T(8,128)(2,1)S(1)}, u32[]{:S(2)}, u32[]{:S(2)}) collective-permute-start(bf16[24,2688]{1,0:T(8,128)(2,1)S(1)} %add_convert_fusion.2), channel_id=1, source_target_pairs={{0,8},{4,12},{8,0},{12,4},{16,24},{20,28},{24,16},{28,20},{1,9},{5... | collective-permute-start | bytes 387080 | tf_op jit(solution)/shard_map/ppermute | solution.py:271
  61.5 6.4 %copy-start.3 = (f32[24,1280]{1,0:T(8,128)S(1)}, f32[24,1280]{1,0:T(8,128)}, u32[]{:S(2)}) copy-start(f32[24,1280]{1,0:T(8,128)} %get-tuple-element.50.picked) | copy-start | bytes 368644

commit v2 on v1

--- a/solution.py
+++ b/solution.py
@@ -88,20 +88,19 @@
     load_ref[:, 2 * width :] = in_lanes(terms(logit) + terms(square), 128, first).astype(bf16)
 
 
-def weights_kernel(after, *refs):
+def weights_kernel(*refs):
     *pairs, sem = refs
     half = len(pairs) // 2
     for copy in fetch(list(zip(pairs[:half], pairs[half:])), sem):
         copy.wait()
 
 
-def prep_kernel(after, counts, chosen, mixw, states, cot, *refs):
+def prep_kernel(counts, chosen, mixw, states, cot, *refs):
     mixed_ref, cot_ref, want_ref, *places, sem = refs
     for copy in fetch(list(zip((counts, chosen, mixw, states, cot), places)), sem):
         copy.wait()
     counts, chosen, mixw, states, cot = places
-    me = lax.axis_index("dp")
-    mine = counts[0, me]
+    mine = counts[0, lax.axis_index("dp")]
     tokens, cap = want_ref.shape
     row = lax.broadcasted_iota(jnp.int32, (tokens, cap), 0)
     col = lax.broadcasted_iota(jnp.int32, (tokens, cap), 1)
@@ -233,7 +232,7 @@
         copy.wait()
 
 
-def last_kernel(want, picked, load, mixed, cot, router, gain, *refs):
+def last_kernel(want, picked, taken, mixed, cot, router, gain, *refs):
     *blocks, updated_ref, grad_ref = refs
     _, width = cot.shape
     sums = blocks[0][...].astype(f32)
@@ -245,7 +244,7 @@
     inner = jnp.sum(jnp.where(kind < PARTS, 0.0, scalars), axis=1, keepdims=True)
     new_rows = (picked[...] + sums[:, :width]).astype(bf16)
     drows = (
-        load[:, width : 2 * width].astype(f32)
+        taken[: picked.shape[0], width:].astype(f32)
         + sums[:, width : 2 * width] * gain[...].astype(f32)
         - picked[...] * inner
         + dlogit * router[...].astype(f32)
@@ -292,8 +291,15 @@
             blocks[k ^ step] = over_dp(blocks[k], step)
     weight = sds((ff, width), bf16)
     weights = call(
-        weights_kernel, (weight,) * 3, [anywhere] + [hbm] * 3, [sem], nbytes=13 << 20, vmem=48_000_000,
-    )(load, gate_weight.T, up_weight.T, down_weight)
+        weights_kernel, (weight,) * 3, [hbm] * 3, [sem], nbytes=13 << 20, vmem=48_000_000,
+    )(gate_weight.T, up_weight.T, down_weight)
+    mixed, cot_kept, want = call(
+        prep_kernel,
+        (sds((tokens, width), bf16), sds((tokens, width), bf16), sds((tokens, cap), bf16)),
+        [hbm] * 5,
+        [copy_of(x, pltpu.SMEM) for x in (counts, chosen, mix_weights)] + [copy_of(states), copy_of(cotangent), sem],
+        nbytes=3 << 20,
+    )(counts, chosen, mix_weights, states, cotangent)
 
     def summed(chosen_slots):
         part = len(chosen_slots)
@@ -311,7 +317,9 @@
         return own, over_tensor(send, 2), taken
 
     def acted(part, own, got):
-        act = call(functools.partial(act_kernel, ff, lanes, model_width), sds(got.shape, bf16), [VMEM] * 2)(own, got)
+        act = call(
+            functools.partial(act_kernel, ff, lanes, model_width), sds(got.shape, bf16), [VMEM] * 2
+        )(own, got)
         *some, act = call(
             functools.partial(second_kernel, part, lanes),
             tuple([block] * part + [sds((part * cap, 3 * lanes), bf16)]),
@@ -319,14 +327,7 @@
         )(act, over_tensor(act, 1), *weights)
         return some, act
 
-    mixed, cot_kept, want = call(
-        prep_kernel,
-        (sds((tokens, width), bf16), sds((tokens, width), bf16), sds((tokens, cap), bf16)),
-        [anywhere] + [hbm] * 5,
-        [copy_of(x, pltpu.SMEM) for x in (counts, chosen, mix_weights)] + [copy_of(states), copy_of(cotangent), sem],
-        nbytes=3 << 20,
-    )(load, counts, chosen, mix_weights, states, cotangent)
-    chunks = {"near": (0, 1, 2, 3), "mid": (4, 5), "far": (6, 7)}
+    chunks = {"n": (0, 1, 2, 3), "m": (4, 5), "f": (6, 7)}
     sums = {name: summed(some) for name, some in chunks.items()}
     outs, acts, taken = [], [], []
     for name, some in chunks.items():
@@ -369,7 +370,7 @@
     grad_gate, grad_up = (grad.T for grad in grads((dgate, dup), (pg, pg)))
     updated, grad_input = call(
         last_kernel, (sds((tokens, width), bf16), sds((tokens, width), bf16)), [VMEM] * 11
-    )(want, picked, load, mixed, cot_kept, router.reshape(1, width), norm_gain.reshape(1, width), outs[0], *back)
+    )(want, picked, taken[0], mixed, cot_kept, router.reshape(1, width), norm_gain.reshape(1, width), outs[0], *back)
     return updated, grad_input, grad_gate, grad_up, grad_down
 
 

time: 69.2 us -> 68.5 us (0.990)
  local copies, waits for them, and re-layouts: 0.97 us -> 0.07 us
    unnamed x18, local copies, waits for them, and re-layouts: 0.95 us -> 0.05 us
  transfers between devices with their start and end apart: 23 -> 23, of which waited for: 8 -> 8; matrix products, arithmetic and copies ran while one was open for 0% -> 0% of each run, Pallas kernels for 32% -> 33%
where the time goes in v2:
time: 68.5 us; the launch traced here: 68.3 us
  Pallas kernels  26 us (38%)
  starting transfers between devices  24.3 us (35%)
  waiting for transfers between devices  16.9 us (25%)
  between operations  0.95 us (1%)
    ppermute x14, starting transfers between devices, over_dp(): return lax.ppermute(x, 'dp', [(i, i ^ k) for i in range(slots)])  19.9 us
    ppermute x14, waiting for transfers between devices, over_dp(): return lax.ppermute(x, 'dp', [(i, i ^ k) for i in range(slots)])  11.9 us
    pallas_call x2, Pallas kernels, grads(): pl.pallas_call(functools.partial(grad_kernel, tile, count), out_shape=(ou...  6.38 us
    pallas_call x3, Pallas kernels, summed(): call(functools.partial(first_kernel, part, lanes), (sds((half, 3 * lanes)...  6.29 us
    ppermute x9, waiting for transfers between devices, over_tensor(): return lax.ppermute(x, 'tensor', [(i, i ^ k) for i in range(tensor)])  4.95 us
    ppermute x9, starting transfers between devices, over_tensor(): return lax.ppermute(x, 'tensor', [(i, i ^ k) for i in range(tensor)])  4.44 us
    pallas_call x3, Pallas kernels, acted(): call(functools.partial(second_kernel, part, lanes), tuple([block] * part...  3.52 us
    pallas_call x1, Pallas kernels, fast(): call(weights_kernel, (weight,) * 3, [hbm] * 3, [sem], nbytes=13 << 20, vm...  3.06 us
  transfers between devices with their start and end apart: 23, of which 8 were waited for; matrix products, arithmetic and copies ran while one was open for 0% of the time, Pallas kernels for 33%

profile of v2, /device:TPU:0, one launch (start us, length us, event | category | flops | bytes accessed | tf_op | source)
XLA Modules:
  0.0 68.3 jit_solution(4325147433934678688)
XLA Ops:
  0.6 2.5 %shard_map.138 = (f32[24,1280]{1,0:T(8,128)}, bf16[24,2688]{1,0:T(8,128)(2,1)}) custom-call(s32[1,8]{1,0:T(1,128)} %counts.3, s32[1,24]{1,0:T(1,128)} %chosen.3, f32[4]{0:T(128)} %mixw.3, bf16[4,128,1280]{2,1,0:T(8,128)(2,1)} %states.3, bf16[128,1280]{1,0:T(8,128)(2,1)} %cot.3, bf16[1280]{0:T(1024)(128)(2,1)} %router.1, bf16[1280]{0:T(1024)(128)(2,1)} %gain.1), custom_call_target="tpu_custom_call" | custom-call | tf_op jit(solution)/shard_map/pallas_call | solution.py:279
  3.1 4.1 %collective-permute-start.9 = (bf16[24,2688]{1,0:T(8,128)(2,1)}, bf16[24,2688]{1,0:T(8,128)(2,1)S(1)}, u32[]{:S(2)}, u32[]{:S(2)}) collective-permute-start(bf16[24,2688]{1,0:T(8,128)(2,1)} %get-tuple-element.50.refs_0_), channel_id=1, source_target_pairs={{0,16},{4,20},{8,24},{12,28},{16,0},{20,4},{24,8},{28,12},{1,17},{... | collective-permute-start | bytes 387080 | tf_op jit(solution)/shard_map/ppermute | solution.py:270
  7.3 1.6 %collective-permute-start.1 = (bf16[24,2688]{1,0:T(8,128)(2,1)}, bf16[24,2688]{1,0:T(8,128)(2,1)S(1)}, u32[]{:S(2)}, u32[]{:S(2)}) collective-permute-start(bf16[24,2688]{1,0:T(8,128)(2,1)} %get-tuple-element.50.refs_0_), channel_id=1, source_target_pairs={{0,8},{4,12},{8,0},{12,4},{16,24},{20,28},{24,16},{28,20},{1,9},{5... | collective-permute-start | bytes 387080 | tf_op jit(solution)/shard_map/ppermute | solution.py:270
  8.9 5.0 %collective-permute-done.9.refs_0_ = bf16[24,2688]{1,0:T(8,128)(2,1)S(1)} collective-permute-done((bf16[24,2688]{1,0:T(8,128)(2,1)}, bf16[24,2688]{1,0:T(8,128)(2,1)S(1)}, u32[]{:S(2)}, u32[]{:S(2)}) %collective-permute-start.9) | collective-permute-done | bytes 129056 | tf_op jit(solution)/shard_map/ppermute | solution.py:270
  13.8 0.7 %collective-permute-start.15 = (bf16[24,2688]{1,0:T(8,128)(2,1)S(1)}, bf16[24,2688]{1,0:T(8,128)(2,1)S(1)}, u32[]{:S(2)}, u32[]{:S(2)}) collective-permute-start(bf16[24,2688]{1,0:T(8,128)(2,1)S(1)} %collective-permute-done.9.refs_0_), channel_id=1, source_target_pairs={{0,8},{4,12},{8,0},{12,4},{16,24},{20,28},{24,16},{28,20},{1,9},{5... | collective-permute-start | bytes 387080 | tf_op jit(solution)/shard_map/ppermute | solution.py:270
  14.5 1.5 %collective-permute-start = (bf16[24,2688]{1,0:T(8,128)(2,1)}, bf16[24,2688]{1,0:T(8,128)(2,1)S(1)}, u32[]{:S(2)}, u32[]{:S(2)}) collective-permute-start(bf16[24,2688]{1,0:T(8,128)(2,1)} %get-tuple-element.50.refs_0_), channel_id=1, source_target_pairs={{0,4},{4,0},{8,12},{12,8},{16,20},{20,16},{24,28},{28,24},{1,5},{5... | collective-permute-start | bytes 387080 | tf_op jit(solution)/shard_map/ppermute | solution.py:270
  16.1 0.0 collective-permute-done.1.refs_2_
  16.1 0.5 collective-permute-start.2
  16.6 2.2 %collective-permute-done.15.refs_0_ = bf16[24,2688]{1,0:T(8,128)(2,1)S(1)} collective-permute-done((bf16[24,2688]{1,0:T(8,128)(2,1)S(1)}, bf16[24,2688]{1,0:T(8,128)(2,1)S(1)}, u32[]{:S(2)}, u32[]{:S(2)}) %collective-permute-start.15) | collective-permute-done | bytes 129056 | tf_op jit(solution)/shard_map/ppermute | solution.py:270
  18.8 1.6 %collective-permute-start.16 = (bf16[24,2688]{1,0:T(8,128)(2,1)S(1)}, bf16[24,2688]{1,0:T(8,128)(2,1)S(1)}, u32[]{:S(2)}, u32[]{:S(2)}) collective-permute-start(bf16[24,2688]{1,0:T(8,128)(2,1)S(1)} %collective-permute-done.15.refs_0_), channel_id=1, source_target_pairs={{0,4},{4,0},{8,12},{12,8},{16,20},{20,16},{24,28},{28,24},{1,5},{5... | collective-permute-start | bytes 387080 | tf_op jit(solution)/shard_map/ppermute | solution.py:270
  20.3 3.1 %shard_map.139 = (bf16[864,1280]{1,0:T(8,128)(2,1)S(1)}, bf16[864,1280]{1,0:T(8,128)(2,1)S(1)}, bf16[864,1280]{1,0:T(8,128)(2,1)S(1)}) custom-call(bf16[864,1280]{1,0:T(8,128)(2,1)} %bitcast.4, bf16[864,1280]{1,0:T(8,128)(2,1)} %bitcast.5, bf16[864,1280]{1,0:T(8,128)(2,1)} %refs_2_.1), custom_call_target="tpu_custom_call" | custom-call | bytes 13631488 | tf_op jit(solution)/shard_map/pallas_call | solution.py:293
  23.4 0.5 collective-permute-start.10
  23.9 0.0 collective-permute-done.refs_1_
  23.9 0.0 collective-permute-done.2.refs_3_
  23.9 2.4 %shard_map.140 = (f32[48,2688]{1,0:T(8,128)S(1)}, bf16[48,2688]{1,0:T(8,128)(2,1)S(1)}, bf16[96,2560]{1,0:T(8,128)(2,1)S(1)}) custom-call(bf16[24,2688]{1,0:T(8,128)(2,1)S(1)} %copy-done.2, bf16[24,2688]{1,0:T(8,128)(2,1)S(1)} %collective-permute-done.refs_1_, bf16[24,2688]{1,0:T(8,128)(2,1)S(1)} %collective-permute-done.1.refs_2_, ...), custom_call_target="tpu_custom_call" | custom-call | tf_op jit(solution)/shard_map/pallas_call | solution.py:308
  26.3 0.1 collective-permute-start.3
  26.4 0.2 collective-permute-done.16.refs_1_
  26.6 2.0 %shard_map.148 = (f32[24,2688]{1,0:T(8,128)S(1)}, bf16[24,2688]{1,0:T(8,128)(2,1)S(1)}, bf16[48,2560]{1,0:T(8,128)(2,1)S(1)}) custom-call(bf16[24,2688]{1,0:T(8,128)(2,1)S(1)} %collective-permute-done.15.refs_0_, bf16[24,2688]{1,0:T(8,128)(2,1)S(1)} %collective-permute-done.16.refs_1_, bf16[864,1280]{1,0:T(8,128)(2,1)S(1)} %get-tuple-element.51.refs_4_.gate_w.refs_2_, ...), custom_call_target="tpu_custom_call" | custom-call | tf_op jit(solution)/shard_map/pallas_call | solution.py:308
  28.6 0.4 collective-permute-start.17
  28.9 0.0 collective-permute-done.10.refs_1_
  28.9 2.0 %shard_map.144 = (f32[24,2688]{1,0:T(8,128)S(1)}, bf16[24,2688]{1,0:T(8,128)(2,1)S(1)}, bf16[48,2560]{1,0:T(8,128)(2,1)S(1)}) custom-call(bf16[24,2688]{1,0:T(8,128)(2,1)S(1)} %collective-permute-done.9.refs_0_, bf16[24,2688]{1,0:T(8,128)(2,1)S(1)} %collective-permute-done.10.refs_1_, bf16[864,1280]{1,0:T(8,128)(2,1)S(1)} %get-tuple-element.51.refs_4_.gate_w.refs_2_, ...), custom_call_target="tpu_custom_call" | custom-call | tf_op jit(solution)/shard_map/pallas_call | solution.py:308
  30.9 0.3 collective-permute-start.11
  31.2 0.0 collective-permute-done.17.got
  31.2 1.6 %collective-permute-start.18 = (bf16[24,2688]{1,0:T(8,128)(2,1)S(1)}, bf16[24,2688]{1,0:T(8,128)(2,1)S(1)}, u32[]{:S(2)}, u32[]{:S(2)}) collective-permute-start(bf16[24,2688]{1,0:T(8,128)(2,1)S(1)} %get-tuple-element.74), channel_id=1, source_target_pairs={{0,2},{1,3},{2,0},{3,1},{4,6},{5,7},{6,4},{7,5},{8,10},{9,11},{10,... | collective-permute-start | bytes 387080 | tf_op jit(solution)/shard_map/ppermute | solution.py:273
  32.8 1.1 %collective-permute-start.12 = (bf16[24,2688]{1,0:T(8,128)(2,1)S(1)}, bf16[24,2688]{1,0:T(8,128)(2,1)S(1)}, u32[]{:S(2)}, u32[]{:S(2)}) collective-permute-start(bf16[24,2688]{1,0:T(8,128)(2,1)S(1)} %get-tuple-element.68), channel_id=1, source_target_pairs={{0,2},{1,3},{2,0},{3,1},{4,6},{5,7},{6,4},{7,5},{8,10},{9,11},{10,... | collective-permute-start | bytes 387080 | tf_op jit(solution)/shard_map/ppermute | solution.py:273
  33.9 0.1 shard_map.141
  34.0 1.0 %collective-permute-start.4 = (bf16[48,2688]{1,0:T(8,128)(2,1)S(1)}, bf16[48,2688]{1,0:T(8,128)(2,1)S(1)}, u32[]{:S(2)}, u32[]{:S(2)}) collective-permute-start(bf16[48,2688]{1,0:T(8,128)(2,1)S(1)} %get-tuple-element.60), channel_id=1, source_target_pairs={{0,2},{1,3},{2,0},{3,1},{4,6},{5,7},{6,4},{7,5},{8,10},{9,11},{10,... | collective-permute-start | bytes 774152 | tf_op jit(solution)/shard_map/ppermute | solution.py:273
  35.1 2.6 %collective-permute-done.18.got = bf16[24,2688]{1,0:T(8,128)(2,1)S(1)} collective-permute-done((bf16[24,2688]{1,0:T(8,128)(2,1)S(1)}, bf16[24,2688]{1,0:T(8,128)(2,1)S(1)}, u32[]{:S(2)}, u32[]{:S(2)}) %collective-permute-start.18) | collective-permute-done | bytes 129056 | tf_op jit(solution)/shard_map/ppermute | solution.py:273
  37.6 0.4 shard_map.150.own
  38.0 0.0 collective-permute-start.19
  38.0 2.3 %collective-permute-done.12.got = bf16[24,2688]{1,0:T(8,128)(2,1)S(1)} collective-permute-done((bf16[24,2688]{1,0:T(8,128)(2,1)S(1)}, bf16[24,2688]{1,0:T(8,128)(2,1)S(1)}, u32[]{:S(2)}, u32[]{:S(2)}) %collective-permute-start.12) | collective-permute-done | bytes 129056 | tf_op jit(solution)/shard_map/ppermute | solution.py:273
  40.4 0.4 shard_map.146.own
  40.8 0.0 collective-permute-start.13
  40.8 0.0 collective-permute-done.19.got
  40.8 1.1 %shard_map.151 = (bf16[24,2688]{1,0:T(8,128)(2,1)S(1)}, bf16[24,2688]{1,0:T(8,128)(2,1)S(1)}, bf16[48,2688]{1,0:T(8,128)(2,1)S(1)}) custom-call(bf16[24,2688]{1,0:T(8,128)(2,1)S(1)} %shard_map.150.own, bf16[24,2688]{1,0:T(8,128)(2,1)S(1)} %collective-permute-done.19.got, bf16[864,1280]{1,0:T(8,128)(2,1)S(1)} %get-tuple-element.51.refs_4_.gate_w.refs_2_, ...), custom_call_target="tpu_custom_call" | custom-call | tf_op jit(solution)/shard_map/pallas_call | solution.py:323
  41.9 1.6 %collective-permute-start.20 = (bf16[24,2688]{1,0:T(8,128)(2,1)S(1)}, bf16[24,2688]{1,0:T(8,128)(2,1)S(1)}, u32[]{:S(2)}, u32[]{:S(2)}) collective-permute-start(bf16[24,2688]{1,0:T(8,128)(2,1)S(1)} %get-tuple-element.76), channel_id=1, source_target_pairs={{0,4},{4,0},{8,12},{12,8},{16,20},{20,16},{24,28},{28,24},{1,5},{5... | collective-permute-start | bytes 387080 | tf_op jit(solution)/shard_map/ppermute | solution.py:270
  43.5 0.0 collective-permute-done.13.got
  43.5 1.1 %shard_map.147 = (bf16[24,2688]{1,0:T(8,128)(2,1)S(1)}, bf16[24,2688]{1,0:T(8,128)(2,1)S(1)}, bf16[48,2688]{1,0:T(8,128)(2,1)S(1)}) custom-call(bf16[24,2688]{1,0:T(8,128)(2,1)S(1)} %shard_map.146.own, bf16[24,2688]{1,0:T(8,128)(2,1)S(1)} %collective-permute-done.13.got, bf16[864,1280]{1,0:T(8,128)(2,1)S(1)} %get-tuple-element.51.refs_4_.gate_w.refs_2_, ...), custom_call_target="tpu_custom_call" | custom-call | tf_op jit(solution)/shard_map/pallas_call | solution.py:323
  44.6 0.6 collective-permute-start.14
  45.2 0.0 collective-permute-done.4.got
  45.2 0.5 shard_map.142.own
  45.7 0.0 collective-permute-start.5
  45.8 2.4 %collective-permute-done.20 = bf16[24,2688]{1,0:T(8,128)(2,1)S(1)} collective-permute-done((bf16[24,2688]{1,0:T(8,128)(2,1)S(1)}, bf16[24,2688]{1,0:T(8,128)(2,1)S(1)}, u32[]{:S(2)}, u32[]{:S(2)}) %collective-permute-start.20) | collective-permute-done | bytes 129056 | tf_op jit(solution)/shard_map/ppermute | solution.py:270
  48.2 0.0 copy-start
  48.2 0.0 copy-start.1
  48.2 0.0 copy-start.4
  48.3 0.0 copy-start.5
  48.3 0.0 copy-start.6
  48.3 1.0 %collective-permute-start.21 = (bf16[24,2688]{1,0:T(8,128)(2,1)S(1)}, bf16[24,2688]{1,0:T(8,128)(2,1)S(1)}, u32[]{:S(2)}, u32[]{:S(2)}) collective-permute-start(bf16[24,2688]{1,0:T(8,128)(2,1)S(1)} %add_convert_fusion.1), channel_id=1, source_target_pairs={{0,8},{4,12},{8,0},{12,4},{16,24},{20,28},{24,16},{28,20},{1,9},{5... | collective-permute-start | bytes 387080 | tf_op jit(solution)/shard_map/ppermute | solution.py:270
  49.3 1.3 %shard_map.143 = (bf16[24,2688]{1,0:T(8,128)(2,1)S(1)}, bf16[24,2688]{1,0:T(8,128)(2,1)S(1)}, bf16[24,2688]{1,0:T(8,128)(2,1)S(1)}, bf16[24,2688]{1,0:T(8,128)(2,1)S(1)}, bf16[96,2688]{1,0:T(8,128)(2,1)S(1)}) custom-call(bf16[48,2688]{1,0:T(8,128)(2,1)S(1)} %shard_map.142.own, bf16[48,2688]{1,0:T(8,128)(2,1)S(1)} %collective-permute-done.5.got, ...), custom_call_target="tpu_custom_call" | custom-call | tf_op jit(solution)/shard_map/pallas_call | solution.py:323
  50.6 0.0 copy-start.7
  50.7 0.0 copy-start.8
  50.7 1.7 %collective-permute-start.6 = (bf16[24,2688]{1,0:T(8,128)(2,1)S(1)}, bf16[24,2688]{1,0:T(8,128)(2,1)S(1)}, u32[]{:S(2)}, u32[]{:S(2)}) collective-permute-start(bf16[24,2688]{1,0:T(8,128)(2,1)S(1)} %get-tuple-element.62), channel_id=1, source_target_pairs={{0,4},{4,0},{8,12},{12,8},{16,20},{20,16},{24,28},{28,24},{1,5},{5... | collective-permute-start | bytes 387080 | tf_op jit(solution)/shard_map/ppermute | solution.py:270
  52.4 0.4 collective-permute-start.7
  52.8 0.5 collective-permute-done.21
  53.3 2.9 %collective-permute-start.22 = (bf16[24,2688]{1,0:T(8,128)(2,1)S(1)}, bf16[24,2688]{1,0:T(8,128)(2,1)S(1)}, u32[]{:S(2)}, u32[]{:S(2)}) collective-permute-start(bf16[24,2688]{1,0:T(8,128)(2,1)S(1)} %add_convert_fusion), channel_id=1, source_target_pairs={{0,16},{4,20},{8,24},{12,28},{16,0},{20,4},{24,8},{28,12},{1,17},{... | collective-permute-start | bytes 387080 | tf_op jit(solution)/shard_map/ppermute | solution.py:270
  56.2 1.6 %collective-permute-done.7 = bf16[24,2688]{1,0:T(8,128)(2,1)S(1)} collective-permute-done((bf16[24,2688]{1,0:T(8,128)(2,1)S(1)}, bf16[24,2688]{1,0:T(8,128)(2,1)S(1)}, u32[]{:S(2)}, u32[]{:S(2)}) %collective-permute-start.7) | collective-permute-done | bytes 129056 | tf_op jit(solution)/shard_map/ppermute | solution.py:270
  57.9 1.1 %collective-permute-start.8 = (bf16[24,2688]{1,0:T(8,128)(2,1)S(1)}, bf16[24,2688]{1,0:T(8,128)(2,1)S(1)}, u32[]{:S(2)}, u32[]{:S(2)}) collective-permute-start(bf16[24,2688]{1,0:T(8,128)(2,1)S(1)} %add_convert_fusion.2), channel_id=1, source_target_pairs={{0,8},{4,12},{8,0},{12,4},{16,24},{20,28},{24,16},{28,20},{1,9},{5... | collective-permute-start | bytes 387080 | tf_op jit(solution)/shard_map/ppermute | solution.py:270
  59.0 1.6 %shard_map.137 = (bf16[128,1280]{1,0:T(8,128)(2,1)S(1)}, bf16[128,1280]{1,0:T(8,128)(2,1)S(1)}, bf16[128,24]{1,0:T(8,128)(2,1)S(1)}) custom-call(s32[1,8]{1,0:T(1,128)S(1)} %copy-done.4, s32[1,24]{1,0:T(1,128)S(1)} %copy-done.5, f32[4]{0:T(128)S(1)} %copy-done.6, bf16[4,128,1280]{2,1,0:T(8,128)(2,1)S(1)} %copy-done, bf16[128,1280]{1,0:T(8,128)(2,1)S(1)} %copy-done.1), custom_call_target="tpu_custom_call" | custom-call | bytes 3145728 | tf_op jit(solution)/shard_map/pallas_call | solution.py:296
  60.7 0.1 shard_map.153
  60.8 0.0 copy-start.3
  60.8 2.5 %shard_map.155 = f32[864,1280]{1,0:T(8,128)} custom-call(bf16[192,864]{1,0:T(8,128)(2,1)S(1)} %get-tuple-element.89.refs_0_, bf16[192,1280]{1,0:T(8,128)(2,1)S(1)} %get-tuple-element.90.refs_1_), custom_call_target="tpu_custom_call" | custom-call | bytes 4423680 | tf_op jit(solution)/shard_map/pallas_call | solution.py:358
  63.3 3.9 %shard_map.154 = (f32[864,1280]{1,0:T(8,128)}, f32[864,1280]{1,0:T(8,128)}) custom-call(bf16[192,864]{1,0:T(8,128)(2,1)S(1)} %get-tuple-element.84.refs_0_, bf16[192,864]{1,0:T(8,128)(2,1)S(1)} %get-tuple-element.85.refs_1_, bf16[192,1280]{1,0:T(8,128)(2,1)S(1)} %get-tuple-element.86.refs_2_.refs_3_, bf16[192,1280]{1,0:T(8,128)(2,1)S(1)} %get-tuple-element.86.refs_2_.refs_3_), custom_call_target="tpu_custom_call" | custom-call | bytes 8847360 | tf_op jit(solution)/shard_map/pallas_call | solution.py:358
  67.3 1.1 %shard_map.152 = (bf16[128,1280]{1,0:T(8,128)(2,1)}, bf16[128,1280]{1,0:T(8,128)(2,1)}) custom-call(bf16[128,24]{1,0:T(8,128)(2,1)S(1)} %get-tuple-element.48.want, f32[24,1280]{1,0:T(8,128)S(1)} %copy-done.3, bf16[96,2560]{1,0:T(8,128)(2,1)S(1)} %get-tuple-element.54.taken.refs_3_, bf16[128,1280]{1,0:T(8,128)(2,1)S(1)} %get-tuple-element.55.mixed, ...), custom_call_target="tpu_custom_call" | custom-call | tf_op jit(solution)/shard_map/pallas_call | solution.py:371
  (24 shorter events, 0.3 us)
Async XLA Ops:
  3.1 10.7 %collective-permute-start.9 = (bf16[24,2688]{1,0:T(8,128)(2,1)}, bf16[24,2688]{1,0:T(8,128)(2,1)S(1)}, u32[]{:S(2)}, u32[]{:S(2)}) collective-permute-start(bf16[24,2688]{1,0:T(8,128)(2,1)} %get-tuple-element.50.refs_0_), channel_id=1, source_target_pairs={{0,16},{4,20},{8,24},{12,28},{16,0},{20,4},{24,8},{28,12},{1,17},{... | collective-permute-start | bytes 387080 | tf_op jit(solution)/shard_map/ppermute | solution.py:270
  7.3 8.8 %collective-permute-start.1 = (bf16[24,2688]{1,0:T(8,128)(2,1)}, bf16[24,2688]{1,0:T(8,128)(2,1)S(1)}, u32[]{:S(2)}, u32[]{:S(2)}) collective-permute-start(bf16[24,2688]{1,0:T(8,128)(2,1)} %get-tuple-element.50.refs_0_), channel_id=1, source_target_pairs={{0,8},{4,12},{8,0},{12,4},{16,24},{20,28},{24,16},{28,20},{1,9},{5... | collective-permute-start | bytes 387080 | tf_op jit(solution)/shard_map/ppermute | solution.py:270
  13.8 4.9 %collective-permute-start.15 = (bf16[24,2688]{1,0:T(8,128)(2,1)S(1)}, bf16[24,2688]{1,0:T(8,128)(2,1)S(1)}, u32[]{:S(2)}, u32[]{:S(2)}) collective-permute-start(bf16[24,2688]{1,0:T(8,128)(2,1)S(1)} %collective-permute-done.9.refs_0_), channel_id=1, source_target_pairs={{0,8},{4,12},{8,0},{12,4},{16,24},{20,28},{24,16},{28,20},{1,9},{5... | collective-permute-start | bytes 387080 | tf_op jit(solution)/shard_map/ppermute | solution.py:270
  14.5 9.4 %collective-permute-start = (bf16[24,2688]{1,0:T(8,128)(2,1)}, bf16[24,2688]{1,0:T(8,128)(2,1)S(1)}, u32[]{:S(2)}, u32[]{:S(2)}) collective-permute-start(bf16[24,2688]{1,0:T(8,128)(2,1)} %get-tuple-element.50.refs_0_), channel_id=1, source_target_pairs={{0,4},{4,0},{8,12},{12,8},{16,20},{20,16},{24,28},{28,24},{1,5},{5... | collective-permute-start | bytes 387080 | tf_op jit(solution)/shard_map/ppermute | solution.py:270
  16.1 7.9 %collective-permute-start.2 = (bf16[24,2688]{1,0:T(8,128)(2,1)S(1)}, bf16[24,2688]{1,0:T(8,128)(2,1)S(1)}, u32[]{:S(2)}, u32[]{:S(2)}) collective-permute-start(bf16[24,2688]{1,0:T(8,128)(2,1)S(1)} %collective-permute-done.1.refs_2_), channel_id=1, source_target_pairs={{0,4},{4,0},{8,12},{12,8},{16,20},{20,16},{24,28},{28,24},{1,5},{5... | collective-permute-start | bytes 387080 | tf_op jit(solution)/shard_map/ppermute | solution.py:270
  18.8 7.8 %collective-permute-start.16 = (bf16[24,2688]{1,0:T(8,128)(2,1)S(1)}, bf16[24,2688]{1,0:T(8,128)(2,1)S(1)}, u32[]{:S(2)}, u32[]{:S(2)}) collective-permute-start(bf16[24,2688]{1,0:T(8,128)(2,1)S(1)} %collective-permute-done.15.refs_0_), channel_id=1, source_target_pairs={{0,4},{4,0},{8,12},{12,8},{16,20},{20,16},{24,28},{28,24},{1,5},{5... | collective-permute-start | bytes 387080 | tf_op jit(solution)/shard_map/ppermute | solution.py:270
  20.3 3.6 %copy-start.2 = (bf16[24,2688]{1,0:T(8,128)(2,1)S(1)}, bf16[24,2688]{1,0:T(8,128)(2,1)}, u32[]{:S(2)}) copy-start(bf16[24,2688]{1,0:T(8,128)(2,1)} %get-tuple-element.50.refs_0_) | copy-start | bytes 387076
  23.4 5.5 %collective-permute-start.10 = (bf16[24,2688]{1,0:T(8,128)(2,1)S(1)}, bf16[24,2688]{1,0:T(8,128)(2,1)S(1)}, u32[]{:S(2)}, u32[]{:S(2)}) collective-permute-start(bf16[24,2688]{1,0:T(8,128)(2,1)S(1)} %collective-permute-done.9.refs_0_), channel_id=1, source_target_pairs={{0,4},{4,0},{8,12},{12,8},{16,20},{20,16},{24,28},{28,24},{1,5},{5... | collective-permute-start | bytes 387080 | tf_op jit(solution)/shard_map/ppermute | solution.py:270
  26.3 7.6 %collective-permute-start.3 = (bf16[48,2688]{1,0:T(8,128)(2,1)S(1)}, bf16[48,2688]{1,0:T(8,128)(2,1)S(1)}, u32[]{:S(2)}, u32[]{:S(2)}) collective-permute-start(bf16[48,2688]{1,0:T(8,128)(2,1)S(1)} %get-tuple-element.58), channel_id=1, source_target_pairs={{0,1},{1,0},{2,3},{3,2},{4,5},{5,4},{6,7},{7,6},{8,9},{9,8},{10,11... | collective-permute-start | bytes 774152 | tf_op jit(solution)/shard_map/ppermute | solution.py:273
  28.6 2.6 %collective-permute-start.17 = (bf16[24,2688]{1,0:T(8,128)(2,1)S(1)}, bf16[24,2688]{1,0:T(8,128)(2,1)S(1)}, u32[]{:S(2)}, u32[]{:S(2)}) collective-permute-start(bf16[24,2688]{1,0:T(8,128)(2,1)S(1)} %get-tuple-element.72), channel_id=1, source_target_pairs={{0,1},{1,0},{2,3},{3,2},{4,5},{5,4},{6,7},{7,6},{8,9},{9,8},{10,11... | collective-permute-start | bytes 387080 | tf_op jit(solution)/shard_map/ppermute | solution.py:273
  30.9 1.9 %collective-permute-start.11 = (bf16[24,2688]{1,0:T(8,128)(2,1)S(1)}, bf16[24,2688]{1,0:T(8,128)(2,1)S(1)}, u32[]{:S(2)}, u32[]{:S(2)}) collective-permute-start(bf16[24,2688]{1,0:T(8,128)(2,1)S(1)} %get-tuple-element.66), channel_id=1, source_target_pairs={{0,1},{1,0},{2,3},{3,2},{4,5},{5,4},{6,7},{7,6},{8,9},{9,8},{10,11... | collective-permute-start | bytes 387080 | tf_op jit(solution)/shard_map/ppermute | solution.py:273
  31.2 6.4 %collective-permute-start.18 = (bf16[24,2688]{1,0:T(8,128)(2,1)S(1)}, bf16[24,2688]{1,0:T(8,128)(2,1)S(1)}, u32[]{:S(2)}, u32[]{:S(2)}) collective-permute-start(bf16[24,2688]{1,0:T(8,128)(2,1)S(1)} %get-tuple-element.74), channel_id=1, source_target_pairs={{0,2},{1,3},{2,0},{3,1},{4,6},{5,7},{6,4},{7,5},{8,10},{9,11},{10,... | collective-permute-start | bytes 387080 | tf_op jit(solution)/shard_map/ppermute | solution.py:273
  32.8 7.6 %collective-permute-start.12 = (bf16[24,2688]{1,0:T(8,128)(2,1)S(1)}, bf16[24,2688]{1,0:T(8,128)(2,1)S(1)}, u32[]{:S(2)}, u32[]{:S(2)}) collective-permute-start(bf16[24,2688]{1,0:T(8,128)(2,1)S(1)} %get-tuple-element.68), channel_id=1, source_target_pairs={{0,2},{1,3},{2,0},{3,1},{4,6},{5,7},{6,4},{7,5},{8,10},{9,11},{10,... | collective-permute-start | bytes 387080 | tf_op jit(solution)/shard_map/ppermute | solution.py:273
  34.0 11.2 %collective-permute-start.4 = (bf16[48,2688]{1,0:T(8,128)(2,1)S(1)}, bf16[48,2688]{1,0:T(8,128)(2,1)S(1)}, u32[]{:S(2)}, u32[]{:S(2)}) collective-permute-start(bf16[48,2688]{1,0:T(8,128)(2,1)S(1)} %get-tuple-element.60), channel_id=1, source_target_pairs={{0,2},{1,3},{2,0},{3,1},{4,6},{5,7},{6,4},{7,5},{8,10},{9,11},{10,... | collective-permute-start | bytes 774152 | tf_op jit(solution)/shard_map/ppermute | solution.py:273
  38.0 2.8 %collective-permute-start.19 = (bf16[24,2688]{1,0:T(8,128)(2,1)S(1)}, bf16[24,2688]{1,0:T(8,128)(2,1)S(1)}, u32[]{:S(2)}, u32[]{:S(2)}) collective-permute-start(bf16[24,2688]{1,0:T(8,128)(2,1)S(1)} %shard_map.150.own), channel_id=1, source_target_pairs={{0,1},{1,0},{2,3},{3,2},{4,5},{5,4},{6,7},{7,6},{8,9},{9,8},{10,11... | collective-permute-start | bytes 387080 | tf_op jit(solution)/shard_map/ppermute | solution.py:273
  40.8 2.7 %collective-permute-start.13 = (bf16[24,2688]{1,0:T(8,128)(2,1)S(1)}, bf16[24,2688]{1,0:T(8,128)(2,1)S(1)}, u32[]{:S(2)}, u32[]{:S(2)}) collective-permute-start(bf16[24,2688]{1,0:T(8,128)(2,1)S(1)} %shard_map.146.own), channel_id=1, source_target_pairs={{0,1},{1,0},{2,3},{3,2},{4,5},{5,4},{6,7},{7,6},{8,9},{9,8},{10,11... | collective-permute-start | bytes 387080 | tf_op jit(solution)/shard_map/ppermute | solution.py:273
  41.9 6.3 %collective-permute-start.20 = (bf16[24,2688]{1,0:T(8,128)(2,1)S(1)}, bf16[24,2688]{1,0:T(8,128)(2,1)S(1)}, u32[]{:S(2)}, u32[]{:S(2)}) collective-permute-start(bf16[24,2688]{1,0:T(8,128)(2,1)S(1)} %get-tuple-element.76), channel_id=1, source_target_pairs={{0,4},{4,0},{8,12},{12,8},{16,20},{20,16},{24,28},{28,24},{1,5},{5... | collective-permute-start | bytes 387080 | tf_op jit(solution)/shard_map/ppermute | solution.py:270
  44.6 8.1 %collective-permute-start.14 = (bf16[24,2688]{1,0:T(8,128)(2,1)S(1)}, bf16[24,2688]{1,0:T(8,128)(2,1)S(1)}, u32[]{:S(2)}, u32[]{:S(2)}) collective-permute-start(bf16[24,2688]{1,0:T(8,128)(2,1)S(1)} %get-tuple-element.70), channel_id=1, source_target_pairs={{0,4},{4,0},{8,12},{12,8},{16,20},{20,16},{24,28},{28,24},{1,5},{5... | collective-permute-start | bytes 387080 | tf_op jit(solution)/shard_map/ppermute | solution.py:270
  45.7 3.6 %collective-permute-start.5 = (bf16[48,2688]{1,0:T(8,128)(2,1)S(1)}, bf16[48,2688]{1,0:T(8,128)(2,1)S(1)}, u32[]{:S(2)}, u32[]{:S(2)}) collective-permute-start(bf16[48,2688]{1,0:T(8,128)(2,1)S(1)} %shard_map.142.own), channel_id=1, source_target_pairs={{0,1},{1,0},{2,3},{3,2},{4,5},{5,4},{6,7},{7,6},{8,9},{9,8},{10,11... | collective-permute-start | bytes 774152 | tf_op jit(solution)/shard_map/ppermute | solution.py:273
  48.2 10.8 %copy-start = (bf16[4,128,1280]{2,1,0:T(8,128)(2,1)S(1)}, bf16[4,128,1280]{2,1,0:T(8,128)(2,1)}, u32[]{:S(2)}) copy-start(bf16[4,128,1280]{2,1,0:T(8,128)(2,1)} %states.3) | copy-start | bytes 3932164
  48.2 10.8 %copy-start.1 = (bf16[128,1280]{1,0:T(8,128)(2,1)S(1)}, bf16[128,1280]{1,0:T(8,128)(2,1)}, u32[]{:S(2)}) copy-start(bf16[128,1280]{1,0:T(8,128)(2,1)} %cot.3) | copy-start | bytes 983044
  48.2 10.8 %copy-start.4 = (s32[1,8]{1,0:T(1,128)S(1)}, s32[1,8]{1,0:T(1,128)}, u32[]{:S(2)}) copy-start(s32[1,8]{1,0:T(1,128)} %counts.3) | copy-start | bytes 100
  48.3 10.8 %copy-start.5 = (s32[1,24]{1,0:T(1,128)S(1)}, s32[1,24]{1,0:T(1,128)}, u32[]{:S(2)}) copy-start(s32[1,24]{1,0:T(1,128)} %chosen.3) | copy-start | bytes 292
  48.3 10.8 %copy-start.6 = (f32[4]{0:T(128)S(1)}, f32[4]{0:T(128)}, u32[]{:S(2)}) copy-start(f32[4]{0:T(128)} %mixw.3) | copy-start | bytes 52
  48.3 5.0 %collective-permute-start.21 = (bf16[24,2688]{1,0:T(8,128)(2,1)S(1)}, bf16[24,2688]{1,0:T(8,128)(2,1)S(1)}, u32[]{:S(2)}, u32[]{:S(2)}) collective-permute-start(bf16[24,2688]{1,0:T(8,128)(2,1)S(1)} %add_convert_fusion.1), channel_id=1, source_target_pairs={{0,8},{4,12},{8,0},{12,4},{16,24},{20,28},{24,16},{28,20},{1,9},{5... | collective-permute-start | bytes 387080 | tf_op jit(solution)/shard_map/ppermute | solution.py:270
  50.6 10.0 %copy-start.7 = (bf16[1280]{0:T(1024)(128)(2,1)S(1)}, bf16[1280]{0:T(1024)(128)(2,1)}, u32[]{:S(2)}) copy-start(bf16[1280]{0:T(1024)(128)(2,1)} %router.1) | copy-start | bytes 7684
  50.7 10.0 %copy-start.8 = (bf16[1280]{0:T(1024)(128)(2,1)S(1)}, bf16[1280]{0:T(1024)(128)(2,1)}, u32[]{:S(2)}) copy-start(bf16[1280]{0:T(1024)(128)(2,1)} %gain.1) | copy-start | bytes 7684
  50.7 16.6 %collective-permute-start.6 = (bf16[24,2688]{1,0:T(8,128)(2,1)S(1)}, bf16[24,2688]{1,0:T(8,128)(2,1)S(1)}, u32[]{:S(2)}, u32[]{:S(2)}) collective-permute-start(bf16[24,2688]{1,0:T(8,128)(2,1)S(1)} %get-tuple-element.62), channel_id=1, source_target_pairs={{0,4},{4,0},{8,12},{12,8},{16,20},{20,16},{24,28},{28,24},{1,5},{5... | collective-permute-start | bytes 387080 | tf_op jit(solution)/shard_map/ppermute | solution.py:270
  52.4 5.5 %collective-permute-start.7 = (bf16[24,2688]{1,0:T(8,128)(2,1)S(1)}, bf16[24,2688]{1,0:T(8,128)(2,1)S(1)}, u32[]{:S(2)}, u32[]{:S(2)}) collective-permute-start(bf16[24,2688]{1,0:T(8,128)(2,1)S(1)} %get-tuple-element.64), channel_id=1, source_target_pairs={{0,4},{4,0},{8,12},{12,8},{16,20},{20,16},{24,28},{28,24},{1,5},{5... | collective-permute-start | bytes 387080 | tf_op jit(solution)/shard_map/ppermute | solution.py:270
  53.3 13.9 %collective-permute-start.22 = (bf16[24,2688]{1,0:T(8,128)(2,1)S(1)}, bf16[24,2688]{1,0:T(8,128)(2,1)S(1)}, u32[]{:S(2)}, u32[]{:S(2)}) collective-permute-start(bf16[24,2688]{1,0:T(8,128)(2,1)S(1)} %add_convert_fusion), channel_id=1, source_target_pairs={{0,16},{4,20},{8,24},{12,28},{16,0},{20,4},{24,8},{28,12},{1,17},{... | collective-permute-start | bytes 387080 | tf_op jit(solution)/shard_map/ppermute | solution.py:270
  57.9 9.3 %collective-permute-start.8 = (bf16[24,2688]{1,0:T(8,128)(2,1)S(1)}, bf16[24,2688]{1,0:T(8,128)(2,1)S(1)}, u32[]{:S(2)}, u32[]{:S(2)}) collective-permute-start(bf16[24,2688]{1,0:T(8,128)(2,1)S(1)} %add_convert_fusion.2), channel_id=1, source_target_pairs={{0,8},{4,12},{8,0},{12,4},{16,24},{20,28},{24,16},{28,20},{1,9},{5... | collective-permute-start | bytes 387080 | tf_op jit(solution)/shard_map/ppermute | solution.py:270
  60.8 6.4 %copy-start.3 = (f32[24,1280]{1,0:T(8,128)S(1)}, f32[24,1280]{1,0:T(8,128)}, u32[]{:S(2)}) copy-start(f32[24,1280]{1,0:T(8,128)} %get-tuple-element.49.picked) | copy-start | bytes 368644

commit v3 on v2

--- a/solution.py
+++ b/solution.py
@@ -117,12 +117,7 @@
 
 
 def first_kernel(slots, lanes, *refs):
-    blocks, (gate_w, up_w, down_w, own_ref, send_ref, rows_ref, sums_ref) = refs[:slots], refs[slots : slots + 7]
-    if len(refs) > slots + 7:
-        mine_ref, sem = refs[slots + 7 :]
-        (copy,) = fetch([(blocks[0], mine_ref)], sem)
-        copy.wait()
-        blocks = (mine_ref,) + blocks[1:]
+    blocks, (gate_w, up_w, down_w, own_ref, send_ref, rows_ref, sums_ref) = refs[:slots], refs[slots:]
     core = lax.axis_index("tensor") % 2
     ff, width = gate_w.shape
     rows = jnp.concatenate([block[...].astype(f32) for block in blocks], axis=0)
@@ -304,12 +299,11 @@
     def summed(chosen_slots):
         part = len(chosen_slots)
         rows, half = part * cap, part * cap // 2
-        near = chosen_slots[0] == 0
         own, send, taken = call(
             functools.partial(first_kernel, part, lanes),
             (sds((half, 3 * lanes), f32), sds((half, 3 * lanes), bf16), sds((rows, 2 * width), bf16)),
-            [anywhere if near else VMEM] + [VMEM] * (part + 2),
-            [pltpu.VMEM((rows, 3 * lanes), f32)] + ([copy_of(load), sem] if near else []),
+            [VMEM] * (part + 3),
+            [pltpu.VMEM((rows, 3 * lanes), f32)],
         )(*[blocks[k] for k in chosen_slots], *weights)
         send, own = call(
             add_kernel, (sds((half, 3 * lanes), bf16), sds((half, 3 * lanes), f32)), [VMEM] * 2

time: 68.5 us -> 68.5 us (level)
  transfers between devices with their start and end apart: 23 -> 23, of which waited for: 8 -> 8; matrix products, arithmetic and copies ran while one was open for 0% -> 0% of each run, Pallas kernels for 33% -> 32%
where the time goes in v3:
time: 68.5 us; the launch traced here: 68.3 us
  Pallas kernels  25.8 us (38%)
  starting transfers between devices  24.4 us (36%)
  waiting for transfers between devices  17 us (25%)
  between operations  0.94 us (1%)
    ppermute x14, starting transfers between devices, over_dp(): return lax.ppermute(x, 'dp', [(i, i ^ k) for i in range(slots)])  20 us
    ppermute x14, waiting for transfers between devices, over_dp(): return lax.ppermute(x, 'dp', [(i, i ^ k) for i in range(slots)])  12.1 us
    pallas_call x2, Pallas kernels, grads(): pl.pallas_call(functools.partial(grad_kernel, tile, count), out_shape=(ou...  6.38 us
    pallas_call x3, Pallas kernels, summed(): call(functools.partial(first_kernel, part, lanes), (sds((half, 3 * lanes)...  6.04 us
    ppermute x9, waiting for transfers between devices, over_tensor(): return lax.ppermute(x, 'tensor', [(i, i ^ k) for i in range(tensor)])  4.92 us
    ppermute x9, starting transfers between devices, over_tensor(): return lax.ppermute(x, 'tensor', [(i, i ^ k) for i in range(tensor)])  4.44 us
    pallas_call x3, Pallas kernels, acted(): call(functools.partial(second_kernel, part, lanes), tuple([block] * part...  3.52 us
    pallas_call x1, Pallas kernels, fast(): call(weights_kernel, (weight,) * 3, [hbm] * 3, [sem], nbytes=13 << 20, vm...  3.06 us
  transfers between devices with their start and end apart: 23, of which 8 were waited for; matrix products, arithmetic and copies ran while one was open for 0% of the time, Pallas kernels for 32%

profile of v3, /device:TPU:0, one launch (start us, length us, event | category | flops | bytes accessed | tf_op | source)
XLA Modules:
  0.0 68.3 jit_solution(4122380813538356859)
XLA Ops:
  0.6 2.5 %shard_map.138 = (f32[24,1280]{1,0:T(8,128)}, bf16[24,2688]{1,0:T(8,128)(2,1)}) custom-call(s32[1,8]{1,0:T(1,128)} %counts.3, s32[1,24]{1,0:T(1,128)} %chosen.3, f32[4]{0:T(128)} %mixw.3, bf16[4,128,1280]{2,1,0:T(8,128)(2,1)} %states.3, bf16[128,1280]{1,0:T(8,128)(2,1)} %cot.3, bf16[1280]{0:T(1024)(128)(2,1)} %router.1, bf16[1280]{0:T(1024)(128)(2,1)} %gain.1), custom_call_target="tpu_custom_call" | custom-call | tf_op jit(solution)/shard_map/pallas_call | solution.py:274
  3.1 4.1 %collective-permute-start.9 = (bf16[24,2688]{1,0:T(8,128)(2,1)}, bf16[24,2688]{1,0:T(8,128)(2,1)S(1)}, u32[]{:S(2)}, u32[]{:S(2)}) collective-permute-start(bf16[24,2688]{1,0:T(8,128)(2,1)} %get-tuple-element.50.refs_0_), channel_id=1, source_target_pairs={{0,16},{4,20},{8,24},{12,28},{16,0},{20,4},{24,8},{28,12},{1,17},{... | collective-permute-start | bytes 387080 | tf_op jit(solution)/shard_map/ppermute | solution.py:265
  7.3 1.6 %collective-permute-start.1 = (bf16[24,2688]{1,0:T(8,128)(2,1)}, bf16[24,2688]{1,0:T(8,128)(2,1)S(1)}, u32[]{:S(2)}, u32[]{:S(2)}) collective-permute-start(bf16[24,2688]{1,0:T(8,128)(2,1)} %get-tuple-element.50.refs_0_), channel_id=1, source_target_pairs={{0,8},{4,12},{8,0},{12,4},{16,24},{20,28},{24,16},{28,20},{1,9},{5... | collective-permute-start | bytes 387080 | tf_op jit(solution)/shard_map/ppermute | solution.py:265
  8.9 5.0 %collective-permute-done.9.refs_0_ = bf16[24,2688]{1,0:T(8,128)(2,1)S(1)} collective-permute-done((bf16[24,2688]{1,0:T(8,128)(2,1)}, bf16[24,2688]{1,0:T(8,128)(2,1)S(1)}, u32[]{:S(2)}, u32[]{:S(2)}) %collective-permute-start.9) | collective-permute-done | bytes 129056 | tf_op jit(solution)/shard_map/ppermute | solution.py:265
  13.8 0.7 %collective-permute-start.15 = (bf16[24,2688]{1,0:T(8,128)(2,1)S(1)}, bf16[24,2688]{1,0:T(8,128)(2,1)S(1)}, u32[]{:S(2)}, u32[]{:S(2)}) collective-permute-start(bf16[24,2688]{1,0:T(8,128)(2,1)S(1)} %collective-permute-done.9.refs_0_), channel_id=1, source_target_pairs={{0,8},{4,12},{8,0},{12,4},{16,24},{20,28},{24,16},{28,20},{1,9},{5... | collective-permute-start | bytes 387080 | tf_op jit(solution)/shard_map/ppermute | solution.py:265
  14.5 1.5 %collective-permute-start = (bf16[24,2688]{1,0:T(8,128)(2,1)}, bf16[24,2688]{1,0:T(8,128)(2,1)S(1)}, u32[]{:S(2)}, u32[]{:S(2)}) collective-permute-start(bf16[24,2688]{1,0:T(8,128)(2,1)} %get-tuple-element.50.refs_0_), channel_id=1, source_target_pairs={{0,4},{4,0},{8,12},{12,8},{16,20},{20,16},{24,28},{28,24},{1,5},{5... | collective-permute-start | bytes 387080 | tf_op jit(solution)/shard_map/ppermute | solution.py:265
  16.1 0.0 collective-permute-done.1.refs_2_
  16.1 0.5 collective-permute-start.2
  16.6 2.2 %collective-permute-done.15.refs_0_ = bf16[24,2688]{1,0:T(8,128)(2,1)S(1)} collective-permute-done((bf16[24,2688]{1,0:T(8,128)(2,1)S(1)}, bf16[24,2688]{1,0:T(8,128)(2,1)S(1)}, u32[]{:S(2)}, u32[]{:S(2)}) %collective-permute-start.15) | collective-permute-done | bytes 129056 | tf_op jit(solution)/shard_map/ppermute | solution.py:265
  18.8 1.6 %collective-permute-start.16 = (bf16[24,2688]{1,0:T(8,128)(2,1)S(1)}, bf16[24,2688]{1,0:T(8,128)(2,1)S(1)}, u32[]{:S(2)}, u32[]{:S(2)}) collective-permute-start(bf16[24,2688]{1,0:T(8,128)(2,1)S(1)} %collective-permute-done.15.refs_0_), channel_id=1, source_target_pairs={{0,4},{4,0},{8,12},{12,8},{16,20},{20,16},{24,28},{28,24},{1,5},{5... | collective-permute-start | bytes 387080 | tf_op jit(solution)/shard_map/ppermute | solution.py:265
  20.3 3.1 %shard_map.139 = (bf16[864,1280]{1,0:T(8,128)(2,1)S(1)}, bf16[864,1280]{1,0:T(8,128)(2,1)S(1)}, bf16[864,1280]{1,0:T(8,128)(2,1)S(1)}) custom-call(bf16[864,1280]{1,0:T(8,128)(2,1)} %bitcast.4, bf16[864,1280]{1,0:T(8,128)(2,1)} %bitcast.5, bf16[864,1280]{1,0:T(8,128)(2,1)} %refs_2_.1), custom_call_target="tpu_custom_call" | custom-call | bytes 13631488 | tf_op jit(solution)/shard_map/pallas_call | solution.py:288
  23.4 0.5 collective-permute-start.10
  23.9 0.0 collective-permute-done.refs_1_
  23.9 0.0 collective-permute-done.2.refs_3_
  23.9 2.1 %shard_map.140 = (f32[48,2688]{1,0:T(8,128)S(1)}, bf16[48,2688]{1,0:T(8,128)(2,1)S(1)}, bf16[96,2560]{1,0:T(8,128)(2,1)S(1)}) custom-call(bf16[24,2688]{1,0:T(8,128)(2,1)S(1)} %copy-done.2, bf16[24,2688]{1,0:T(8,128)(2,1)S(1)} %collective-permute-done.refs_1_, bf16[24,2688]{1,0:T(8,128)(2,1)S(1)} %collective-permute-done.1.refs_2_, ...), custom_call_target="tpu_custom_call" | custom-call | tf_op jit(solution)/shard_map/pallas_call | solution.py:302
  26.1 0.1 collective-permute-start.3
  26.1 0.5 collective-permute-done.16.refs_1_
  26.6 2.0 %shard_map.148 = (f32[24,2688]{1,0:T(8,128)S(1)}, bf16[24,2688]{1,0:T(8,128)(2,1)S(1)}, bf16[48,2560]{1,0:T(8,128)(2,1)S(1)}) custom-call(bf16[24,2688]{1,0:T(8,128)(2,1)S(1)} %collective-permute-done.15.refs_0_, bf16[24,2688]{1,0:T(8,128)(2,1)S(1)} %collective-permute-done.16.refs_1_, bf16[864,1280]{1,0:T(8,128)(2,1)S(1)} %get-tuple-element.51.refs_4_.gate_w.refs_2_, ...), custom_call_target="tpu_custom_call" | custom-call | tf_op jit(solution)/shard_map/pallas_call | solution.py:302
  28.6 0.1 collective-permute-start.17
  28.7 0.0 collective-permute-done.10.refs_1_
  28.7 2.0 %shard_map.144 = (f32[24,2688]{1,0:T(8,128)S(1)}, bf16[24,2688]{1,0:T(8,128)(2,1)S(1)}, bf16[48,2560]{1,0:T(8,128)(2,1)S(1)}) custom-call(bf16[24,2688]{1,0:T(8,128)(2,1)S(1)} %collective-permute-done.9.refs_0_, bf16[24,2688]{1,0:T(8,128)(2,1)S(1)} %collective-permute-done.10.refs_1_, bf16[864,1280]{1,0:T(8,128)(2,1)S(1)} %get-tuple-element.51.refs_4_.gate_w.refs_2_, ...), custom_call_target="tpu_custom_call" | custom-call | tf_op jit(solution)/shard_map/pallas_call | solution.py:302
  30.6 0.5 collective-permute-start.11
  31.2 1.6 %collective-permute-start.18 = (bf16[24,2688]{1,0:T(8,128)(2,1)S(1)}, bf16[24,2688]{1,0:T(8,128)(2,1)S(1)}, u32[]{:S(2)}, u32[]{:S(2)}) collective-permute-start(bf16[24,2688]{1,0:T(8,128)(2,1)S(1)} %get-tuple-element.74), channel_id=1, source_target_pairs={{0,2},{1,3},{2,0},{3,1},{4,6},{5,7},{6,4},{7,5},{8,10},{9,11},{10,... | collective-permute-start | bytes 387080 | tf_op jit(solution)/shard_map/ppermute | solution.py:268
  32.8 0.0 collective-permute-done.11.got
  32.8 0.9 %collective-permute-start.12 = (bf16[24,2688]{1,0:T(8,128)(2,1)S(1)}, bf16[24,2688]{1,0:T(8,128)(2,1)S(1)}, u32[]{:S(2)}, u32[]{:S(2)}) collective-permute-start(bf16[24,2688]{1,0:T(8,128)(2,1)S(1)} %get-tuple-element.68), channel_id=1, source_target_pairs={{0,2},{1,3},{2,0},{3,1},{4,6},{5,7},{6,4},{7,5},{8,10},{9,11},{10,... | collective-permute-start | bytes 387080 | tf_op jit(solution)/shard_map/ppermute | solution.py:268
  33.7 0.0 collective-permute-done.3.got
  33.7 0.1 shard_map.141
  33.8 1.2 %collective-permute-start.4 = (bf16[48,2688]{1,0:T(8,128)(2,1)S(1)}, bf16[48,2688]{1,0:T(8,128)(2,1)S(1)}, u32[]{:S(2)}, u32[]{:S(2)}) collective-permute-start(bf16[48,2688]{1,0:T(8,128)(2,1)S(1)} %get-tuple-element.60), channel_id=1, source_target_pairs={{0,2},{1,3},{2,0},{3,1},{4,6},{5,7},{6,4},{7,5},{8,10},{9,11},{10,... | collective-permute-start | bytes 774152 | tf_op jit(solution)/shard_map/ppermute | solution.py:268
  35.1 2.6 %collective-permute-done.18.got = bf16[24,2688]{1,0:T(8,128)(2,1)S(1)} collective-permute-done((bf16[24,2688]{1,0:T(8,128)(2,1)S(1)}, bf16[24,2688]{1,0:T(8,128)(2,1)S(1)}, u32[]{:S(2)}, u32[]{:S(2)}) %collective-permute-start.18) | collective-permute-done | bytes 129056 | tf_op jit(solution)/shard_map/ppermute | solution.py:268
  37.6 0.4 shard_map.150.own
  38.0 0.0 collective-permute-start.19
  38.0 2.3 %collective-permute-done.12.got = bf16[24,2688]{1,0:T(8,128)(2,1)S(1)} collective-permute-done((bf16[24,2688]{1,0:T(8,128)(2,1)S(1)}, bf16[24,2688]{1,0:T(8,128)(2,1)S(1)}, u32[]{:S(2)}, u32[]{:S(2)}) %collective-permute-start.12) | collective-permute-done | bytes 129056 | tf_op jit(solution)/shard_map/ppermute | solution.py:268
  40.4 0.4 shard_map.146.own
  40.8 0.0 collective-permute-done.19.got
  40.8 1.1 %shard_map.151 = (bf16[24,2688]{1,0:T(8,128)(2,1)S(1)}, bf16[24,2688]{1,0:T(8,128)(2,1)S(1)}, bf16[48,2688]{1,0:T(8,128)(2,1)S(1)}) custom-call(bf16[24,2688]{1,0:T(8,128)(2,1)S(1)} %shard_map.150.own, bf16[24,2688]{1,0:T(8,128)(2,1)S(1)} %collective-permute-done.19.got, bf16[864,1280]{1,0:T(8,128)(2,1)S(1)} %get-tuple-element.51.refs_4_.gate_w.refs_2_, ...), custom_call_target="tpu_custom_call" | custom-call | tf_op jit(solution)/shard_map/pallas_call | solution.py:317
  41.9 1.6 %collective-permute-start.20 = (bf16[24,2688]{1,0:T(8,128)(2,1)S(1)}, bf16[24,2688]{1,0:T(8,128)(2,1)S(1)}, u32[]{:S(2)}, u32[]{:S(2)}) collective-permute-start(bf16[24,2688]{1,0:T(8,128)(2,1)S(1)} %get-tuple-element.76), channel_id=1, source_target_pairs={{0,4},{4,0},{8,12},{12,8},{16,20},{20,16},{24,28},{28,24},{1,5},{5... | collective-permute-start | bytes 387080 | tf_op jit(solution)/shard_map/ppermute | solution.py:265
  43.5 0.0 collective-permute-done.13.got
  43.5 1.1 %shard_map.147 = (bf16[24,2688]{1,0:T(8,128)(2,1)S(1)}, bf16[24,2688]{1,0:T(8,128)(2,1)S(1)}, bf16[48,2688]{1,0:T(8,128)(2,1)S(1)}) custom-call(bf16[24,2688]{1,0:T(8,128)(2,1)S(1)} %shard_map.146.own, bf16[24,2688]{1,0:T(8,128)(2,1)S(1)} %collective-permute-done.13.got, bf16[864,1280]{1,0:T(8,128)(2,1)S(1)} %get-tuple-element.51.refs_4_.gate_w.refs_2_, ...), custom_call_target="tpu_custom_call" | custom-call | tf_op jit(solution)/shard_map/pallas_call | solution.py:317
  44.6 0.6 collective-permute-start.14
  45.2 0.5 shard_map.142.own
  45.7 0.0 collective-permute-start.5
  45.7 2.4 %collective-permute-done.20 = bf16[24,2688]{1,0:T(8,128)(2,1)S(1)} collective-permute-done((bf16[24,2688]{1,0:T(8,128)(2,1)S(1)}, bf16[24,2688]{1,0:T(8,128)(2,1)S(1)}, u32[]{:S(2)}, u32[]{:S(2)}) %collective-permute-start.20) | collective-permute-done | bytes 129056 | tf_op jit(solution)/shard_map/ppermute | solution.py:265
  48.2 0.0 copy-start
  48.2 0.0 copy-start.1
  48.2 0.0 copy-start.4
  48.2 0.0 copy-start.5
  48.3 0.0 copy-start.6
  48.3 0.8 %collective-permute-start.21 = (bf16[24,2688]{1,0:T(8,128)(2,1)S(1)}, bf16[24,2688]{1,0:T(8,128)(2,1)S(1)}, u32[]{:S(2)}, u32[]{:S(2)}) collective-permute-start(bf16[24,2688]{1,0:T(8,128)(2,1)S(1)} %add_convert_fusion.1), channel_id=1, source_target_pairs={{0,8},{4,12},{8,0},{12,4},{16,24},{20,28},{24,16},{28,20},{1,9},{5... | collective-permute-start | bytes 387080 | tf_op jit(solution)/shard_map/ppermute | solution.py:265
  49.1 0.0 collective-permute-done.5.got
  49.1 1.3 %shard_map.143 = (bf16[24,2688]{1,0:T(8,128)(2,1)S(1)}, bf16[24,2688]{1,0:T(8,128)(2,1)S(1)}, bf16[24,2688]{1,0:T(8,128)(2,1)S(1)}, bf16[24,2688]{1,0:T(8,128)(2,1)S(1)}, bf16[96,2688]{1,0:T(8,128)(2,1)S(1)}) custom-call(bf16[48,2688]{1,0:T(8,128)(2,1)S(1)} %shard_map.142.own, bf16[48,2688]{1,0:T(8,128)(2,1)S(1)} %collective-permute-done.5.got, ...), custom_call_target="tpu_custom_call" | custom-call | tf_op jit(solution)/shard_map/pallas_call | solution.py:317
  50.4 0.0 copy-start.7
  50.4 0.0 copy-start.8
  50.4 1.7 %collective-permute-start.6 = (bf16[24,2688]{1,0:T(8,128)(2,1)S(1)}, bf16[24,2688]{1,0:T(8,128)(2,1)S(1)}, u32[]{:S(2)}, u32[]{:S(2)}) collective-permute-start(bf16[24,2688]{1,0:T(8,128)(2,1)S(1)} %get-tuple-element.62), channel_id=1, source_target_pairs={{0,4},{4,0},{8,12},{12,8},{16,20},{20,16},{24,28},{28,24},{1,5},{5... | collective-permute-start | bytes 387080 | tf_op jit(solution)/shard_map/ppermute | solution.py:265
  52.1 0.4 collective-permute-start.7
  52.5 0.8 %collective-permute-done.21 = bf16[24,2688]{1,0:T(8,128)(2,1)S(1)} collective-permute-done((bf16[24,2688]{1,0:T(8,128)(2,1)S(1)}, bf16[24,2688]{1,0:T(8,128)(2,1)S(1)}, u32[]{:S(2)}, u32[]{:S(2)}) %collective-permute-start.21) | collective-permute-done | bytes 129056 | tf_op jit(solution)/shard_map/ppermute | solution.py:265
  53.3 3.0 %collective-permute-start.22 = (bf16[24,2688]{1,0:T(8,128)(2,1)S(1)}, bf16[24,2688]{1,0:T(8,128)(2,1)S(1)}, u32[]{:S(2)}, u32[]{:S(2)}) collective-permute-start(bf16[24,2688]{1,0:T(8,128)(2,1)S(1)} %add_convert_fusion), channel_id=1, source_target_pairs={{0,16},{4,20},{8,24},{12,28},{16,0},{20,4},{24,8},{28,12},{1,17},{... | collective-permute-start | bytes 387080 | tf_op jit(solution)/shard_map/ppermute | solution.py:265
  56.4 1.2 %collective-permute-done.7 = bf16[24,2688]{1,0:T(8,128)(2,1)S(1)} collective-permute-done((bf16[24,2688]{1,0:T(8,128)(2,1)S(1)}, bf16[24,2688]{1,0:T(8,128)(2,1)S(1)}, u32[]{:S(2)}, u32[]{:S(2)}) %collective-permute-start.7) | collective-permute-done | bytes 129056 | tf_op jit(solution)/shard_map/ppermute | solution.py:265
  57.7 1.4 %collective-permute-start.8 = (bf16[24,2688]{1,0:T(8,128)(2,1)S(1)}, bf16[24,2688]{1,0:T(8,128)(2,1)S(1)}, u32[]{:S(2)}, u32[]{:S(2)}) collective-permute-start(bf16[24,2688]{1,0:T(8,128)(2,1)S(1)} %add_convert_fusion.2), channel_id=1, source_target_pairs={{0,8},{4,12},{8,0},{12,4},{16,24},{20,28},{24,16},{28,20},{1,9},{5... | collective-permute-start | bytes 387080 | tf_op jit(solution)/shard_map/ppermute | solution.py:265
  59.0 1.6 %shard_map.137 = (bf16[128,1280]{1,0:T(8,128)(2,1)S(1)}, bf16[128,1280]{1,0:T(8,128)(2,1)S(1)}, bf16[128,24]{1,0:T(8,128)(2,1)S(1)}) custom-call(s32[1,8]{1,0:T(1,128)S(1)} %copy-done.4, s32[1,24]{1,0:T(1,128)S(1)} %copy-done.5, f32[4]{0:T(128)S(1)} %copy-done.6, bf16[4,128,1280]{2,1,0:T(8,128)(2,1)S(1)} %copy-done, bf16[128,1280]{1,0:T(8,128)(2,1)S(1)} %copy-done.1), custom_call_target="tpu_custom_call" | custom-call | bytes 3145728 | tf_op jit(solution)/shard_map/pallas_call | solution.py:291
  60.7 0.1 shard_map.153
  60.8 0.0 copy-start.3
  60.8 2.5 %shard_map.155 = f32[864,1280]{1,0:T(8,128)} custom-call(bf16[192,864]{1,0:T(8,128)(2,1)S(1)} %get-tuple-element.89.refs_0_, bf16[192,1280]{1,0:T(8,128)(2,1)S(1)} %get-tuple-element.90.refs_1_), custom_call_target="tpu_custom_call" | custom-call | bytes 4423680 | tf_op jit(solution)/shard_map/pallas_call | solution.py:352
  63.3 3.9 %shard_map.154 = (f32[864,1280]{1,0:T(8,128)}, f32[864,1280]{1,0:T(8,128)}) custom-call(bf16[192,864]{1,0:T(8,128)(2,1)S(1)} %get-tuple-element.84.refs_0_, bf16[192,864]{1,0:T(8,128)(2,1)S(1)} %get-tuple-element.85.refs_1_, bf16[192,1280]{1,0:T(8,128)(2,1)S(1)} %get-tuple-element.86.refs_2_.refs_3_, bf16[192,1280]{1,0:T(8,128)(2,1)S(1)} %get-tuple-element.86.refs_2_.refs_3_), custom_call_target="tpu_custom_call" | custom-call | bytes 8847360 | tf_op jit(solution)/shard_map/pallas_call | solution.py:352
  67.3 1.1 %shard_map.152 = (bf16[128,1280]{1,0:T(8,128)(2,1)}, bf16[128,1280]{1,0:T(8,128)(2,1)}) custom-call(bf16[128,24]{1,0:T(8,128)(2,1)S(1)} %get-tuple-element.48.want, f32[24,1280]{1,0:T(8,128)S(1)} %copy-done.3, bf16[96,2560]{1,0:T(8,128)(2,1)S(1)} %get-tuple-element.54.taken.refs_3_, bf16[128,1280]{1,0:T(8,128)(2,1)S(1)} %get-tuple-element.55.mixed, ...), custom_call_target="tpu_custom_call" | custom-call | tf_op jit(solution)/shard_map/pallas_call | solution.py:365
  (24 shorter events, 0.3 us)
Async XLA Ops:
  3.1 10.7 %collective-permute-start.9 = (bf16[24,2688]{1,0:T(8,128)(2,1)}, bf16[24,2688]{1,0:T(8,128)(2,1)S(1)}, u32[]{:S(2)}, u32[]{:S(2)}) collective-permute-start(bf16[24,2688]{1,0:T(8,128)(2,1)} %get-tuple-element.50.refs_0_), channel_id=1, source_target_pairs={{0,16},{4,20},{8,24},{12,28},{16,0},{20,4},{24,8},{28,12},{1,17},{... | collective-permute-start | bytes 387080 | tf_op jit(solution)/shard_map/ppermute | solution.py:265
  7.3 8.8 %collective-permute-start.1 = (bf16[24,2688]{1,0:T(8,128)(2,1)}, bf16[24,2688]{1,0:T(8,128)(2,1)S(1)}, u32[]{:S(2)}, u32[]{:S(2)}) collective-permute-start(bf16[24,2688]{1,0:T(8,128)(2,1)} %get-tuple-element.50.refs_0_), channel_id=1, source_target_pairs={{0,8},{4,12},{8,0},{12,4},{16,24},{20,28},{24,16},{28,20},{1,9},{5... | collective-permute-start | bytes 387080 | tf_op jit(solution)/shard_map/ppermute | solution.py:265
  13.8 4.9 %collective-permute-start.15 = (bf16[24,2688]{1,0:T(8,128)(2,1)S(1)}, bf16[24,2688]{1,0:T(8,128)(2,1)S(1)}, u32[]{:S(2)}, u32[]{:S(2)}) collective-permute-start(bf16[24,2688]{1,0:T(8,128)(2,1)S(1)} %collective-permute-done.9.refs_0_), channel_id=1, source_target_pairs={{0,8},{4,12},{8,0},{12,4},{16,24},{20,28},{24,16},{28,20},{1,9},{5... | collective-permute-start | bytes 387080 | tf_op jit(solution)/shard_map/ppermute | solution.py:265
  14.5 9.4 %collective-permute-start = (bf16[24,2688]{1,0:T(8,128)(2,1)}, bf16[24,2688]{1,0:T(8,128)(2,1)S(1)}, u32[]{:S(2)}, u32[]{:S(2)}) collective-permute-start(bf16[24,2688]{1,0:T(8,128)(2,1)} %get-tuple-element.50.refs_0_), channel_id=1, source_target_pairs={{0,4},{4,0},{8,12},{12,8},{16,20},{20,16},{24,28},{28,24},{1,5},{5... | collective-permute-start | bytes 387080 | tf_op jit(solution)/shard_map/ppermute | solution.py:265
  16.1 7.9 %collective-permute-start.2 = (bf16[24,2688]{1,0:T(8,128)(2,1)S(1)}, bf16[24,2688]{1,0:T(8,128)(2,1)S(1)}, u32[]{:S(2)}, u32[]{:S(2)}) collective-permute-start(bf16[24,2688]{1,0:T(8,128)(2,1)S(1)} %collective-permute-done.1.refs_2_), channel_id=1, source_target_pairs={{0,4},{4,0},{8,12},{12,8},{16,20},{20,16},{24,28},{28,24},{1,5},{5... | collective-permute-start | bytes 387080 | tf_op jit(solution)/shard_map/ppermute | solution.py:265
  18.8 7.8 %collective-permute-start.16 = (bf16[24,2688]{1,0:T(8,128)(2,1)S(1)}, bf16[24,2688]{1,0:T(8,128)(2,1)S(1)}, u32[]{:S(2)}, u32[]{:S(2)}) collective-permute-start(bf16[24,2688]{1,0:T(8,128)(2,1)S(1)} %collective-permute-done.15.refs_0_), channel_id=1, source_target_pairs={{0,4},{4,0},{8,12},{12,8},{16,20},{20,16},{24,28},{28,24},{1,5},{5... | collective-permute-start | bytes 387080 | tf_op jit(solution)/shard_map/ppermute | solution.py:265
  20.3 3.6 %copy-start.2 = (bf16[24,2688]{1,0:T(8,128)(2,1)S(1)}, bf16[24,2688]{1,0:T(8,128)(2,1)}, u32[]{:S(2)}) copy-start(bf16[24,2688]{1,0:T(8,128)(2,1)} %get-tuple-element.50.refs_0_) | copy-start | bytes 387076
  23.4 5.3 %collective-permute-start.10 = (bf16[24,2688]{1,0:T(8,128)(2,1)S(1)}, bf16[24,2688]{1,0:T(8,128)(2,1)S(1)}, u32[]{:S(2)}, u32[]{:S(2)}) collective-permute-start(bf16[24,2688]{1,0:T(8,128)(2,1)S(1)} %collective-permute-done.9.refs_0_), channel_id=1, source_target_pairs={{0,4},{4,0},{8,12},{12,8},{16,20},{20,16},{24,28},{28,24},{1,5},{5... | collective-permute-start | bytes 387080 | tf_op jit(solution)/shard_map/ppermute | solution.py:265
  26.1 7.7 %collective-permute-start.3 = (bf16[48,2688]{1,0:T(8,128)(2,1)S(1)}, bf16[48,2688]{1,0:T(8,128)(2,1)S(1)}, u32[]{:S(2)}, u32[]{:S(2)}) collective-permute-start(bf16[48,2688]{1,0:T(8,128)(2,1)S(1)} %get-tuple-element.58), channel_id=1, source_target_pairs={{0,1},{1,0},{2,3},{3,2},{4,5},{5,4},{6,7},{7,6},{8,9},{9,8},{10,11... | collective-permute-start | bytes 774152 | tf_op jit(solution)/shard_map/ppermute | solution.py:268
  28.6 2.6 %collective-permute-start.17 = (bf16[24,2688]{1,0:T(8,128)(2,1)S(1)}, bf16[24,2688]{1,0:T(8,128)(2,1)S(1)}, u32[]{:S(2)}, u32[]{:S(2)}) collective-permute-start(bf16[24,2688]{1,0:T(8,128)(2,1)S(1)} %get-tuple-element.72), channel_id=1, source_target_pairs={{0,1},{1,0},{2,3},{3,2},{4,5},{5,4},{6,7},{7,6},{8,9},{9,8},{10,11... | collective-permute-start | bytes 387080 | tf_op jit(solution)/shard_map/ppermute | solution.py:268
  30.6 2.1 %collective-permute-start.11 = (bf16[24,2688]{1,0:T(8,128)(2,1)S(1)}, bf16[24,2688]{1,0:T(8,128)(2,1)S(1)}, u32[]{:S(2)}, u32[]{:S(2)}) collective-permute-start(bf16[24,2688]{1,0:T(8,128)(2,1)S(1)} %get-tuple-element.66), channel_id=1, source_target_pairs={{0,1},{1,0},{2,3},{3,2},{4,5},{5,4},{6,7},{7,6},{8,9},{9,8},{10,11... | collective-permute-start | bytes 387080 | tf_op jit(solution)/shard_map/ppermute | solution.py:268
  31.2 6.4 %collective-permute-start.18 = (bf16[24,2688]{1,0:T(8,128)(2,1)S(1)}, bf16[24,2688]{1,0:T(8,128)(2,1)S(1)}, u32[]{:S(2)}, u32[]{:S(2)}) collective-permute-start(bf16[24,2688]{1,0:T(8,128)(2,1)S(1)} %get-tuple-element.74), channel_id=1, source_target_pairs={{0,2},{1,3},{2,0},{3,1},{4,6},{5,7},{6,4},{7,5},{8,10},{9,11},{10,... | collective-permute-start | bytes 387080 | tf_op jit(solution)/shard_map/ppermute | solution.py:268
  32.8 7.6 %collective-permute-start.12 = (bf16[24,2688]{1,0:T(8,128)(2,1)S(1)}, bf16[24,2688]{1,0:T(8,128)(2,1)S(1)}, u32[]{:S(2)}, u32[]{:S(2)}) collective-permute-start(bf16[24,2688]{1,0:T(8,128)(2,1)S(1)} %get-tuple-element.68), channel_id=1, source_target_pairs={{0,2},{1,3},{2,0},{3,1},{4,6},{5,7},{6,4},{7,5},{8,10},{9,11},{10,... | collective-permute-start | bytes 387080 | tf_op jit(solution)/shard_map/ppermute | solution.py:268
  33.8 11.4 %collective-permute-start.4 = (bf16[48,2688]{1,0:T(8,128)(2,1)S(1)}, bf16[48,2688]{1,0:T(8,128)(2,1)S(1)}, u32[]{:S(2)}, u32[]{:S(2)}) collective-permute-start(bf16[48,2688]{1,0:T(8,128)(2,1)S(1)} %get-tuple-element.60), channel_id=1, source_target_pairs={{0,2},{1,3},{2,0},{3,1},{4,6},{5,7},{6,4},{7,5},{8,10},{9,11},{10,... | collective-permute-start | bytes 774152 | tf_op jit(solution)/shard_map/ppermute | solution.py:268
  38.0 2.8 %collective-permute-start.19 = (bf16[24,2688]{1,0:T(8,128)(2,1)S(1)}, bf16[24,2688]{1,0:T(8,128)(2,1)S(1)}, u32[]{:S(2)}, u32[]{:S(2)}) collective-permute-start(bf16[24,2688]{1,0:T(8,128)(2,1)S(1)} %shard_map.150.own), channel_id=1, source_target_pairs={{0,1},{1,0},{2,3},{3,2},{4,5},{5,4},{6,7},{7,6},{8,9},{9,8},{10,11... | collective-permute-start | bytes 387080 | tf_op jit(solution)/shard_map/ppermute | solution.py:268
  40.8 2.7 %collective-permute-start.13 = (bf16[24,2688]{1,0:T(8,128)(2,1)S(1)}, bf16[24,2688]{1,0:T(8,128)(2,1)S(1)}, u32[]{:S(2)}, u32[]{:S(2)}) collective-permute-start(bf16[24,2688]{1,0:T(8,128)(2,1)S(1)} %shard_map.146.own), channel_id=1, source_target_pairs={{0,1},{1,0},{2,3},{3,2},{4,5},{5,4},{6,7},{7,6},{8,9},{9,8},{10,11... | collective-permute-start | bytes 387080 | tf_op jit(solution)/shard_map/ppermute | solution.py:268
  41.9 6.2 %collective-permute-start.20 = (bf16[24,2688]{1,0:T(8,128)(2,1)S(1)}, bf16[24,2688]{1,0:T(8,128)(2,1)S(1)}, u32[]{:S(2)}, u32[]{:S(2)}) collective-permute-start(bf16[24,2688]{1,0:T(8,128)(2,1)S(1)} %get-tuple-element.76), channel_id=1, source_target_pairs={{0,4},{4,0},{8,12},{12,8},{16,20},{20,16},{24,28},{28,24},{1,5},{5... | collective-permute-start | bytes 387080 | tf_op jit(solution)/shard_map/ppermute | solution.py:265
  44.6 7.9 %collective-permute-start.14 = (bf16[24,2688]{1,0:T(8,128)(2,1)S(1)}, bf16[24,2688]{1,0:T(8,128)(2,1)S(1)}, u32[]{:S(2)}, u32[]{:S(2)}) collective-permute-start(bf16[24,2688]{1,0:T(8,128)(2,1)S(1)} %get-tuple-element.70), channel_id=1, source_target_pairs={{0,4},{4,0},{8,12},{12,8},{16,20},{20,16},{24,28},{28,24},{1,5},{5... | collective-permute-start | bytes 387080 | tf_op jit(solution)/shard_map/ppermute | solution.py:265
  45.7 3.4 %collective-permute-start.5 = (bf16[48,2688]{1,0:T(8,128)(2,1)S(1)}, bf16[48,2688]{1,0:T(8,128)(2,1)S(1)}, u32[]{:S(2)}, u32[]{:S(2)}) collective-permute-start(bf16[48,2688]{1,0:T(8,128)(2,1)S(1)} %shard_map.142.own), channel_id=1, source_target_pairs={{0,1},{1,0},{2,3},{3,2},{4,5},{5,4},{6,7},{7,6},{8,9},{9,8},{10,11... | collective-permute-start | bytes 774152 | tf_op jit(solution)/shard_map/ppermute | solution.py:268
  48.2 10.8 %copy-start = (bf16[4,128,1280]{2,1,0:T(8,128)(2,1)S(1)}, bf16[4,128,1280]{2,1,0:T(8,128)(2,1)}, u32[]{:S(2)}) copy-start(bf16[4,128,1280]{2,1,0:T(8,128)(2,1)} %states.3) | copy-start | bytes 3932164
  48.2 10.8 %copy-start.1 = (bf16[128,1280]{1,0:T(8,128)(2,1)S(1)}, bf16[128,1280]{1,0:T(8,128)(2,1)}, u32[]{:S(2)}) copy-start(bf16[128,1280]{1,0:T(8,128)(2,1)} %cot.3) | copy-start | bytes 983044
  48.2 10.8 %copy-start.4 = (s32[1,8]{1,0:T(1,128)S(1)}, s32[1,8]{1,0:T(1,128)}, u32[]{:S(2)}) copy-start(s32[1,8]{1,0:T(1,128)} %counts.3) | copy-start | bytes 100
  48.2 10.8 %copy-start.5 = (s32[1,24]{1,0:T(1,128)S(1)}, s32[1,24]{1,0:T(1,128)}, u32[]{:S(2)}) copy-start(s32[1,24]{1,0:T(1,128)} %chosen.3) | copy-start | bytes 292
  48.3 10.8 %copy-start.6 = (f32[4]{0:T(128)S(1)}, f32[4]{0:T(128)}, u32[]{:S(2)}) copy-start(f32[4]{0:T(128)} %mixw.3) | copy-start | bytes 52
  48.3 5.0 %collective-permute-start.21 = (bf16[24,2688]{1,0:T(8,128)(2,1)S(1)}, bf16[24,2688]{1,0:T(8,128)(2,1)S(1)}, u32[]{:S(2)}, u32[]{:S(2)}) collective-permute-start(bf16[24,2688]{1,0:T(8,128)(2,1)S(1)} %add_convert_fusion.1), channel_id=1, source_target_pairs={{0,8},{4,12},{8,0},{12,4},{16,24},{20,28},{24,16},{28,20},{1,9},{5... | collective-permute-start | bytes 387080 | tf_op jit(solution)/shard_map/ppermute | solution.py:265
  50.4 10.2 %copy-start.7 = (bf16[1280]{0:T(1024)(128)(2,1)S(1)}, bf16[1280]{0:T(1024)(128)(2,1)}, u32[]{:S(2)}) copy-start(bf16[1280]{0:T(1024)(128)(2,1)} %router.1) | copy-start | bytes 7684
  50.4 10.2 %copy-start.8 = (bf16[1280]{0:T(1024)(128)(2,1)S(1)}, bf16[1280]{0:T(1024)(128)(2,1)}, u32[]{:S(2)}) copy-start(bf16[1280]{0:T(1024)(128)(2,1)} %gain.1) | copy-start | bytes 7684
  50.4 16.8 %collective-permute-start.6 = (bf16[24,2688]{1,0:T(8,128)(2,1)S(1)}, bf16[24,2688]{1,0:T(8,128)(2,1)S(1)}, u32[]{:S(2)}, u32[]{:S(2)}) collective-permute-start(bf16[24,2688]{1,0:T(8,128)(2,1)S(1)} %get-tuple-element.62), channel_id=1, source_target_pairs={{0,4},{4,0},{8,12},{12,8},{16,20},{20,16},{24,28},{28,24},{1,5},{5... | collective-permute-start | bytes 387080 | tf_op jit(solution)/shard_map/ppermute | solution.py:265
  52.1 5.5 %collective-permute-start.7 = (bf16[24,2688]{1,0:T(8,128)(2,1)S(1)}, bf16[24,2688]{1,0:T(8,128)(2,1)S(1)}, u32[]{:S(2)}, u32[]{:S(2)}) collective-permute-start(bf16[24,2688]{1,0:T(8,128)(2,1)S(1)} %get-tuple-element.64), channel_id=1, source_target_pairs={{0,4},{4,0},{8,12},{12,8},{16,20},{20,16},{24,28},{28,24},{1,5},{5... | collective-permute-start | bytes 387080 | tf_op jit(solution)/shard_map/ppermute | solution.py:265
  53.3 13.9 %collective-permute-start.22 = (bf16[24,2688]{1,0:T(8,128)(2,1)S(1)}, bf16[24,2688]{1,0:T(8,128)(2,1)S(1)}, u32[]{:S(2)}, u32[]{:S(2)}) collective-permute-start(bf16[24,2688]{1,0:T(8,128)(2,1)S(1)} %add_convert_fusion), channel_id=1, source_target_pairs={{0,16},{4,20},{8,24},{12,28},{16,0},{20,4},{24,8},{28,12},{1,17},{... | collective-permute-start | bytes 387080 | tf_op jit(solution)/shard_map/ppermute | solution.py:265
  57.7 9.6 %collective-permute-start.8 = (bf16[24,2688]{1,0:T(8,128)(2,1)S(1)}, bf16[24,2688]{1,0:T(8,128)(2,1)S(1)}, u32[]{:S(2)}, u32[]{:S(2)}) collective-permute-start(bf16[24,2688]{1,0:T(8,128)(2,1)S(1)} %add_convert_fusion.2), channel_id=1, source_target_pairs={{0,8},{4,12},{8,0},{12,4},{16,24},{20,28},{24,16},{28,20},{1,9},{5... | collective-permute-start | bytes 387080 | tf_op jit(solution)/shard_map/ppermute | solution.py:265
  60.8 6.4 %copy-start.3 = (f32[24,1280]{1,0:T(8,128)S(1)}, f32[24,1280]{1,0:T(8,128)}, u32[]{:S(2)}) copy-start(f32[24,1280]{1,0:T(8,128)} %get-tuple-element.49.picked) | copy-start | bytes 368644
